TPU v7x, 32 devices: a whole 2x2x4 slice. The times are simulated.
32 devices in a mesh: dp: 8 (over z, x), seq: 4 (over y, core).
Axes of the slice: x: 2, y: 2, z: 4, core: 2. Of those that a mesh axis runs over, the one named last changes fastest.
Arguments:
- stream_in: bfloat16 [16, 1024, 768], P('dp', 'seq'), may hold values from -6 to 6
- chosen: int32 [16, 256], P('dp', 'seq'), may hold values from 0 to 255, as said below
- counts: int32 [16, 4], P('dp'), may hold values from 16 to 64, as said below
- route_w: bfloat16 [768], replicated, may hold values from -0.21875 to 0.21875
- gain_a1: bfloat16 [768], replicated, may hold values from 0.5 to 1.5
- qkv_a: bfloat16 [768, 2304], replicated, may hold values from -0.21875 to 0.21875
- out_a: bfloat16 [768, 768], replicated, may hold values from -1.25 to 1.25
- gain_a2: bfloat16 [768], replicated, may hold values from 0.5 to 1.5
- up_a: bfloat16 [768, 3072], replicated, may hold values from -0.21875 to 0.21875
- down_a: bfloat16 [3072, 768], replicated, may hold values from -0.109375 to 0.109375
- gain_b1: bfloat16 [768], replicated, may hold values from 0.5 to 1.5
- qkv_b: bfloat16 [768, 2304], replicated, may hold values from -0.21875 to 0.21875
- out_b: bfloat16 [768, 768], replicated, may hold values from -1.75 to 1.75
- gain_b2: bfloat16 [768], replicated, may hold values from 0.5 to 1.5
- up_b: bfloat16 [768, 3072], replicated, may hold values from -0.21875 to 0.21875
- down_b: bfloat16 [3072, 768], replicated, may hold values from -0.109375 to 0.109375
- cotangent: bfloat16 [16, 1024, 768], P('dp', 'seq'), may hold values from -6 to 6
Outputs:
- output: bfloat16 [16, 1024, 768], P('dp', 'seq')
- grad_input: float32 [16, 1024, 768], P('dp', 'seq')
- grad_route: float32 [768], P('dp')
- grad_gain_a1: float32 [768], P('dp')
- grad_qkv_a: float32 [768, 2304], P('dp')
- grad_out_a: float32 [768, 768], P('dp')
- grad_gain_a2: float32 [768], P('dp')
- grad_up_a: float32 [768, 3072], P('dp')
- grad_down_a: float32 [3072, 768], P('dp')
- grad_gain_b1: float32 [768], P('dp')
- grad_qkv_b: float32 [768, 2304], P('dp')
- grad_out_b: float32 [768, 768], P('dp')
- grad_gain_b2: float32 [768], P('dp')
- grad_up_b: float32 [768, 3072], P('dp')
- grad_down_b: float32 [3072, 768], P('dp')
Inputs may be any that keep to these rules, and one draw needn't show every extreme that they name: `chosen`: in each row, the slots of one device hold in their first counts entries distinct positions in increasing order; the other slots hold 0. `counts`: some device of some sequence holds exactly 64 routed tokens.
All inputs are finite; a program needn't handle non-finite values.
Results may differ from a plain program's by a relative error of at most 0.023.
Values may be sent and summed in bfloat16 or wider, within the bound.
No kernel may reach another device: no remote copies, remote signals or barrier semaphores. Data moves between devices by JAX's collectives and lax.ppermute only.
A program may use at most 192 MiB of HBM per device.

v0:
```python
import jax
import jax.numpy as jnp
from jax import lax
from jax.sharding import PartitionSpec as P

HEADS = 12
HEAD_DIM = 64


EPSILON = 1e-06
EXACT = lax.Precision.HIGHEST


def norm_rows(vector, gain_vec):
    return (
        vector * lax.rsqrt(jnp.mean(vector * vector, axis=-1, keepdims=True) + EPSILON) * gain_vec
    )


def project(left_side, weight):
    return jnp.einsum("bnd,de->bne", left_side, weight, preferred_element_type=jnp.float32)


def project_back(gradient, weight):
    return jnp.einsum("bne,de->bnd", gradient, weight, preferred_element_type=jnp.float32)


def weight_grad(left_side, gradient):
    return jnp.einsum("bnd,bne->de", left_side, gradient, preferred_element_type=jnp.float32)


def split_heads(vector):
    return vector.reshape(vector.shape[0], HEADS, HEAD_DIM)


def score_rows(queries, key_rows, visible):
    scores = jnp.einsum(
        "qhd,khd->hqk",
        split_heads(queries),
        split_heads(key_rows),
        preferred_element_type=jnp.float32,
    ) * HEAD_DIM ** (-0.5)
    return jnp.where(visible[None], scores, -1e30)


def attend_forward(item_set):
    queries, key_rows, value_rows, visible = item_set
    scores = score_rows(queries, key_rows, visible)
    row_max = jnp.max(scores, axis=-1, keepdims=True)
    exponent = jnp.exp(scores - row_max)
    row_total = jnp.sum(exponent, axis=-1, keepdims=True)
    probability = (exponent / row_total).astype(jnp.bfloat16)
    mixture = jnp.einsum(
        "hqk,khd->qhd", probability, split_heads(value_rows), preferred_element_type=jnp.float32
    )
    return (mixture.reshape(queries.shape[0], -1).astype(jnp.bfloat16), row_max, row_total)


def attend_backward(item_set):
    queries, key_rows, value_rows, visible, row_max, row_total, grad_mixture = item_set
    scores = score_rows(queries, key_rows, visible)
    probability = jnp.exp(scores - row_max) / row_total
    grad_heads = split_heads(grad_mixture)
    grad_values = jnp.einsum(
        "hqk,qhd->khd",
        probability.astype(jnp.bfloat16),
        grad_heads,
        preferred_element_type=jnp.float32,
    )
    grad_probs = jnp.einsum(
        "qhd,khd->hqk", grad_heads, split_heads(value_rows), preferred_element_type=jnp.float32
    )
    inner_sum = jnp.sum(probability * grad_probs, axis=-1, keepdims=True)
    grad_scores = (probability * (grad_probs - inner_sum)).astype(jnp.bfloat16)
    scaling = HEAD_DIM ** (-0.5)
    grad_query = (
        jnp.einsum(
            "hqk,khd->qhd", grad_scores, split_heads(key_rows), preferred_element_type=jnp.float32
        )
        * scaling
    )
    grad_keys = (
        jnp.einsum(
            "hqk,qhd->khd", grad_scores, split_heads(queries), preferred_element_type=jnp.float32
        )
        * scaling
    )
    row_count = queries.shape[0]
    key_count = key_rows.shape[0]
    return (
        grad_query.reshape(row_count, -1),
        grad_keys.reshape(key_count, -1),
        grad_values.reshape(key_count, -1),
    )


def layer_forward(resid, router, visible, gain_one, w_qkv, w_out, gain_two, w_up, w_down, fetcher):
    model_width = resid.shape[-1]
    act_in = norm_rows(resid, gain_one.astype(jnp.float32)).astype(jnp.bfloat16)
    packed = project(act_in, w_qkv)
    queries = packed[..., :model_width].astype(jnp.bfloat16)
    key_rows = packed[..., model_width : 2 * model_width].astype(jnp.bfloat16)
    value_rows = packed[..., 2 * model_width :].astype(jnp.bfloat16)
    all_keys, all_values = fetcher(key_rows, value_rows)
    mixture, row_max, row_total = lax.map(attend_forward, (queries, all_keys, all_values, visible))
    attended = project(mixture, w_out)
    middle = resid + router[..., None] * attended
    ff_in = norm_rows(middle, gain_two.astype(jnp.float32)).astype(jnp.bfloat16)
    hidden = project(ff_in, w_up)
    activated = jax.nn.gelu(hidden).astype(jnp.bfloat16)
    done = middle + project(activated, w_down)
    kept_state = (
        resid,
        act_in,
        queries,
        key_rows,
        value_rows,
        all_keys,
        all_values,
        mixture,
        row_max,
        row_total,
        attended,
        middle,
        ff_in,
        hidden,
        activated,
    )
    return (done, kept_state)


def layer_backward(
    grad_done,
    router,
    visible,
    gain_one,
    w_qkv,
    w_out,
    gain_two,
    w_up,
    w_down,
    kept_state,
    refetch,
    send_back,
):
    (
        resid,
        act_in,
        queries,
        key_rows,
        value_rows,
        all_keys,
        all_values,
        mixture,
        row_max,
        row_total,
        attended,
        middle,
        ff_in,
        hidden,
        activated,
    ) = kept_state
    grad_ff = grad_done.astype(jnp.bfloat16)
    grad_down = weight_grad(activated, grad_ff)
    grad_act = project_back(grad_ff, w_down)
    unused_value, gelu_pull = jax.vjp(jax.nn.gelu, hidden)
    grad_hidden = gelu_pull(grad_act)[0].astype(jnp.bfloat16)
    grad_up = weight_grad(ff_in, grad_hidden)
    grad_ffin = project_back(grad_hidden, w_up)
    unused_norm, norm_pull = jax.vjp(norm_rows, middle, gain_two.astype(jnp.float32))
    grad_mid_norm, grad_gain_two = norm_pull(grad_ffin)
    grad_middle = grad_done + grad_mid_norm
    grad_attended = (router[..., None] * grad_middle).astype(jnp.bfloat16)
    grad_router = jnp.sum(attended * grad_middle, axis=-1)
    grad_out = weight_grad(mixture, grad_attended)
    grad_mixture = project_back(grad_attended, w_out).astype(jnp.bfloat16)
    all_keys, all_values = refetch(key_rows, value_rows, all_keys, all_values)
    grad_query, grad_all_keys, grad_all_values = lax.map(
        attend_backward, (queries, all_keys, all_values, visible, row_max, row_total, grad_mixture)
    )
    grad_keys, grad_values = send_back(grad_all_keys, grad_all_values)
    grad_packed = jnp.concatenate(
        [
            grad_query.astype(jnp.bfloat16),
            grad_keys.astype(jnp.bfloat16),
            grad_values.astype(jnp.bfloat16),
        ],
        axis=-1,
    )
    grad_qkv = weight_grad(act_in, grad_packed)
    grad_act_in = project_back(grad_packed, w_qkv)
    unused_first, first_pull = jax.vjp(norm_rows, resid, gain_one.astype(jnp.float32))
    grad_res_norm, grad_gain_one = first_pull(grad_act_in)
    grad_resid = grad_middle + grad_res_norm
    return (
        grad_resid,
        grad_router,
        (grad_gain_one, grad_qkv, grad_out, grad_gain_two, grad_up, grad_down),
    )


def per_device(
    stream_in,
    chosen,
    counts,
    route_w,
    gain_a1,
    qkv_a,
    out_a,
    gain_a2,
    up_a,
    down_a,
    gain_b1,
    qkv_b,
    out_b,
    gain_b2,
    up_b,
    down_b,
    cotangent,
):
    seq_count, shard_rows, model_width = stream_in.shape
    slot_count = chosen.shape[1]
    group_size = lax.axis_size("seq")
    my_index = lax.axis_index("seq")
    seq_ids = jnp.arange(seq_count, dtype=jnp.int32)[:, None]
    owner_ids = jnp.arange(group_size, dtype=jnp.int32)
    own_load = jnp.sum(jnp.where(owner_ids[None, :] == my_index, counts, 0), axis=1)
    place_ids = jnp.arange(slot_count, dtype=jnp.int32)
    live_slots = place_ids[None, :] < own_load[:, None]
    key_slots = jnp.arange(group_size * slot_count, dtype=jnp.int32)
    key_owner = key_slots // slot_count
    key_place = key_slots % slot_count
    key_load = jnp.sum(
        jnp.where(key_owner[None, :, None] == owner_ids[None, None, :], counts[:, None, :], 0),
        axis=2,
    )
    key_live = key_place[None, :] < key_load
    same_owner = key_owner[None, :] == my_index
    earlier = key_owner[None, :] < my_index
    ordered_ok = earlier | same_owner & (key_place[None, :] <= place_ids[:, None])
    sel_visible = key_live[:, None, :] & ordered_ok[None]
    sel_visible = sel_visible | (same_owner & (key_place[None, :] == place_ids[:, None]))[None]

    def fetch_sel(key_rows, value_rows):
        return (
            lax.all_gather(key_rows, "seq", axis=1, tiled=True),
            lax.all_gather(value_rows, "seq", axis=1, tiled=True),
        )

    def fetch_full(key_rows, value_rows):
        return (
            lax.all_gather(key_rows, "seq", axis=1, tiled=True),
            lax.all_gather(value_rows, "seq", axis=1, tiled=True),
        )

    def send_sel(grad_keys, grad_values):
        return (
            lax.psum_scatter(
                grad_keys.astype(jnp.bfloat16), "seq", scatter_dimension=1, tiled=True
            ).astype(jnp.float32),
            lax.psum_scatter(
                grad_values.astype(jnp.bfloat16), "seq", scatter_dimension=1, tiled=True
            ).astype(jnp.float32),
        )

    def send_full(grad_keys, grad_values):
        return (
            lax.psum_scatter(
                grad_keys.astype(jnp.bfloat16), "seq", scatter_dimension=1, tiled=True
            ).astype(jnp.float32),
            lax.psum_scatter(
                grad_values.astype(jnp.bfloat16), "seq", scatter_dimension=1, tiled=True
            ).astype(jnp.float32),
        )

    def refetch_sel(key_rows, value_rows, old_keys, old_values):
        return (old_keys, old_values)

    def refetch_full(key_rows, value_rows, old_keys, old_values):
        return (old_keys, old_values)

    picked_low = stream_in[seq_ids, chosen]
    picked = picked_low.astype(jnp.float32)
    router = jnp.einsum("bcd,d->bc", picked_low, route_w, preferred_element_type=jnp.float32)
    done_sel, kept_sel = layer_forward(
        picked, router, sel_visible, gain_a1, qkv_a, out_a, gain_a2, up_a, down_a, fetch_sel
    )
    change = jnp.where(live_slots[..., None], done_sel - picked, 0.0)
    middle = stream_in.astype(jnp.float32).at[seq_ids, chosen].add(change)
    positions = my_index * shard_rows + jnp.arange(shard_rows, dtype=jnp.int32)
    causal = jnp.arange(group_size * shard_rows, dtype=jnp.int32)[None, :] <= positions[:, None]
    full_visible = jnp.broadcast_to(causal[None], (seq_count, shard_rows, group_size * shard_rows))
    unit_gates = jnp.ones((seq_count, shard_rows), jnp.float32)
    final_rows, kept_full = layer_forward(
        middle, unit_gates, full_visible, gain_b1, qkv_b, out_b, gain_b2, up_b, down_b, fetch_full
    )
    grad_middle, unused_router, dense_grads = layer_backward(
        cotangent.astype(jnp.float32),
        unit_gates,
        full_visible,
        gain_b1,
        qkv_b,
        out_b,
        gain_b2,
        up_b,
        down_b,
        kept_full,
        refetch_full,
        send_full,
    )
    grad_done = jnp.where(live_slots[..., None], grad_middle[seq_ids, chosen], 0.0)
    grad_picked, grad_router, sel_grads = layer_backward(
        grad_done,
        router,
        sel_visible,
        gain_a1,
        qkv_a,
        out_a,
        gain_a2,
        up_a,
        down_a,
        kept_sel,
        refetch_sel,
        send_sel,
    )
    grad_picked = grad_picked + grad_router[..., None] * route_w.astype(jnp.float32) - grad_done
    grad_route = jnp.einsum("bc,bcd->d", grad_router, picked, precision=EXACT)
    grad_input = grad_middle.at[seq_ids, chosen].add(grad_picked)
    g_ga1, g_qa, g_oa, g_ga2, g_ua, g_da = sel_grads
    g_gb1, g_qb, g_ob, g_gb2, g_ub, g_db = dense_grads
    reduced = (
        lax.psum_scatter(
            grad_route.astype(jnp.bfloat16), "dp", scatter_dimension=0, tiled=True
        ).astype(jnp.float32),
        lax.psum_scatter(g_ga1.astype(jnp.bfloat16), "dp", scatter_dimension=0, tiled=True).astype(
            jnp.float32
        ),
        lax.psum_scatter(g_qa.astype(jnp.bfloat16), "dp", scatter_dimension=0, tiled=True).astype(
            jnp.float32
        ),
        lax.psum_scatter(g_oa.astype(jnp.bfloat16), "dp", scatter_dimension=0, tiled=True).astype(
            jnp.float32
        ),
        lax.psum_scatter(g_ga2.astype(jnp.bfloat16), "dp", scatter_dimension=0, tiled=True).astype(
            jnp.float32
        ),
        lax.psum_scatter(g_ua.astype(jnp.bfloat16), "dp", scatter_dimension=0, tiled=True).astype(
            jnp.float32
        ),
        lax.psum_scatter(g_da.astype(jnp.bfloat16), "dp", scatter_dimension=0, tiled=True).astype(
            jnp.float32
        ),
        lax.psum_scatter(g_gb1.astype(jnp.bfloat16), "dp", scatter_dimension=0, tiled=True).astype(
            jnp.float32
        ),
        lax.psum_scatter(g_qb.astype(jnp.bfloat16), "dp", scatter_dimension=0, tiled=True).astype(
            jnp.float32
        ),
        lax.psum_scatter(g_ob.astype(jnp.bfloat16), "dp", scatter_dimension=0, tiled=True).astype(
            jnp.float32
        ),
        lax.psum_scatter(g_gb2.astype(jnp.bfloat16), "dp", scatter_dimension=0, tiled=True).astype(
            jnp.float32
        ),
        lax.psum_scatter(g_ub.astype(jnp.bfloat16), "dp", scatter_dimension=0, tiled=True).astype(
            jnp.float32
        ),
        lax.psum_scatter(g_db.astype(jnp.bfloat16), "dp", scatter_dimension=0, tiled=True).astype(
            jnp.float32
        ),
    )
    reduced = (
        lax.psum(reduced[0].astype(jnp.bfloat16), "seq").astype(jnp.float32),
        lax.psum(reduced[1].astype(jnp.bfloat16), "seq").astype(jnp.float32),
        lax.psum(reduced[2].astype(jnp.bfloat16), "seq").astype(jnp.float32),
        lax.psum(reduced[3].astype(jnp.bfloat16), "seq").astype(jnp.float32),
        lax.psum(reduced[4].astype(jnp.bfloat16), "seq").astype(jnp.float32),
        lax.psum(reduced[5].astype(jnp.bfloat16), "seq").astype(jnp.float32),
        lax.psum(reduced[6].astype(jnp.bfloat16), "seq").astype(jnp.float32),
        lax.psum(reduced[7].astype(jnp.bfloat16), "seq").astype(jnp.float32),
        lax.psum(reduced[8].astype(jnp.bfloat16), "seq").astype(jnp.float32),
        lax.psum(reduced[9].astype(jnp.bfloat16), "seq").astype(jnp.float32),
        lax.psum(reduced[10].astype(jnp.bfloat16), "seq").astype(jnp.float32),
        lax.psum(reduced[11].astype(jnp.bfloat16), "seq").astype(jnp.float32),
        lax.psum(reduced[12].astype(jnp.bfloat16), "seq").astype(jnp.float32),
    )
    r_route, r_ga1, r_qa, r_oa, r_ga2, r_ua, r_da, r_gb1, r_qb, r_ob, r_gb2, r_ub, r_db = reduced
    return (
        final_rows.astype(jnp.bfloat16),
        grad_input,
        r_route,
        r_ga1,
        r_qa,
        r_oa,
        r_ga2,
        r_ua,
        r_da,
        r_gb1,
        r_qb,
        r_ob,
        r_gb2,
        r_ub,
        r_db,
    )


def solution(mesh):
    return jax.shard_map(
        per_device,
        mesh=mesh,
        in_specs=(
            P("dp", "seq", None),
            P("dp", "seq"),
            P("dp", None),
            P(),
            P(),
            P(),
            P(),
            P(),
            P(),
            P(),
            P(),
            P(),
            P(),
            P(),
            P(),
            P(),
            P("dp", "seq", None),
        ),
        out_specs=(
            P("dp", "seq", None),
            P("dp", "seq", None),
            P("dp"),
            P("dp"),
            P("dp", None),
            P("dp", None),
            P("dp"),
            P("dp", None),
            P("dp", None),
            P("dp"),
            P("dp", None),
            P("dp", None),
            P("dp"),
            P("dp", None),
            P("dp", None),
        ),
        check_vma=False,
    )
```

profile of v0, /device:TPU:0, one launch (start us, length us, event | category | flops | bytes accessed | tf_op | source)
XLA Modules:
  0.0 1333.2 jit_solution(4088721109171331179)
XLA Ops:
  18.3 4.1 gather_fusion
  28.8 10.3 all_gather.13
  41.4 10.6 all_gather.12
  55.7 18.7 %while.60 = (s32[]{:T(128)}, bf16[2,64,768]{1,2,0:T(8,128)(2,1)}, f32[2,12,64,1]{2,1,3,0:T(8,128)}, f32[2,12,64,1]{2,1,3,0:T(8,128)}, bf16[2,256,768]{1,2,0:T(8,...) while((s32[]{:T(128)}, bf16[2,64,768]{1,2,0:T(8,128)(2,1)}, ...), condition=%wide.region_6.7_spmd.clone, body=%wide.region_3.6_spmd.sunk.clone | while | flops 51952128 | bytes 10507465 | solution.py:105
  83.5 21.9 %scatter_fusion = f32[2,256,768]{2,1,0:T(8,128)} fusion(f32[2,256,768]{2,1,0:T(8,128)} %convert_element_type.257, s32[128]{0:T(128)S(1)} %reshape.450, f32[128,768]{1,0:T(8,128)} %bitcast.400), kind=kCustom, calls=%fused_computation.2 | custom fusion | flops 98304 | bytes 1180672 | tf_op jit(solution)/shard_map/scatter-add | solution.py:289
  116.8 24.4 %all-gather.5.cloned.1.call-done = bf16[2,1024,768]{2,1,0:T(8,128)(2,1)} async-done(((bf16[2,256,768]{2,1,0:T(8,128)(2,1)}), bf16[2,1024,768]{2,1,0:T(8,128)(2,1)}) %all-gather.5.cloned.1.call-update) | async-done | bytes 3145744 | tf_op jit(solution)/shard_map/all_gather | solution.py:252
  141.2 4.7 copy.126
  145.9 26.0 %all-gather.3.cloned.1.call-done = bf16[2,1024,768]{2,1,0:T(8,128)(2,1)} async-done(((bf16[2,256,768]{2,1,0:T(8,128)(2,1)}), bf16[2,1024,768]{2,1,0:T(8,128)(2,1)}) %all-gather.3.cloned.1.call-update) | async-done | bytes 3145744 | tf_op jit(solution)/shard_map/all_gather | solution.py:253
  171.9 4.7 copy.124
  178.5 30.6 %while.61 = (s32[]{:T(128)}, bf16[2,256,768]{1,2,0:T(8,128)(2,1)}, f32[2,12,256,1]{2,1,3,0:T(8,128)}, f32[2,12,256,1]{2,1,3,0:T(8,128)}, bf16[2,1024,768]{1,2,0:...) while((s32[]{:T(128)}, bf16[2,256,768]{1,2,0:T(8,128)(2,1)}, ...), condition=%wide.region_13.14_spmd.clone, body=%wide.region_10.13_spmd.sunk.clone | while | flops 843245568 | bytes 70250816 | solution.py:105
  184.6 3.6 fusion.230
  188.3 3.9 fusion.231
  199.9 3.6 fusion.230
  203.6 3.9 fusion.231
  215.3 6.5 fusion.23
  229.6 100.2 %while.62 = (s32[]{:T(128)}, bf16[2,256,768]{2,1,0:T(8,128)(2,1)}, bf16[2,1024,768]{2,1,0:T(8,128)(2,1)}, bf16[2,1024,768]{2,1,0:T(8,128)(2,1)}, bf16[2,1024,768...) while((s32[]{:T(128)}, bf16[2,256,768]{2,1,0:T(8,128)(2,1)}, ...), condition=%wide.region_18.19_spmd.clone, body=%wide.region_16.18_spmd.sunk.clone | while | flops 2046686208 | bytes 136855824 | solution.py:178
  241.4 7.8 multiply_reduce_fusion.16
  249.2 5.5 multiply_convert_fusion.24
  254.6 7.0 fusion.243
  291.6 7.8 multiply_reduce_fusion.16
  299.3 5.5 multiply_convert_fusion.24
  304.8 7.0 fusion.243
  330.6 37.3 %reduce-scatter.15.cloned.1.call-done = bf16[2,256,768]{2,1,0:T(8,128)(2,1)} async-done(((bf16[2,1024,768]{2,1,0:T(8,128)(2,1)}), bf16[2,256,768]{2,1,0:T(8,128)(2,1)}) %reduce-scatter.15.cloned.1.call-update) | async-done | bytes 786448 | tf_op jit(solution)/shard_map/reduce_scatter | solution.py:271
  367.9 40.5 %reduce-scatter.13.cloned.1.call-done = bf16[2,256,768]{2,1,0:T(8,128)(2,1)} async-done(((bf16[2,1024,768]{2,1,0:T(8,128)(2,1)}), bf16[2,256,768]{2,1,0:T(8,128)(2,1)}) %reduce-scatter.13.cloned.1.call-update) | async-done | bytes 786448 | tf_op jit(solution)/shard_map/reduce_scatter | solution.py:268
  408.5 5.0 multiply_reduce_fusion.3
  415.1 4.2 gather_fusion.1
  419.3 4.9 fusion.54
  424.3 5.0 multiply_reduce_fusion.8
  434.1 50.8 %while.63 = (s32[]{:T(128)}, bf16[2,64,768]{2,1,0:T(8,128)(2,1)}, bf16[2,256,768]{2,1,0:T(8,128)(2,1)}, bf16[2,256,768]{2,1,0:T(8,128)(2,1)}, bf16[2,256,768]{1,...) while((s32[]{:T(128)}, bf16[2,64,768]{2,1,0:T(8,128)(2,1)}, ...), condition=%wide.region_25.26_spmd.clone, body=%wide.region_23.25_spmd.sunk.clone | while | flops 128285952 | bytes 15114441 | solution.py:178
  492.0 8.5 bitcast_convert_fusion
  501.2 7.3 bitcast_convert_fusion.1
  509.1 6.0 bitcast_convert_fusion.4
  515.2 19.3 %reduce-scatter.17.cloned.1.call-done = bf16[2,64,768]{2,1,0:T(8,128)(2,1)} async-done(((bf16[2,256,768]{2,1,0:T(8,128)(2,1)}), bf16[2,64,768]{2,1,0:T(8,128)(2,1)}) %reduce-scatter.17.cloned.1.call-update) | async-done | bytes 196624 | tf_op jit(solution)/shard_map/reduce_scatter | solution.py:258
  534.5 4.2 bitcast_convert_fusion.5
  538.8 5.3 bitcast_convert_fusion.2
  544.2 4.9 bitcast_convert_fusion.3
  551.7 51.1 %reduce-scatter.31.cloned.1.call-done = bf16[96,768]{1,0:T(8,128)(2,1)} async-done(((bf16[768,768]{1,0:T(8,128)(2,1)}), bf16[96,768]{1,0:T(8,128)(2,1)}) %reduce-scatter.31.cloned.1.call-update) | async-done | bytes 147472 | tf_op jit(solution)/shard_map/reduce_scatter | solution.py:359
  602.8 67.0 %reduce-scatter.23.cloned.1.call-done = bf16[96,768]{1,0:T(8,128)(2,1)} async-done(((bf16[768,768]{1,0:T(8,128)(2,1)}), bf16[96,768]{1,0:T(8,128)(2,1)}) %reduce-scatter.23.cloned.1.call-update) | async-done | bytes 147472 | tf_op jit(solution)/shard_map/reduce_scatter | solution.py:341
  669.8 98.1 %reduce-scatter.35.cloned.1.call-done = bf16[384,768]{1,0:T(8,128)(2,1)} async-done(((bf16[3072,768]{1,0:T(8,128)(2,1)}), bf16[384,768]{1,0:T(8,128)(2,1)}) %reduce-scatter.35.cloned.1.call-update) | async-done | bytes 589840 | tf_op jit(solution)/shard_map/reduce_scatter | solution.py:368
  767.9 98.5 %reduce-scatter.33.cloned.1.call-done = bf16[96,3072]{1,0:T(8,128)(2,1)} async-done(((bf16[768,3072]{1,0:T(8,128)(2,1)}), bf16[96,3072]{1,0:T(8,128)(2,1)}) %reduce-scatter.33.cloned.1.call-update) | async-done | bytes 589840 | tf_op jit(solution)/shard_map/reduce_scatter | solution.py:365
  866.4 82.7 %reduce-scatter.29.cloned.1.call-done = bf16[96,2304]{1,0:T(8,128)(2,1)} async-done(((bf16[768,2304]{1,0:T(8,128)(2,1)}), bf16[96,2304]{1,0:T(8,128)(2,1)}) %reduce-scatter.29.cloned.1.call-update) | async-done | bytes 442384 | tf_op jit(solution)/shard_map/reduce_scatter | solution.py:356
  949.1 82.3 %reduce-scatter.21.cloned.1.call-done = bf16[96,2304]{1,0:T(8,128)(2,1)} async-done(((bf16[768,2304]{1,0:T(8,128)(2,1)}), bf16[96,2304]{1,0:T(8,128)(2,1)}) %reduce-scatter.21.cloned.1.call-update) | async-done | bytes 442384 | tf_op jit(solution)/shard_map/reduce_scatter | solution.py:338
  1031.3 98.7 %reduce-scatter.27.cloned.1.call-done = bf16[384,768]{1,0:T(8,128)(2,1)} async-done(((bf16[3072,768]{1,0:T(8,128)(2,1)}), bf16[384,768]{1,0:T(8,128)(2,1)}) %reduce-scatter.27.cloned.1.call-update) | async-done | bytes 589840 | tf_op jit(solution)/shard_map/reduce_scatter | solution.py:350
  1130.0 98.5 %reduce-scatter.25.cloned.1.call-done = bf16[96,3072]{1,0:T(8,128)(2,1)} async-done(((bf16[768,3072]{1,0:T(8,128)(2,1)}), bf16[96,3072]{1,0:T(8,128)(2,1)}) %reduce-scatter.25.cloned.1.call-update) | async-done | bytes 589840 | tf_op jit(solution)/shard_map/reduce_scatter | solution.py:347
  1228.6 9.4 add_convert_fusion
  1241.9 19.5 %scatter_fusion.1 = f32[2,256,768]{2,1,0:T(8,128)} fusion(f32[2,256,768]{2,1,0:T(8,128)} %fusion.56, s32[128]{0:T(128)S(1)} %copy-done.7, f32[128,768]{1,0:T(8,128)} %bitcast.399), kind=kCustom, calls=%fused_computation.3 | custom fusion | flops 98304 | bytes 1180672 | tf_op jit(solution)/shard_map/scatter-add | solution.py:328
  1261.4 36.1 %all-reduce.5 = (bf16[768]{0:T(1024)(128)(2,1)}, bf16[768]{0:T(1024)(128)(2,1)}, bf16[768]{0:T(1024)(128)(2,1)}, bf16[768]{0:T(1024)(128)(2,1)}, bf16[768]{0:T(1024)(128)(2,1)}) all-reduce(bf16[768]{0:T(1024)(128)(2,1)S(1)} %copy-done.75, bf16[768]{0:T(1024)(128)(2,1)} %get-tuple-element.391, ...), channel_id=6, replica_groups=mesh['dp'=8,'seq'=4] {'dp'}, use_global_device_ids=true, to_apply=%region_31.32.clone | all-reduce | flops 3840 | bytes 15360
  1301.8 6.7 all-reduce.6
  (436 shorter events, 247.0 us)
Async XLA Ops:
  7.2 100.4 %copy-start = (bf16[768,2304]{1,0:T(8,128)(2,1)S(1)}, bf16[768,2304]{1,0:T(8,128)(2,1)}, u32[]{:S(2)}) copy-start(bf16[768,2304]{1,0:T(8,128)(2,1)} %param.36) | copy-start | bytes 10616836
  7.2 134.0 %all-gather.5.cloned.1.call-start = ((), (), s32[]{:S(2)}) async-start(), calls=%async_computation.13 | async-start | bytes 3932160 | tf_op jit(solution)/shard_map/all_gather | solution.py:252
  11.8 16.2 %copy-start.8 = (s32[128]{0:T(128)}, s32[128]{0:T(128)S(1)}, u32[]{:S(2)}) copy-start(s32[128]{0:T(128)S(1)} %reshape.438) | copy-start | bytes 1540
  11.9 71.5 %copy-start.6 = (s32[128]{0:T(128)}, s32[128]{0:T(128)S(1)}, u32[]{:S(2)}) copy-start(s32[128]{0:T(128)S(1)} %reshape.450) | copy-start | bytes 1540
  13.9 14.1 %copy-start.43 = (f32[768]{0:T(1024)}, f32[768]{0:T(1024)S(1)}, u32[]{:S(2)}) copy-start(f32[768]{0:T(1024)S(1)} %convert_element_type.259) | copy-start | bytes 9220
  14.6 63.1 %copy-start.37 = (f32[768]{0:T(1024)}, f32[768]{0:T(1024)S(1)}, u32[]{:S(2)}) copy-start(f32[768]{0:T(1024)S(1)} %convert_element_type.261) | copy-start | bytes 9220
  28.8 25.6 %copy-start.80 = (s32[2,256]{1,0:T(2,128)S(1)}, s32[2,256]{1,0:T(2,128)}, u32[]{:S(2)}) copy-start(s32[2,256]{1,0:T(2,128)} %select_reduce_fusion) | copy-start | bytes 6148
  28.8 25.6 %copy-start.81 = (s32[256]{0:T(256)S(1)}, s32[256]{0:T(256)}, u32[]{:S(2)}) copy-start(s32[256]{0:T(256)} %and_select_fusion.1) | copy-start | bytes 3076
  55.7 18.7 %copy-start.63 = (f32[1,2,64]{2,0,1:T(1,128)S(1)}, f32[1,2,64]{2,0,1:T(1,128)}, u32[]{:S(2)}) copy-start(f32[1,2,64]{2,0,1:T(1,128)} %fusion.116) | copy-start | bytes 1540
  83.5 24.1 %copy-start.66 = (f32[768]{0:T(1024)S(1)}, f32[768]{0:T(1024)}, u32[]{:S(2)}) copy-start(f32[768]{0:T(1024)} %convert_element_type.264) | copy-start | bytes 9220
  112.5 59.4 %all-gather.3.cloned.1.call-start = ((), (), s32[]{:S(2)}) async-start(), calls=%async_computation.12 | async-start | bytes 3932160 | tf_op jit(solution)/shard_map/all_gather | solution.py:253
  113.3 254.7 %reduce-scatter.15.cloned.1.call-start = ((), (), s32[]{:S(2)}) async-start(), calls=%async_computation.15 | async-start | bytes 3932160 | tf_op jit(solution)/shard_map/reduce_scatter | solution.py:271
  113.6 111.7 %copy-start.46 = (f32[768]{0:T(1024)}, f32[768]{0:T(1024)S(1)}, u32[]{:S(2)}) copy-start(f32[768]{0:T(1024)S(1)} %convert_element_type.266) | copy-start | bytes 9220
  212.2 13.1 copy-start.18
  212.2 13.1 copy-start.55
  215.3 6.5 copy-start.20
  329.8 78.7 %copy-start.67 = (f32[768]{0:T(1024)S(1)}, f32[768]{0:T(1024)}, u32[]{:S(2)}) copy-start(f32[768]{0:T(1024)} %convert_element_type.264) | copy-start | bytes 9220
  329.8 78.7 %copy-start.77 = (f32[2,256]{1,0:T(2,128)S(1)}, f32[2,256]{1,0:T(2,128)}, u32[]{:S(2)}) copy-start(f32[2,256]{1,0:T(2,128)} %copy-done.76) | copy-start | bytes 6148
  329.8 78.6 %reduce-scatter.13.cloned.1.call-start = ((), (), s32[]{:S(2)}) async-start(), calls=%async_computation.14 | async-start | bytes 3932160 | tf_op jit(solution)/shard_map/reduce_scatter | solution.py:268
  330.4 184.8 %reduce-scatter.19.cloned.1.call-start = ((), (), s32[]{:S(2)}) async-start(), calls=%async_computation.17 | async-start | bytes 983040 | tf_op jit(solution)/shard_map/reduce_scatter | solution.py:261
  408.5 5.1 copy-start.17
  424.3 6.7 copy-start.25
  424.3 6.7 copy-start.64
  484.8 49.7 %reduce-scatter.17.cloned.1.call-start = ((), (), s32[]{:S(2)}) async-start(), calls=%async_computation.16 | async-start | bytes 983040 | tf_op jit(solution)/shard_map/reduce_scatter | solution.py:258
  485.4 117.3 %reduce-scatter.31.cloned.1.call-start = ((), (), s32[]{:S(2)}) async-start(), calls=%async_computation.23 | async-start | bytes 1327104 | tf_op jit(solution)/shard_map/reduce_scatter | solution.py:359
  488.9 180.8 %reduce-scatter.23.cloned.1.call-start = ((), (), s32[]{:S(2)}) async-start(), calls=%async_computation.19 | async-start | bytes 1327104 | tf_op jit(solution)/shard_map/reduce_scatter | solution.py:341
  491.7 276.2 %reduce-scatter.35.cloned.1.call-start = ((), (), s32[]{:S(2)}) async-start(), calls=%async_computation.25 | async-start | bytes 5308416 | tf_op jit(solution)/shard_map/reduce_scatter | solution.py:368
  500.5 365.9 %reduce-scatter.33.cloned.1.call-start = ((), (), s32[]{:S(2)}) async-start(), calls=%async_computation.24 | async-start | bytes 5308416 | tf_op jit(solution)/shard_map/reduce_scatter | solution.py:365
  508.5 440.6 %reduce-scatter.29.cloned.1.call-start = ((), (), s32[]{:S(2)}) async-start(), calls=%async_computation.22 | async-start | bytes 3981312 | tf_op jit(solution)/shard_map/reduce_scatter | solution.py:356
  515.1 19.4 %copy-start.44 = (f32[768]{0:T(1024)S(1)}, f32[768]{0:T(1024)}, u32[]{:S(2)}) copy-start(f32[768]{0:T(1024)} %copy-done.43) | copy-start | bytes 9220
  515.1 19.4 %copy-start.60 = (f32[2,64]{1,0:T(2,128)S(1)}, f32[2,64]{1,0:T(2,128)}, u32[]{:S(2)}) copy-start(f32[2,64]{1,0:T(2,128)} %copy-done.59) | copy-start | bytes 1540
  515.2 516.2 %reduce-scatter.21.cloned.1.call-start = ((), (), s32[]{:S(2)}) async-start(), calls=%async_computation.18 | async-start | bytes 3981312 | tf_op jit(solution)/shard_map/reduce_scatter | solution.py:338
  538.7 591.3 %reduce-scatter.27.cloned.1.call-start = ((), (), s32[]{:S(2)}) async-start(), calls=%async_computation.21 | async-start | bytes 5308416 | tf_op jit(solution)/shard_map/reduce_scatter | solution.py:350
  544.1 684.4 %reduce-scatter.25.cloned.1.call-start = ((), (), s32[]{:S(2)}) async-start(), calls=%async_computation.20 | async-start | bytes 5308416 | tf_op jit(solution)/shard_map/reduce_scatter | solution.py:347
  549.1 765.2 %all-reduce.10.cloned.1.call-start = ((), (), s32[]{:S(2)}) async-start(), calls=%async_computation.26 | async-start | bytes 7077888 | tf_op jit(solution)/shard_map/psum | solution.py:375
  1228.6 9.5 copy-start.15
  1228.6 9.5 copy-start.69
  1228.6 10.3 copy-start.21
  1228.6 10.3 copy-start.52
  1228.6 10.3 copy-start.53
  1228.6 10.3 copy-start.54
  1241.9 19.5 %copy-start.74 = (bf16[768]{0:T(1024)(128)(2,1)S(1)}, bf16[768]{0:T(1024)(128)(2,1)}, u32[]{:S(2)}) copy-start(bf16[768]{0:T(1024)(128)(2,1)} %get-tuple-element.389) | copy-start | bytes 4612
  1241.9 19.5 %copy-start.75 = (bf16[768]{0:T(1024)(128)(2,1)S(1)}, bf16[768]{0:T(1024)(128)(2,1)}, u32[]{:S(2)}) copy-start(bf16[768]{0:T(1024)(128)(2,1)} %convolution_reduce_fusion) | copy-start | bytes 4612
  1241.9 19.5 %copy-start.87 = (bf16[768]{0:T(1024)(128)(2,1)S(1)}, bf16[768]{0:T(1024)(128)(2,1)}, u32[]{:S(2)}) copy-start(bf16[768]{0:T(1024)(128)(2,1)} %get-tuple-element.385) | copy-start | bytes 4612
  1314.4 7.5 copy-start.42
  1314.4 8.6 copy-start.41
  1317.8 6.3 copy-start.40
  1319.8 5.4 copy-start.39
  (74 other events, 204.4 us)
Sparse Core Ops, SparseCore 0:
  112.6 28.5 all-gather.4
  143.4 28.5 all-gather.2
  329.9 37.9 reduce-scatter.14
  370.5 37.9 reduce-scatter.12
  485.0 23.1 reduce-scatter.18
  511.3 23.2 reduce-scatter.16
  538.5 64.2 reduce-scatter.30
  606.7 63.0 reduce-scatter.22
  673.4 94.3 reduce-scatter.34
  771.3 95.0 reduce-scatter.32
  870.0 78.9 reduce-scatter.28
  952.5 78.7 reduce-scatter.20
  1035.0 94.9 reduce-scatter.26
  1133.5 95.0 reduce-scatter.24
  1231.3 75.9 all-reduce.9
where the time goes:
time: 1350 us; the launch traced here: 1330 us
  waiting for transfers between devices  826 us (61%)
  matrix products  174 us (13%)
  local copies, waits for them, and re-layouts  154 us (11%)
  other arithmetic  96.9 us (7%)
  blocking collectives  63.8 us (5%)
  between operations  15.7 us (1%)
    reduce_scatter x1, waiting for transfers between devices, per_device(): lax.psum_scatter(g_da.astype(jnp.bfloat16), 'dp', scatter_dimension=0, ti...  98.7 us
    reduce_scatter x1, waiting for transfers between devices, per_device(): lax.psum_scatter(g_ua.astype(jnp.bfloat16), 'dp', scatter_dimension=0, ti...  98.5 us
    reduce_scatter x1, waiting for transfers between devices, per_device(): lax.psum_scatter(g_ub.astype(jnp.bfloat16), 'dp', scatter_dimension=0, ti...  98.5 us
    reduce_scatter x1, waiting for transfers between devices, per_device(): lax.psum_scatter(g_db.astype(jnp.bfloat16), 'dp', scatter_dimension=0, ti...  98.1 us
    reduce_scatter x1, waiting for transfers between devices, per_device(): lax.psum_scatter(g_qb.astype(jnp.bfloat16), 'dp', scatter_dimension=0, ti...  82.7 us
    reduce_scatter x1, waiting for transfers between devices, per_device(): lax.psum_scatter(g_qa.astype(jnp.bfloat16), 'dp', scatter_dimension=0, ti...  82.3 us
    reduce_scatter x1, waiting for transfers between devices, per_device(): lax.psum_scatter(g_oa.astype(jnp.bfloat16), 'dp', scatter_dimension=0, ti...  67 us
    reduce_scatter x1, waiting for transfers between devices, per_device(): lax.psum_scatter(g_ob.astype(jnp.bfloat16), 'dp', scatter_dimension=0, ti...  51.1 us
  transfers between devices with their start and end apart: 15, of which 13 were waited for; matrix products, arithmetic and copies ran while one was open for 7% of the time, Pallas kernels for 0%

commit v1 on v0

v1 whole, which is shorter than its diff:
```python
import jax
import jax.numpy as jnp
from jax import lax
from jax.experimental import pallas as pl
from jax.experimental.pallas import tpu as pltpu
from jax.sharding import PartitionSpec as P

HEADS = 12
HEAD_DIM = 64
EPSILON = 1e-06
EXACT = lax.Precision.HIGHEST
F32 = jnp.float32
BF16 = jnp.bfloat16
OWNERS = 4
LANES = 128
BLOCK = 256
VMEM_BYTES = 60 * 1024 * 1024

SMEM_SPEC = pl.BlockSpec(memory_space=pltpu.SMEM)
VMEM_SPEC = pl.BlockSpec(memory_space=pltpu.VMEM)
NT = (((1,), (1,)), ((), ()))
TN = (((0,), (0,)), ((), ()))


def dot(left, right, dims=(((1,), (0,)), ((), ()))):
    return lax.dot_general(left, right, dims, preferred_element_type=F32)


def cost(flops, moved, exps=0):
    return pl.CostEstimate(flops=int(flops), bytes_accessed=int(moved), transcendentals=int(exps))


def project_kernel(place, x_ref, gain_ref, w_ref, act_ref, *outs):
    width = x_ref.shape[-1]
    half = width // 2
    for i in range(2):
        x = x_ref[i].astype(F32)
        scale = lax.rsqrt(jnp.mean(x * x, axis=-1, keepdims=True) + EPSILON)
        act_ref[i] = (x * scale * gain_ref[...].astype(F32)).astype(BF16)
    for r in (3, 2, 1, 0):
        act = act_ref[place[0] ^ (r >> 1)]
        at = (place[1] ^ (r & 1)) * half
        for part in range(3):
            columns = pl.ds(pl.multiple_of(part * width + at, LANES), half)
            outs[r][part] = dot(act, w_ref[:, columns]).astype(BF16)


def project_pieces(place, x, gain, weight):
    seqs, rows, width = x.shape
    piece = jax.ShapeDtypeStruct((3, rows, width // 2), BF16)
    outs = pl.pallas_call(
        project_kernel,
        name="project_pieces",
        out_shape=[jax.ShapeDtypeStruct(x.shape, BF16)] + [piece] * OWNERS,
        in_specs=[SMEM_SPEC] + [VMEM_SPEC] * 3,
        out_specs=[VMEM_SPEC] * (1 + OWNERS),
        compiler_params=pltpu.CompilerParams(vmem_limit_bytes=VMEM_BYTES),
        cost_estimate=cost(
            2 * seqs * rows * width * 3 * width, 6 * width * width + 12 * seqs * rows * width
        ),
    )(place, x, gain.reshape(1, width), weight)
    return outs[0], outs[1:]


def lane_head(head):
    lanes = lax.broadcasted_iota(jnp.int32, (1, LANES), 1)
    return (lanes < HEAD_DIM) if head == 0 else (lanes >= HEAD_DIM)


def only_head(x, head):
    return jnp.where(lane_head(head), x, jnp.zeros_like(x))


def slot_matrix(chosen_ref, counts, owner, rows):
    slots = chosen_ref.shape[1]
    spots = chosen_ref[pl.ds(owner, 1), :]
    row_ids = lax.broadcasted_iota(jnp.int32, (rows, slots), 0)
    slot_ids = lax.broadcasted_iota(jnp.int32, (rows, slots), 1)
    return jnp.where((row_ids == spots) & (slot_ids < counts[owner]), 1.0, 0.0)


def diagonal_mask(counts, query_axis, rows, routed):
    shape = (BLOCK, BLOCK)
    queries = lax.broadcasted_iota(jnp.int32, shape, query_axis)
    keys = lax.broadcasted_iota(jnp.int32, shape, 1 - query_axis)
    if not routed:
        return keys <= queries
    owner = keys // rows
    load = jnp.where(
        owner == 0,
        counts[0],
        jnp.where(owner == 1, counts[1], jnp.where(owner == 2, counts[2], counts[3])),
    )
    live = (keys - owner * rows) < load
    return (keys == queries) | ((keys < queries) & live)


def attend_kernel(rows, routed, place, counts, *refs):
    if routed:
        base, refs = refs[:OWNERS], refs[OWNERS:]
    else:
        chosen_ref, base, slot_in = refs[0], refs[1 : 1 + OWNERS], refs[1 + OWNERS : 1 + 2 * OWNERS]
        refs = refs[1 + 2 * OWNERS :]
    outs, (merged, stats, mixed) = refs[:OWNERS], refs[OWNERS:]
    me = 2 * place[0] + place[1]
    blocks = OWNERS * rows // BLOCK
    for r in range(OWNERS):
        owner = me ^ r
        at = pl.ds(pl.multiple_of(owner * rows, rows), rows)
        if routed:
            for part in range(3):
                merged[part, at, :] = base[r][part]
        else:
            spots = slot_matrix(chosen_ref, counts, owner, rows)
            covered = jnp.max(spots, axis=1, keepdims=True) > 0.5
            spots = spots.astype(BF16)
            for part in range(3):
                placed = dot(spots, slot_in[r][part])
                merged[part, at, :] = jnp.where(
                    covered, placed, base[r][part].astype(F32)
                ).astype(BF16)
    visible = diagonal_mask(counts, 0, rows, routed)
    for a in range(blocks):
        queries = merged[0, a * BLOCK : (a + 1) * BLOCK, :] * jnp.asarray(HEAD_DIM**-0.5, BF16)
        mixture = jnp.zeros((BLOCK, LANES), F32)
        stat = jnp.zeros((BLOCK, LANES), F32)
        for head in range(2):
            own = only_head(queries, head)
            scores = []
            for b in range(a + 1):
                keys = merged[1, b * BLOCK : (b + 1) * BLOCK, :]
                found = dot(own, keys, NT)
                scores.append(jnp.where(visible, found, -1e30) if b == a else found)
            top = scores[0]
            for found in scores[1:]:
                top = jnp.maximum(top, found)
            top = jnp.max(top, axis=1, keepdims=True)
            total = jnp.zeros((BLOCK, BLOCK), F32)
            part = jnp.zeros((BLOCK, LANES), F32)
            for b in range(a + 1):
                weight = jnp.exp(scores[b] - top)
                total = total + weight
                values = only_head(merged[2, b * BLOCK : (b + 1) * BLOCK, :], head)
                part = part + dot(weight.astype(BF16), values)
            total = jnp.sum(total, axis=1, keepdims=True)
            mixture = mixture + part * (1.0 / total)
            lane = lax.broadcasted_iota(jnp.int32, (1, LANES), 1)
            stat = jnp.where(lane == head, top + jnp.log(total), stat)
        mixed[a * BLOCK : (a + 1) * BLOCK, :] = mixture.astype(BF16)
        stats[0, :, a * BLOCK : (a + 1) * BLOCK] = stat.T[:8, :]
    for r in range(OWNERS):
        at = pl.ds(pl.multiple_of((me ^ r) * rows, rows), rows)
        outs[r][...] = mixed[at, :]


def attend(place, counts, base, chosen=None, slots=None):
    routed = slots is None
    _, rows, half = base[0].shape
    pairs = half // LANES
    length = OWNERS * rows
    inputs = [place, counts]
    specs = [SMEM_SPEC, SMEM_SPEC]
    if not routed:
        inputs.append(chosen)
        specs.append(VMEM_SPEC)
    for group in (base, slots):
        if group is not None:
            inputs += list(group)
            specs += [
                pl.BlockSpec((3, group[0].shape[1], LANES), lambda h: (0, 0, h))
            ] * OWNERS
    blocks = length // BLOCK
    work = blocks * (blocks + 1) // 2 * BLOCK * BLOCK * 2 * pairs
    outs = pl.pallas_call(
        lambda *refs: attend_kernel(rows, routed, *refs),
        name="attend_routed" if routed else "attend_dense",
        grid=(pairs,),
        out_shape=[jax.ShapeDtypeStruct((rows, half), BF16)] * OWNERS
        + [
            jax.ShapeDtypeStruct((3, length, half), BF16),
            jax.ShapeDtypeStruct((pairs, 8, length), F32),
        ],
        in_specs=specs,
        out_specs=[pl.BlockSpec((rows, LANES), lambda h: (0, h))] * OWNERS
        + [
            pl.BlockSpec((3, length, LANES), lambda h: (0, 0, h)),
            pl.BlockSpec((1, 8, length), lambda h: (h, 0, 0)),
        ],
        scratch_shapes=[pltpu.VMEM((length, LANES), BF16)],
        compiler_params=pltpu.CompilerParams(vmem_limit_bytes=VMEM_BYTES),
        cost_estimate=cost(16 * HEAD_DIM * work, 16 * length * half, work),
    )(*inputs)
    return outs[:OWNERS], outs[OWNERS], outs[OWNERS + 1]


def attend_back_kernel(rows, routed, place, counts, *refs):
    if not routed:
        chosen_ref, refs = refs[0], refs[1:]
    merged, stats, grads = refs[0], refs[1], refs[2 : 2 + OWNERS]
    outs, refs = refs[2 + OWNERS : 2 + 2 * OWNERS], refs[2 + 2 * OWNERS :]
    if not routed:
        slot_outs, refs = refs[:OWNERS], refs[OWNERS:]
    incoming, grad_q, grad_k, grad_v = refs
    me = 2 * place[0] + place[1]
    blocks = OWNERS * rows // BLOCK
    for r in range(OWNERS):
        at = pl.ds(pl.multiple_of((me ^ r) * rows, rows), rows)
        incoming[at, :] = grads[r][...]
    for ref in (grad_q, grad_k, grad_v):
        ref[...] = jnp.zeros_like(ref)
    visible = diagonal_mask(counts, 1, rows, routed)
    for a in range(blocks):
        span = slice(a * BLOCK, (a + 1) * BLOCK)
        queries = merged[0, span, :] * jnp.asarray(HEAD_DIM**-0.5, BF16)
        grad_mix = incoming[span, :]
        grad_query = jnp.zeros((BLOCK, LANES), F32)
        for head in range(2):
            own_q = only_head(queries, head)
            own_g = only_head(grad_mix, head)
            level = stats[0, head : head + 1, span]
            probs, grad_probs = [], []
            inner = jnp.zeros((1, BLOCK), F32)
            for b in range(a + 1):
                keys_at = slice(b * BLOCK, (b + 1) * BLOCK)
                prob = jnp.exp(dot(merged[1, keys_at, :], own_q, NT) - level)
                if b == a:
                    prob = jnp.where(visible, prob, 0.0)
                grad_prob = dot(merged[2, keys_at, :], own_g, NT)
                grad_v[keys_at, :] += dot(prob.astype(BF16), own_g)
                inner = inner + jnp.sum(prob * grad_prob, axis=0, keepdims=True)
                probs.append(prob)
                grad_probs.append(grad_prob)
            for b in range(a + 1):
                keys_at = slice(b * BLOCK, (b + 1) * BLOCK)
                grad_score = (probs[b] * (grad_probs[b] - inner)).astype(BF16)
                grad_k[keys_at, :] += dot(grad_score, own_q)
                own_k = only_head(merged[1, keys_at, :], head)
                grad_query = grad_query + dot(grad_score, own_k, TN)
        grad_q[span, :] = grad_query * HEAD_DIM**-0.5
    for r in range(OWNERS):
        owner = me ^ r
        at = pl.ds(pl.multiple_of(owner * rows, rows), rows)
        if not routed:
            spots = slot_matrix(chosen_ref, counts, owner, rows).astype(BF16)
        for part, ref in enumerate((grad_q, grad_k, grad_v)):
            found = ref[at, :].astype(BF16)
            outs[r][part] = found
            if not routed:
                slot_outs[r][part] = dot(spots, found, TN).astype(BF16)


def attend_back(place, counts, merged, stats, grads, chosen=None):
    routed = chosen is None
    rows, half = grads[0].shape
    pairs = half // LANES
    length = OWNERS * rows
    inputs = [place, counts]
    specs = [SMEM_SPEC, SMEM_SPEC]
    shapes = [jax.ShapeDtypeStruct((3, rows, half), BF16)] * OWNERS
    out_specs = [pl.BlockSpec((3, rows, LANES), lambda h: (0, 0, h))] * OWNERS
    if not routed:
        inputs.append(chosen)
        specs.append(VMEM_SPEC)
        slots = chosen.shape[1]
        shapes += [jax.ShapeDtypeStruct((3, slots, half), BF16)] * OWNERS
        out_specs += [pl.BlockSpec((3, slots, LANES), lambda h: (0, 0, h))] * OWNERS
    inputs += [merged, stats] + list(grads)
    specs += [
        pl.BlockSpec((3, length, LANES), lambda h: (0, 0, h)),
        pl.BlockSpec((1, 8, length), lambda h: (h, 0, 0)),
    ] + [pl.BlockSpec((rows, LANES), lambda h: (0, h))] * OWNERS
    blocks = length // BLOCK
    work = blocks * (blocks + 1) // 2 * BLOCK * BLOCK * 2 * pairs
    outs = pl.pallas_call(
        lambda *refs: attend_back_kernel(rows, routed, *refs),
        name="attend_routed_back" if routed else "attend_dense_back",
        grid=(pairs,),
        out_shape=shapes,
        in_specs=specs,
        out_specs=out_specs,
        scratch_shapes=[pltpu.VMEM((length, LANES), BF16)]
        + [pltpu.VMEM((length, LANES), F32)] * 3,
        compiler_params=pltpu.CompilerParams(vmem_limit_bytes=VMEM_BYTES),
        cost_estimate=cost(40 * HEAD_DIM * work, 16 * length * half, work),
    )(*inputs)
    return outs[:OWNERS], outs[OWNERS:]


def bit_reverse(number, bits):
    found = 0
    for k in range(bits):
        found = found | (((number >> k) & 1) << (bits - 1 - k))
    return found


def store_slabs(ref, found, first, slab_rows, at, place, bits):
    for d in range(found.shape[0] // slab_rows):
        spot = bit_reverse(first + d, bits) ^ place[2]
        ref[pl.ds(spot, 1), at : at + slab_rows, :] = found[
            d * slab_rows : (d + 1) * slab_rows
        ].astype(BF16)[None]


def feed_grad_kernel(bits, place, ff_ref, gh_ref, gel_ref, gff_ref, send_ref, own_ref):
    step, kind, tile = pl.program_id(0), pl.program_id(1), pl.program_id(2)
    width = ff_ref.shape[1]
    slabs = 1 << bits
    narrow, wide = width // slabs, OWNERS * width // slabs
    for core_step, ref in ((0, send_ref), (1, own_ref)):
        for t in range(OWNERS):

            @pl.when((step == core_step) & (kind == 0) & (tile == t))
            def _():
                found = dot(ff_ref[...], gh_ref[...], TN)
                store_slabs(ref, found, 0, narrow, t * narrow, place, bits)

            @pl.when((step == core_step) & (kind == 1) & (tile == t))
            def _():
                found = dot(gel_ref[...], gff_ref[...], TN)
                store_slabs(
                    ref, found, t * slabs // OWNERS, wide, OWNERS * narrow, place, bits
                )


def feed_grad(place, bits, ff_in, grad_hidden, activated, grad_ff):
    tokens, width = ff_in.shape
    half = width // 2
    slabs = 1 << bits
    rows = 2 * OWNERS * width // slabs

    def half_of(step, place_ref):
        return place_ref[1] ^ (1 - step)

    return pl.pallas_call(
        lambda *refs: feed_grad_kernel(bits, *refs),
        name="feed_grad",
        grid_spec=pltpu.PrefetchScalarGridSpec(
            num_scalar_prefetch=1,
            grid=(2, 2, OWNERS),
            in_specs=[
                pl.BlockSpec((tokens, width), lambda s, k, t, p: (0, 0)),
                pl.BlockSpec(
                    (tokens, half),
                    lambda s, k, t, p: (
                        0,
                        half_of(s, p) * OWNERS + jnp.where(k == 0, t, OWNERS - 1),
                    ),
                ),
                pl.BlockSpec((tokens, width), lambda s, k, t, p: (0, jnp.where(k == 0, 0, t))),
                pl.BlockSpec((tokens, half), lambda s, k, t, p: (0, half_of(s, p))),
            ],
            out_specs=[pl.BlockSpec((slabs, rows, half), lambda s, k, t, p: (0, 0, 0))] * 2,
        ),
        out_shape=[jax.ShapeDtypeStruct((slabs, rows, half), BF16)] * 2,
        compiler_params=pltpu.CompilerParams(vmem_limit_bytes=VMEM_BYTES),
        cost_estimate=cost(
            16 * tokens * width * width, 16 * width * width + 20 * tokens * width
        ),
    )(place, ff_in, grad_hidden, activated, grad_ff)


def mix_grad_kernel(bits, place, act_ref, p0, p1, p2, p3, mix_ref, gatt_ref, send_ref, own_ref):
    width = act_ref.shape[-1]
    half = width // 2
    narrow = width // (1 << bits)
    pieces = (p0, p1, p2, p3)
    for other, ref in ((1, send_ref), (0, own_ref)):
        for part in range(3):
            found = dot(act_ref[place[0]], pieces[other][part], TN)
            found = found + dot(act_ref[1 - place[0]], pieces[2 + other][part], TN)
            store_slabs(ref, found, 0, narrow, part * narrow, place, bits)
        columns = pl.ds(pl.multiple_of((place[1] ^ other) * half, LANES), half)
        found = dot(mix_ref[0], gatt_ref[0, :, columns], TN)
        found = found + dot(mix_ref[1], gatt_ref[1, :, columns], TN)
        store_slabs(ref, found, 0, narrow, 3 * narrow, place, bits)


def mix_grad(place, bits, act, pieces, mixture, grad_attended):
    seqs, rows, width = act.shape
    half = width // 2
    slabs = 1 << bits
    shape = jax.ShapeDtypeStruct((slabs, OWNERS * width // slabs, half), BF16)
    return pl.pallas_call(
        lambda *refs: mix_grad_kernel(bits, *refs),
        name="mix_grad",
        in_specs=[SMEM_SPEC] + [VMEM_SPEC] * 7,
        out_specs=[VMEM_SPEC] * 2,
        out_shape=[shape] * 2,
        compiler_params=pltpu.CompilerParams(vmem_limit_bytes=VMEM_BYTES),
        cost_estimate=cost(
            8 * seqs * rows * width * width, 8 * width * width + 12 * seqs * rows * width
        ),
    )(place, act, *pieces, mixture, grad_attended)


def swap(x, axis, bit):
    size = lax.axis_size(axis)
    return lax.ppermute(x, axis, [(i, i ^ bit) for i in range(size)])


def exchange(pieces):
    return [pieces[0]] + [swap(pieces[r], "seq", r) for r in range(1, OWNERS)]


def add_low(a, b):
    return (a.astype(F32) + b.astype(F32)).astype(BF16)


def reduce_group(send, own, bits):
    current = add_low(own, swap(send, "seq", 1))
    for k in range(bits):
        n = current.shape[0] // 2
        current = add_low(current[:n], swap(current[n:], "dp", 1 << k))
    current = add_low(current, swap(current, "seq", 2))
    return current[0], swap(current, "seq", 1)[0]


def both_halves(own, other, first):
    return jnp.concatenate(
        [jnp.where(first, own, other), jnp.where(first, other, own)], axis=-1
    )


def assemble(pieces, y_first, core_first):
    near = both_halves(pieces[0], pieces[1], core_first)
    far = both_halves(pieces[2], pieces[3], core_first)
    return jnp.stack([jnp.where(y_first, near, far), jnp.where(y_first, far, near)])


def assemble_packed(pieces, y_first, core_first):
    found = assemble(pieces, y_first, core_first)
    return jnp.concatenate([found[:, 0], found[:, 1], found[:, 2]], axis=-1)


def split_pieces(x, place):
    half = x.shape[-1] // 2
    found = []
    for r in range(OWNERS):
        rows = lax.dynamic_index_in_dim(x, place[0] ^ (r >> 1), 0, keepdims=False)
        found.append(lax.dynamic_slice_in_dim(rows, (place[1] ^ (r & 1)) * half, half, axis=1))
    return found


def norm_rows(vector, gain_vec):
    return (
        vector * lax.rsqrt(jnp.mean(vector * vector, axis=-1, keepdims=True) + EPSILON) * gain_vec
    )


def project(left_side, weight):
    return jnp.einsum("bnd,de->bne", left_side, weight, preferred_element_type=F32)


def project_back(gradient, weight):
    return jnp.einsum("bne,de->bnd", gradient, weight, preferred_element_type=F32)


def feed_forward(resid, router, mixture, w_out, gain_two, w_up, w_down):
    attended = project(mixture, w_out)
    middle = resid + attended if router is None else resid + router[..., None] * attended
    ff_in = norm_rows(middle, gain_two.astype(F32)).astype(BF16)
    hidden = project(ff_in, w_up)
    activated = jax.nn.gelu(hidden).astype(BF16)
    done = middle + project(activated, w_down)
    return done, (attended, middle, ff_in, hidden, activated)


def feed_backward(grad_done, router, w_out, gain_two, w_up, w_down, kept):
    attended, middle, ff_in, hidden, activated = kept
    grad_ff = grad_done.astype(BF16)
    grad_act = project_back(grad_ff, w_down)
    unused_value, gelu_pull = jax.vjp(jax.nn.gelu, hidden)
    grad_hidden = gelu_pull(grad_act)[0].astype(BF16)
    grad_ffin = project_back(grad_hidden, w_up)
    unused_norm, norm_pull = jax.vjp(norm_rows, middle, gain_two.astype(F32))
    grad_mid_norm, grad_gain_two = norm_pull(grad_ffin)
    grad_middle = grad_done + grad_mid_norm
    scaled = grad_middle if router is None else router[..., None] * grad_middle
    grad_attended = scaled.astype(BF16)
    grad_mixture = project_back(grad_attended, w_out).astype(BF16)
    return grad_ff, grad_hidden, grad_middle, grad_gain_two, grad_attended, grad_mixture


def norm_back(x, gain, grad_act_in):
    unused, pull = jax.vjp(norm_rows, x, gain.astype(F32))
    return pull(grad_act_in)


def per_device(
    stream_in,
    chosen,
    counts,
    route_w,
    gain_a1,
    qkv_a,
    out_a,
    gain_a2,
    up_a,
    down_a,
    gain_b1,
    qkv_b,
    out_b,
    gain_b2,
    up_b,
    down_b,
    cotangent,
):
    seqs, rows, width = stream_in.shape
    slots = chosen.shape[1]
    half = width // 2
    dp_size = lax.axis_size("dp")
    bits = dp_size.bit_length() - 1
    me = lax.axis_index("seq")
    y_at, core_at = me // 2, me % 2
    y_first, core_first = y_at == 0, core_at == 0
    place = jnp.stack(
        [y_at, core_at, bit_reverse(lax.axis_index("dp"), bits)]
    ).astype(jnp.int32)
    chosen_all = lax.all_gather(chosen, "seq", axis=0)
    chosen_mine = lax.dynamic_index_in_dim(chosen_all, y_at, 1, keepdims=False)
    counts_mine = lax.dynamic_index_in_dim(counts, y_at, 0, keepdims=False)
    own_load = lax.dynamic_index_in_dim(counts, me, 1, keepdims=False)
    live = jnp.arange(slots, dtype=jnp.int32)[None, :] < own_load[:, None]
    hits = chosen[:, :, None] == jnp.arange(rows, dtype=jnp.int32)
    gather = hits.astype(BF16)
    live_hits = (hits & live[..., None]).astype(F32)
    covered = jnp.any(hits & live[..., None], axis=1)[..., None]

    def scatter(values):
        return jnp.einsum("bcr,bcd->brd", live_hits, values, precision=EXACT)

    act_base, base = project_pieces(place, stream_in, gain_b1, qkv_b)

    picked = jnp.einsum("bcr,brd->bcd", gather, stream_in, preferred_element_type=F32)
    picked_low = picked.astype(BF16)
    router = jnp.einsum("bcd,d->bc", picked_low, route_w, preferred_element_type=F32)
    act_a, pieces = project_pieces(place, picked_low, gain_a1, qkv_a)
    mixed, merged_a, stats_a = attend(place, counts_mine, exchange(pieces))
    base = exchange(base)
    mixture_a = assemble(exchange(mixed), y_first, core_first)
    done_a, kept_a = feed_forward(picked, router, mixture_a, out_a, gain_a2, up_a, down_a)
    change = jnp.where(live[..., None], done_a - picked, 0.0)
    slot_mid = picked + change
    act_slot, slot_pieces = project_pieces(place, slot_mid, gain_b1, qkv_b)
    mixed, merged_b, stats_b = attend(
        place, counts_mine, base, chosen_mine, exchange(slot_pieces)
    )
    mixture_b = assemble(exchange(mixed), y_first, core_first)
    middle = stream_in.astype(F32) + scatter(change)
    done_b, kept_b = feed_forward(middle, None, mixture_b, out_b, gain_b2, up_b, down_b)

    grad_ff_b, grad_hidden_b, grad_mid_b, g_gb2, grad_att_b, grad_mix_b = feed_backward(
        cotangent.astype(F32), None, out_b, gain_b2, up_b, down_b, kept_b
    )
    grads = exchange(split_pieces(grad_mix_b, place))
    flat = lambda x: x.reshape(x.shape[0] * x.shape[1], x.shape[2])
    feed_b = reduce_group(
        *feed_grad(
            place, bits, flat(kept_b[2]), flat(grad_hidden_b), flat(kept_b[4]), flat(grad_ff_b)
        ),
        bits,
    )
    packed_b, packed_slot = attend_back(place, counts_mine, merged_b, stats_b, grads, chosen_mine)
    packed_slot = exchange(packed_slot)
    grad_packed_slot = assemble_packed(packed_slot, y_first, core_first)
    packed_b = exchange(packed_b)

    slot_grad, _ = norm_back(slot_mid, gain_b1, project_back(grad_packed_slot, qkv_b))
    mid_at_slot = jnp.einsum("bcr,brd->bcd", live_hits, grad_mid_b, precision=EXACT)
    grad_done = jnp.where(live[..., None], mid_at_slot + slot_grad, 0.0)
    grad_ff_a, grad_hidden_a, grad_mid_a, g_ga2, grad_att_a, grad_mix_a = feed_backward(
        grad_done, router, out_a, gain_a2, up_a, down_a, kept_a
    )
    grad_router = jnp.sum(kept_a[0] * grad_mid_a, axis=-1)
    grads = exchange(split_pieces(grad_mix_a, place))
    feed_a = reduce_group(
        *feed_grad(
            place, bits, flat(kept_a[2]), flat(grad_hidden_a), flat(kept_a[4]), flat(grad_ff_a)
        ),
        bits,
    )
    packed_a, _ = attend_back(place, counts_mine, merged_a, stats_a, grads)
    packed_a = exchange(packed_a)
    mix_a = reduce_group(*mix_grad(place, bits, act_a, packed_a, mixture_a, grad_att_a), bits)
    grad_packed_a = assemble_packed(packed_a, y_first, core_first)
    res_a, g_ga1 = norm_back(picked, gain_a1, project_back(grad_packed_a, qkv_a))
    grad_picked = (
        grad_mid_a + res_a + grad_router[..., None] * route_w.astype(F32) - grad_done
    )
    grad_route = jnp.einsum("bc,bcd->d", grad_router, picked, precision=EXACT)

    act_b = jnp.where(
        covered,
        jnp.einsum("bcr,bcd->brd", live_hits.astype(BF16), act_slot, preferred_element_type=F32),
        act_base.astype(F32),
    ).astype(BF16)
    mix_b = reduce_group(*mix_grad(place, bits, act_b, packed_b, mixture_b, grad_att_b), bits)
    grad_packed_b = assemble_packed(packed_b, y_first, core_first)
    res_b, g_gb1 = norm_back(middle, gain_b1, project_back(grad_packed_b, qkv_b))
    grad_input = grad_mid_b + res_b + scatter(grad_picked)

    small = lax.psum(jnp.stack([grad_route, g_ga1, g_ga2, g_gb1, g_gb2]), ("dp", "seq"))
    small = lax.dynamic_slice_in_dim(
        small, lax.axis_index("dp") * (width // dp_size), width // dp_size, axis=1
    )

    narrow, wide = width // dp_size, OWNERS * width // dp_size

    def columns(own, other, first, count):
        def flat_half(x):
            parts = [x[first + t * narrow : first + (t + 1) * narrow] for t in range(count)]
            return jnp.concatenate(parts, axis=1).astype(F32)

        return both_halves(flat_half(own), flat_half(other), core_first)

    def qkv_columns(own, other):
        parts = [columns(own, other, part * narrow, 1) for part in range(3)]
        return jnp.concatenate(parts, axis=1)

    def down_rows(own, other):
        at = OWNERS * narrow
        return both_halves(
            own[at : at + wide].astype(F32), other[at : at + wide].astype(F32), core_first
        )

    return (
        done_b.astype(BF16),
        grad_input,
        small[0],
        small[1],
        qkv_columns(*mix_a),
        columns(*mix_a, 3 * narrow, 1),
        small[2],
        columns(*feed_a, 0, OWNERS),
        down_rows(*feed_a),
        small[3],
        qkv_columns(*mix_b),
        columns(*mix_b, 3 * narrow, 1),
        small[4],
        columns(*feed_b, 0, OWNERS),
        down_rows(*feed_b),
    )


def solution(mesh):
    tokens, whole, shared = P("dp", "seq", None), P(), P("dp")
    weights = P("dp", None)
    return jax.shard_map(
        per_device,
        mesh=mesh,
        in_specs=(tokens, P("dp", "seq"), P("dp", None)) + (whole,) * 13 + (tokens,),
        out_specs=(tokens, tokens, shared)
        + (shared, weights, weights, shared, weights, weights) * 2,
        check_vma=False,
    )
```

time: 1350 us -> 602 us (0.45)
  waiting for transfers between devices: 826 us -> 222 us
  local copies, waits for them, and re-layouts: 154 us -> 21.5 us
  matrix products: 174 us -> 59.2 us
  Pallas kernels: 0 us -> 105 us
  other arithmetic: 96.9 us -> 38.2 us
  starting transfers between devices: 1.46 us -> 42.8 us
  blocking collectives: 63.8 us -> 101 us
    reduce_scatter x12 -> x0, waiting for transfers between devices: 774 us -> none  [the longest x1 98.7 us: per_device(): lax.psum_scatter(g_da.astype(jnp.bfloat16), 'dp', scatter_dimension=0, ti...]
    ppermute x0 -> x54, waiting for transfers between devices: none -> 222 us  [swap(): return lax.ppermute(x, axis, [(i, i ^ bit) for i in range(size)])]
    dot_general x53 -> x21, matrix products: 174 us -> 58.8 us  [the longest x9 27.2 us: project_back(): jnp.einsum('bne,de->bnd', gradient, weight, preferred_element_type=F32)]
    pallas_call x0 -> x11, Pallas kernels: none -> 105 us  [the longest x2 36.2 us: feed_grad(): pl.pallas_call(lambda *refs: feed_grad_kernel(bits, *refs), name='feed_gr...]
    psum x1, blocking collectives: 6.74 us -> 78.6 us  [per_device(): lax.psum(jnp.stack([grad_route, g_ga1, g_ga2, g_gb1, g_gb2]), ('dp', 'seq'))]
    all_gather x2 -> x0, waiting for transfers between devices: 50.4 us -> none  [the longest x1 26 us: fetch_full(): lax.all_gather(value_rows, 'seq', axis=1, tiled=True)]
    dynamic_update_slice x32 -> x0, local copies, waits for them, and re-layouts: 48.4 us -> none  [the longest x24 47.1 us: layer_backward(): lax.map(attend_backward, (queries, all_keys, all_values, visible, row_max...]
    ppermute x0 -> x54, starting transfers between devices: none -> 42.8 us  [swap(): return lax.ppermute(x, axis, [(i, i ^ bit) for i in range(size)])]
  transfers between devices with their start and end apart: 15 -> 54, of which waited for: 13 -> 22; matrix products, arithmetic and copies ran while one was open for 7% -> 11% of each run, Pallas kernels for 0% -> 11%
where the time goes in v1:
time: 602 us; the launch traced here: 592 us
  waiting for transfers between devices  222 us (37%)
  Pallas kernels  105 us (17%)
  blocking collectives  101 us (17%)
  matrix products  59.2 us (10%)
  starting transfers between devices  42.8 us (7%)
  other arithmetic  38.2 us (6%)
  local copies, waits for them, and re-layouts  21.5 us (4%)
    ppermute x54, waiting for transfers between devices, swap(): return lax.ppermute(x, axis, [(i, i ^ bit) for i in range(size)])  222 us
    psum x1, blocking collectives, per_device(): lax.psum(jnp.stack([grad_route, g_ga1, g_ga2, g_gb1, g_gb2]), ('dp', 'seq'))  78.6 us
    ppermute x54, starting transfers between devices, swap(): return lax.ppermute(x, axis, [(i, i ^ bit) for i in range(size)])  42.8 us
    pallas_call x2, Pallas kernels, feed_grad(): pl.pallas_call(lambda *refs: feed_grad_kernel(bits, *refs), name='feed_gr...  36.2 us
    dot_general x9, matrix products, project_back(): jnp.einsum('bne,de->bnd', gradient, weight, preferred_element_type=F32)  27.2 us
    pallas_call x2, Pallas kernels, attend_back(): pl.pallas_call(lambda *refs: attend_back_kernel(rows, routed, *refs), nam...  24.5 us
    all_gather x1, blocking collectives, per_device(): chosen_all = lax.all_gather(chosen, 'seq', axis=0)  21.9 us
    dot_general x6, matrix products, project(): jnp.einsum('bnd,de->bne', left_side, weight, preferred_element_type=F32)  21.2 us
  transfers between devices with their start and end apart: 54, of which 22 were waited for; matrix products, arithmetic and copies ran while one was open for 11% of the time, Pallas kernels for 11%

profile of v1, /device:TPU:0, one launch (start us, length us, event | category | flops | bytes accessed | tf_op | source)
XLA Modules:
  0.0 592.2 jit_solution(12076929008794885660)
XLA Ops:
  4.8 4.2 project_pieces.3
  9.4 2.5 collective-permute-start.1
  12.7 6.6 %project_pieces.4 = (bf16[2,256,768]{2,1,0:T(8,128)(2,1)}, bf16[3,256,384]{2,1,0:T(8,128)(2,1)}, bf16[3,256,384]{2,1,0:T(8,128)(2,1)}, bf16[3,256,384]{2,1,0:T(8,128)(2,1)}, bf16[3,256,384]{2,1,0:T(8,128)(2,1)}) custom-call(s32[3]{0:T(128)} %pad_add_fusion.place.refs_0_, bf16[2,256,768]{2,1,0:T(8,128)(2,1)} %x_ref.1, bf16[1,768]{1,0:T(2,128)(2,1)} %reshape.843.gain_ref, ...), custom_call_target="tpu_custom_call" | custom-call | flops 1811939328 | bytes 8257536 | tf_op jit(solution)/shard_map/project_pieces/pallas_call | solution.py:51
  23.1 4.0 attend_routed.1
  29.1 21.9 %all-gather.1 = s32[4,2,64]{2,1,0:T(2,128)S(1)} all-gather(s32[1,2,64]{2,1,0:T(2,128)S(1)} %bitcast.320), channel_id=2, replica_groups=mesh['dp'=8,'seq'=4] {'seq'}, dimensions={0}, use_global_device_ids=true | all-gather | bytes 2560 | tf_op jit(solution)/shard_map/all_gather | solution.py:519
  55.7 4.8 multiply_convert_fusion.2
  60.5 2.4 multiply_reduce_fusion.10
  62.9 4.2 project_pieces.5
  71.8 2.4 multiply_reduce_fusion.3
  78.8 13.0 %attend_dense.1 = (bf16[256,384]{1,0:T(8,128)(2,1)}, bf16[256,384]{1,0:T(8,128)(2,1)}, bf16[256,384]{1,0:T(8,128)(2,1)}, bf16[256,384]{1,0:T(8,128)(2,1)}, bf16[...) custom-call(s32[3]{0:T(128)} %pad_add_fusion.place.refs_0_, s32[4]{0:T(128)} %fusion.164.refs_1_, s32[4,64]{1,0:T(4,128)} %bitcast.324, ...), custom_call_target="tpu_custom_call" | custom-call | flops 4026531840 | bytes 6291456 | tf_op jit(solution)/shard_map/attend_dense/pallas_call | solution.py:174
  93.7 2.6 select_convert_fusion.refs_1_
  96.5 3.2 collective-permute-done.13
  99.7 3.4 collective-permute-done.14
  104.6 8.6 %multiply_convert_fusion = (bf16[2,256,3072]{2,1,0:T(8,128)(2,1)}, f32[2,256,3072]{2,1,0:T(8,128)S(1)}) fusion(bf16[2,256,768]{2,1,0:T(8,128)(2,1)S(1)} %multiply_convert_fusion.1, bf16[768,3072]{1,0:T(8,128)(2,1)} %param.31), kind=kOutput, calls=%fused_computation.11 | convolution fusion | flops 2430074880 | bytes 14942208 | tf_op jit(solution)/shard_map/bnd,de->bne/dot_general | solution.py:451
  113.2 6.4 %fusion.6 = bf16[2,256,3072]{2,1,0:T(8,128)(2,1)S(1)} fusion(f32[2,256,3072]{2,1,0:T(8,128)S(1)} %get-tuple-element.218, bf16[2,256,768]{2,1,0:T(8,128)(2,1)S(1)} %copy-done.30, bf16[3072,768]{1,0:T(8,128)(2,1)S(1)} %bitcast.329), kind=kOutput, calls=%fused_computation.10 | convolution fusion | flops 2447376384 | bytes 14942208 | tf_op jit(solution)/shard_map/bne,de->bnd/dot_general | solution.py:455
  119.7 3.4 multiply_reduce_fusion
  129.2 5.4 collective-permute-done.16.refs_7_
  134.5 3.1 collective-permute-done.17.refs_8_
  138.3 20.0 %attend_dense_back.1 = (bf16[3,256,384]{2,1,0:T(8,128)(2,1)}, bf16[3,256,384]{2,1,0:T(8,128)(2,1)}, bf16[3,256,384]{2,1,0:T(8,128)(2,1)}, bf16[3,256,384]{2,1,0:...) custom-call(s32[3]{0:T(128)} %pad_add_fusion.place.refs_0_, ...), custom_call_target="tpu_custom_call" | custom-call | flops 10066329600 | bytes 6291456 | tf_op jit(solution)/shard_map/attend_dense_back/pallas_call | solution.py:274
  161.8 3.4 collective-permute-done.22
  165.2 2.2 collective-permute-done.23
  171.5 5.0 fusion.42
  176.7 2.3 multiply_reduce_fusion.6
  183.8 3.5 add_convert_fusion.10
  188.3 4.5 attend_routed_back.1
  194.0 20.2 %feed_grad.3 = (bf16[8,768,384]{2,1,0:T(8,128)(2,1)}, bf16[8,768,384]{2,1,0:T(8,128)(2,1)}) custom-call(s32[3]{0:T(128)} %pad_add_fusion.place.refs_0_, bf16[512,768]{1,0:T(8,128)(2,1)} %bitcast.316, bf16[512,3072]{1,0:T(8,128)(2,1)} %bitcast.333, bf16[512,3072]{1,0:T(8,128)(2,1)} %bitcast.332, bf16[512,768]{1,0:T(8,128)(2,1)} %bitcast.315), custom_call_target="tpu_custom_call" | custom-call | flops 4831838208 | bytes 17301504 | tf_op jit(solution)/shard_map/feed_grad/pallas_call | solution.py:334
  218.2 16.0 %feed_grad.2 = (bf16[8,768,384]{2,1,0:T(8,128)(2,1)}, bf16[8,768,384]{2,1,0:T(8,128)(2,1)}) custom-call(s32[3]{0:T(128)} %pad_add_fusion.place.refs_0_, bf16[128,768]{1,0:T(8,128)(2,1)} %bitcast.318, bf16[128,3072]{1,0:T(8,128)(2,1)} %bitcast.317, bf16[128,3072]{1,0:T(8,128)(2,1)} %bitcast.314, bf16[128,768]{1,0:T(8,128)(2,1)} %bitcast.319), custom_call_target="tpu_custom_call" | custom-call | flops 1207959552 | bytes 11403264 | tf_op jit(solution)/shard_map/feed_grad/pallas_call | solution.py:334
  234.6 10.4 %collective-permute-done.29.refs_5_ = bf16[3,64,384]{2,1,0:T(8,128)(2,1)S(1)} collective-permute-done((bf16[3,64,384]{2,1,0:T(8,128)(2,1)}, bf16[3,64,384]{2,1,0:T(8,128)(2,1)S(1)}, u32[]{:S(2)}, u32[]{:S(2)}) %collective-permute-start.29) | collective-permute-done | bytes 147488 | tf_op jit(solution)/shard_map/ppermute | solution.py:398
  246.2 5.5 mix_grad.2
  254.0 7.3 %mix_grad.3 = (bf16[8,384,384]{2,1,0:T(8,128)(2,1)}, bf16[8,384,384]{2,1,0:T(8,128)(2,1)}) custom-call(s32[3]{0:T(128)} %pad_add_fusion.place.refs_0_, bf16[2,256,768]{2,1,0:T(8,128)(2,1)} %select_convert_fusion.refs_1_, bf16[3,256,384]{2,1,0:T(8,128)(2,1)} %get-tuple-element.84.refs_2_, bf16[3,256,384]{2,1,0:T(8,128)(2,1)} %copy-done.38, ...), custom_call_target="tpu_custom_call" | custom-call | flops 2415919104 | bytes 9437184 | tf_op jit(solution)/shard_map/mix_grad/pallas_call | solution.py:383
  262.0 4.1 multiply_reduce_fusion.7
  270.1 2.2 add_convert_fusion.5
  278.8 3.3 multiply_reduce_fusion.1
  282.2 78.6 %psum.7 = f32[5,768]{1,0:T(8,128)} all-reduce(f32[5,768]{1,0:T(8,128)S(1)} %stack.69), channel_id=1, replica_groups=mesh['dp'=8,'seq'=4] {'dp','seq'}, use_global_device_ids=true, to_apply=%region_15.16 | all-reduce | flops 3840 | bytes 30720 | tf_op jit(solution)/shard_map/psum | solution.py:602
  367.0 2.5 fusion.45
  369.5 9.9 %collective-permute-done.32 = bf16[2,384,384]{2,1,0:T(8,128)(2,1)S(1)} collective-permute-done((bf16[2,384,384]{2,1,0:T(8,128)(2,1)S(1)}, bf16[2,384,384]{2,1,0:T(8,128)(2,1)S(1)}, u32[]{:S(2)}, u32[]{:S(2)}) %collective-permute-start.32) | collective-permute-done | bytes 589856 | tf_op jit(solution)/shard_map/ppermute | solution.py:398
  380.1 16.5 %collective-permute-done.44 = bf16[2,384,384]{2,1,0:T(8,128)(2,1)S(1)} collective-permute-done((bf16[2,384,384]{2,1,0:T(8,128)(2,1)S(1)}, bf16[2,384,384]{2,1,0:T(8,128)(2,1)S(1)}, u32[]{:S(2)}, u32[]{:S(2)}) %collective-permute-start.44) | collective-permute-done | bytes 589856 | tf_op jit(solution)/shard_map/ppermute | solution.py:398
  397.0 3.7 add_convert_fusion
  402.9 2.9 collective-permute-start.34
  405.7 4.7 collective-permute-done.45
  411.4 3.5 add_convert_fusion.1
  417.3 2.2 collective-permute-done.46
  421.4 35.4 %collective-permute-done.49 = bf16[4,768,384]{2,1,0:T(8,128)(2,1)} collective-permute-done((bf16[4,768,384]{2,1,0:T(8,128)(2,1)}, bf16[4,768,384]{2,1,0:T(8,128)(2,1)}, u32[]{:S(2)}, u32[]{:S(2)}) %collective-permute-start.49) | collective-permute-done | bytes 2359328 | tf_op jit(solution)/shard_map/ppermute | solution.py:398
  456.8 2.2 add_convert_fusion.2
  461.3 43.3 %collective-permute-done.37 = bf16[4,768,384]{2,1,0:T(8,128)(2,1)S(1)} collective-permute-done((bf16[4,768,384]{2,1,0:T(8,128)(2,1)S(1)}, bf16[4,768,384]{2,1,0:T(8,128)(2,1)S(1)}, u32[]{:S(2)}, u32[]{:S(2)}) %collective-permute-start.37) | collective-permute-done | bytes 2359328 | tf_op jit(solution)/shard_map/ppermute | solution.py:398
  508.6 34.8 %collective-permute-done.38 = bf16[2,768,384]{2,1,0:T(8,128)(2,1)S(1)} collective-permute-done((bf16[2,768,384]{2,1,0:T(8,128)(2,1)S(1)}, bf16[2,768,384]{2,1,0:T(8,128)(2,1)S(1)}, u32[]{:S(2)}, u32[]{:S(2)}) %collective-permute-start.38) | collective-permute-done | bytes 1179680 | tf_op jit(solution)/shard_map/ppermute | solution.py:398
  546.1 24.4 %collective-permute-done.39 = bf16[1,768,384]{2,1,0:T(8,128)(2,1)S(1)} collective-permute-done((bf16[1,768,384]{2,1,0:T(8,128)(2,1)S(1)}, bf16[1,768,384]{2,1,0:T(8,128)(2,1)S(1)}, u32[]{:S(2)}, u32[]{:S(2)}) %collective-permute-start.39) | collective-permute-done | bytes 589856 | tf_op jit(solution)/shard_map/ppermute | solution.py:398
  572.8 13.1 %collective-permute-done.40 = bf16[1,768,384]{2,1,0:T(8,128)(2,1)S(1)} collective-permute-done((bf16[1,768,384]{2,1,0:T(8,128)(2,1)S(1)}, bf16[1,768,384]{2,1,0:T(8,128)(2,1)S(1)}, u32[]{:S(2)}, u32[]{:S(2)}) %collective-permute-start.40) | collective-permute-done | bytes 589856 | tf_op jit(solution)/shard_map/ppermute | solution.py:398
  (454 shorter events, 99.9 us)
Async XLA Ops:
  9.0 13.3 %collective-permute-start = (bf16[3,64,384]{2,1,0:T(8,128)(2,1)}, bf16[3,64,384]{2,1,0:T(8,128)(2,1)S(1)}, u32[]{:S(2)}, u32[]{:S(2)}) collective-permute-start(bf16[3,64,384]{2,1,0:T(8,128)(2,1)} %get-tuple-element.63), channel_id=1, source_target_pairs={{0,1},{1,0},{2,3},{3,2},{4,5},{5,4},{6,7},{7,6},{8,9},{9,8},{10,11... | collective-permute-start | bytes 442376 | tf_op jit(solution)/shard_map/ppermute | solution.py:398
  9.4 12.9 %collective-permute-start.1 = (bf16[3,64,384]{2,1,0:T(8,128)(2,1)}, bf16[3,64,384]{2,1,0:T(8,128)(2,1)S(1)}, u32[]{:S(2)}, u32[]{:S(2)}) collective-permute-start(bf16[3,64,384]{2,1,0:T(8,128)(2,1)} %get-tuple-element.64), channel_id=1, source_target_pairs={{0,2},{1,3},{2,0},{3,1},{4,6},{5,7},{6,4},{7,5},{8,10},{9,11},{10,... | collective-permute-start | bytes 442376 | tf_op jit(solution)/shard_map/ppermute | solution.py:398
  11.9 10.4 %collective-permute-start.2 = (bf16[3,64,384]{2,1,0:T(8,128)(2,1)}, bf16[3,64,384]{2,1,0:T(8,128)(2,1)S(1)}, u32[]{:S(2)}, u32[]{:S(2)}) collective-permute-start(bf16[3,64,384]{2,1,0:T(8,128)(2,1)} %get-tuple-element.65), channel_id=1, source_target_pairs={{0,3},{1,2},{2,1},{3,0},{4,7},{5,6},{6,5},{7,4},{8,11},{9,10},{10,... | collective-permute-start | bytes 442376 | tf_op jit(solution)/shard_map/ppermute | solution.py:398
  19.3 58.8 %collective-permute-start.6 = (bf16[3,256,384]{2,1,0:T(8,128)(2,1)}, bf16[3,256,384]{2,1,0:T(8,128)(2,1)}, u32[]{:S(2)}, u32[]{:S(2)}) collective-permute-start(bf16[3,256,384]{2,1,0:T(8,128)(2,1)} %get-tuple-element.71), channel_id=1, source_target_pairs={{0,1},{1,0},{2,3},{3,2},{4,5},{5,4},{6,7},{7,6},{8,9},{9,8},{10,11... | collective-permute-start | bytes 1769480 | tf_op jit(solution)/shard_map/ppermute | solution.py:398
  19.5 58.6 %collective-permute-start.7 = (bf16[3,256,384]{2,1,0:T(8,128)(2,1)}, bf16[3,256,384]{2,1,0:T(8,128)(2,1)}, u32[]{:S(2)}, u32[]{:S(2)}) collective-permute-start(bf16[3,256,384]{2,1,0:T(8,128)(2,1)} %get-tuple-element.72), channel_id=1, source_target_pairs={{0,2},{1,3},{2,0},{3,1},{4,6},{5,7},{6,4},{7,5},{8,10},{9,11},{10,... | collective-permute-start | bytes 1769480 | tf_op jit(solution)/shard_map/ppermute | solution.py:398
  22.3 55.8 %collective-permute-start.8 = (bf16[3,256,384]{2,1,0:T(8,128)(2,1)}, bf16[3,256,384]{2,1,0:T(8,128)(2,1)}, u32[]{:S(2)}, u32[]{:S(2)}) collective-permute-start(bf16[3,256,384]{2,1,0:T(8,128)(2,1)} %get-tuple-element.73), channel_id=1, source_target_pairs={{0,3},{1,2},{2,1},{3,0},{4,7},{5,6},{6,5},{7,4},{8,11},{9,10},{10,... | collective-permute-start | bytes 1769480 | tf_op jit(solution)/shard_map/ppermute | solution.py:398
  27.1 23.8 %collective-permute-start.4 = (bf16[64,384]{1,0:T(8,128)(2,1)}, bf16[64,384]{1,0:T(8,128)(2,1)S(1)}, u32[]{:S(2)}, u32[]{:S(2)}) collective-permute-start(bf16[64,384]{1,0:T(8,128)(2,1)} %get-tuple-element.68), channel_id=1, source_target_pairs={{0,2},{1,3},{2,0},{3,1},{4,6},{5,7},{6,4},{7,5},{8,10},{9,11},{10,... | collective-permute-start | bytes 147464 | tf_op jit(solution)/shard_map/ppermute | solution.py:398
  28.7 22.5 %collective-permute-start.5 = (bf16[64,384]{1,0:T(8,128)(2,1)}, bf16[64,384]{1,0:T(8,128)(2,1)S(1)}, u32[]{:S(2)}, u32[]{:S(2)}) collective-permute-start(bf16[64,384]{1,0:T(8,128)(2,1)} %get-tuple-element.69), channel_id=1, source_target_pairs={{0,3},{1,2},{2,1},{3,0},{4,7},{5,6},{6,5},{7,4},{8,11},{9,10},{10,... | collective-permute-start | bytes 147464 | tf_op jit(solution)/shard_map/ppermute | solution.py:398
  67.2 4.0 collective-permute-start.9
  69.4 7.0 %collective-permute-start.10 = (bf16[3,64,384]{2,1,0:T(8,128)(2,1)}, bf16[3,64,384]{2,1,0:T(8,128)(2,1)S(1)}, u32[]{:S(2)}, u32[]{:S(2)}) collective-permute-start(bf16[3,64,384]{2,1,0:T(8,128)(2,1)} %get-tuple-element.76), channel_id=1, source_target_pairs={{0,2},{1,3},{2,0},{3,1},{4,6},{5,7},{6,4},{7,5},{8,10},{9,11},{10,... | collective-permute-start | bytes 442376 | tf_op jit(solution)/shard_map/ppermute | solution.py:398
  71.2 6.9 %collective-permute-start.11 = (bf16[3,64,384]{2,1,0:T(8,128)(2,1)}, bf16[3,64,384]{2,1,0:T(8,128)(2,1)S(1)}, u32[]{:S(2)}, u32[]{:S(2)}) collective-permute-start(bf16[3,64,384]{2,1,0:T(8,128)(2,1)} %get-tuple-element.77), channel_id=1, source_target_pairs={{0,3},{1,2},{2,1},{3,0},{4,7},{5,6},{6,5},{7,4},{8,11},{9,10},{10,... | collective-permute-start | bytes 442376 | tf_op jit(solution)/shard_map/ppermute | solution.py:398
  91.8 8.0 %collective-permute-start.13 = (bf16[256,384]{1,0:T(8,128)(2,1)}, bf16[256,384]{1,0:T(8,128)(2,1)S(1)}, u32[]{:S(2)}, u32[]{:S(2)}) collective-permute-start(bf16[256,384]{1,0:T(8,128)(2,1)} %get-tuple-element.80), channel_id=1, source_target_pairs={{0,2},{1,3},{2,0},{3,1},{4,6},{5,7},{6,4},{7,5},{8,10},{9,11},{10,... | collective-permute-start | bytes 589832 | tf_op jit(solution)/shard_map/ppermute | solution.py:398
  93.5 9.7 %collective-permute-start.14 = (bf16[256,384]{1,0:T(8,128)(2,1)}, bf16[256,384]{1,0:T(8,128)(2,1)S(1)}, u32[]{:S(2)}, u32[]{:S(2)}) collective-permute-start(bf16[256,384]{1,0:T(8,128)(2,1)} %get-tuple-element.81), channel_id=1, source_target_pairs={{0,3},{1,2},{2,1},{3,0},{4,7},{5,6},{6,5},{7,4},{8,11},{9,10},{10,... | collective-permute-start | bytes 589832 | tf_op jit(solution)/shard_map/ppermute | solution.py:398
  96.3 6.9 %collective-permute-start.12 = (bf16[256,384]{1,0:T(8,128)(2,1)S(1)}, bf16[256,384]{1,0:T(8,128)(2,1)S(1)}, u32[]{:S(2)}, u32[]{:S(2)}) collective-permute-start(bf16[256,384]{1,0:T(8,128)(2,1)S(1)} %copy-done.89), channel_id=1, source_target_pairs={{0,1},{1,0},{2,3},{3,2},{4,5},{5,4},{6,7},{7,6},{8,9},{9,8},{10,11... | collective-permute-start | bytes 589832 | tf_op jit(solution)/shard_map/ppermute | solution.py:398
  126.8 7.7 %collective-permute-start.16 = (bf16[256,384]{1,0:T(8,128)(2,1)S(1)}, bf16[256,384]{1,0:T(8,128)(2,1)S(1)}, u32[]{:S(2)}, u32[]{:S(2)}) collective-permute-start(bf16[256,384]{1,0:T(8,128)(2,1)S(1)} %get-tuple-element.139), channel_id=1, source_target_pairs={{0,2},{1,3},{2,0},{3,1},{4,6},{5,7},{6,4},{7,5},{8,10},{9,11},{10,... | collective-permute-start | bytes 589832 | tf_op jit(solution)/shard_map/ppermute | solution.py:398
  128.6 9.0 %collective-permute-start.17 = (bf16[256,384]{1,0:T(8,128)(2,1)S(1)}, bf16[256,384]{1,0:T(8,128)(2,1)S(1)}, u32[]{:S(2)}, u32[]{:S(2)}) collective-permute-start(bf16[256,384]{1,0:T(8,128)(2,1)S(1)} %get-tuple-element.138), channel_id=1, source_target_pairs={{0,3},{1,2},{2,1},{3,0},{4,7},{5,6},{6,5},{7,4},{8,11},{9,10},{10,... | collective-permute-start | bytes 589832 | tf_op jit(solution)/shard_map/ppermute | solution.py:398
  158.3 6.9 %collective-permute-start.22 = (bf16[3,64,384]{2,1,0:T(8,128)(2,1)}, bf16[3,64,384]{2,1,0:T(8,128)(2,1)S(1)}, u32[]{:S(2)}, u32[]{:S(2)}) collective-permute-start(bf16[3,64,384]{2,1,0:T(8,128)(2,1)} %get-tuple-element.90), channel_id=1, source_target_pairs={{0,2},{1,3},{2,0},{3,1},{4,6},{5,7},{6,4},{7,5},{8,10},{9,11},{10,... | collective-permute-start | bytes 442376 | tf_op jit(solution)/shard_map/ppermute | solution.py:398
  160.1 7.3 %collective-permute-start.23 = (bf16[3,64,384]{2,1,0:T(8,128)(2,1)}, bf16[3,64,384]{2,1,0:T(8,128)(2,1)S(1)}, u32[]{:S(2)}, u32[]{:S(2)}) collective-permute-start(bf16[3,64,384]{2,1,0:T(8,128)(2,1)} %get-tuple-element.91), channel_id=1, source_target_pairs={{0,3},{1,2},{2,1},{3,0},{4,7},{5,6},{6,5},{7,4},{8,11},{9,10},{10,... | collective-permute-start | bytes 442376 | tf_op jit(solution)/shard_map/ppermute | solution.py:398
  161.5 6.0 %collective-permute-start.21 = (bf16[3,64,384]{2,1,0:T(8,128)(2,1)}, bf16[3,64,384]{2,1,0:T(8,128)(2,1)S(1)}, u32[]{:S(2)}, u32[]{:S(2)}) collective-permute-start(bf16[3,64,384]{2,1,0:T(8,128)(2,1)} %get-tuple-element.89), channel_id=1, source_target_pairs={{0,1},{1,0},{2,3},{3,2},{4,5},{5,4},{6,7},{7,6},{8,9},{9,8},{10,11... | collective-permute-start | bytes 442376 | tf_op jit(solution)/shard_map/ppermute | solution.py:398
  181.7 5.6 collective-permute-start.24
  182.0 5.3 collective-permute-start.25
  192.8 25.0 %collective-permute-start.28 = (bf16[3,64,384]{2,1,0:T(8,128)(2,1)}, bf16[3,64,384]{2,1,0:T(8,128)(2,1)S(1)}, u32[]{:S(2)}, u32[]{:S(2)}) collective-permute-start(bf16[3,64,384]{2,1,0:T(8,128)(2,1)} %get-tuple-element.96), channel_id=1, source_target_pairs={{0,2},{1,3},{2,0},{3,1},{4,6},{5,7},{6,4},{7,5},{8,10},{9,11},{10,... | collective-permute-start | bytes 442376 | tf_op jit(solution)/shard_map/ppermute | solution.py:398
  214.2 38.5 %collective-permute-start.19 = (bf16[3,256,384]{2,1,0:T(8,128)(2,1)}, bf16[3,256,384]{2,1,0:T(8,128)(2,1)S(1)}, u32[]{:S(2)}, u32[]{:S(2)}) collective-permute-start(bf16[3,256,384]{2,1,0:T(8,128)(2,1)} %get-tuple-element.86), channel_id=1, source_target_pairs={{0,2},{1,3},{2,0},{3,1},{4,6},{5,7},{6,4},{7,5},{8,10},{9,11},{10,... | collective-permute-start | bytes 1769480 | tf_op jit(solution)/shard_map/ppermute | solution.py:398
  215.0 38.2 %collective-permute-start.20 = (bf16[3,256,384]{2,1,0:T(8,128)(2,1)}, bf16[3,256,384]{2,1,0:T(8,128)(2,1)}, u32[]{:S(2)}, u32[]{:S(2)}) collective-permute-start(bf16[3,256,384]{2,1,0:T(8,128)(2,1)} %get-tuple-element.87), channel_id=1, source_target_pairs={{0,3},{1,2},{2,1},{3,0},{4,7},{5,6},{6,5},{7,4},{8,11},{9,10},{10,... | collective-permute-start | bytes 1769480 | tf_op jit(solution)/shard_map/ppermute | solution.py:398
  215.8 37.4 %collective-permute-start.18 = (bf16[3,256,384]{2,1,0:T(8,128)(2,1)}, bf16[3,256,384]{2,1,0:T(8,128)(2,1)S(1)}, u32[]{:S(2)}, u32[]{:S(2)}) collective-permute-start(bf16[3,256,384]{2,1,0:T(8,128)(2,1)} %get-tuple-element.85), channel_id=1, source_target_pairs={{0,1},{1,0},{2,3},{3,2},{4,5},{5,4},{6,7},{7,6},{8,9},{9,8},{10,11... | collective-permute-start | bytes 1769480 | tf_op jit(solution)/shard_map/ppermute | solution.py:398
  217.3 27.8 %collective-permute-start.29 = (bf16[3,64,384]{2,1,0:T(8,128)(2,1)}, bf16[3,64,384]{2,1,0:T(8,128)(2,1)S(1)}, u32[]{:S(2)}, u32[]{:S(2)}) collective-permute-start(bf16[3,64,384]{2,1,0:T(8,128)(2,1)} %get-tuple-element.97), channel_id=1, source_target_pairs={{0,3},{1,2},{2,1},{3,0},{4,7},{5,6},{6,5},{7,4},{8,11},{9,10},{10,... | collective-permute-start | bytes 442376 | tf_op jit(solution)/shard_map/ppermute | solution.py:398
  217.7 27.8 %collective-permute-start.27 = (bf16[3,64,384]{2,1,0:T(8,128)(2,1)}, bf16[3,64,384]{2,1,0:T(8,128)(2,1)S(1)}, u32[]{:S(2)}, u32[]{:S(2)}) collective-permute-start(bf16[3,64,384]{2,1,0:T(8,128)(2,1)} %get-tuple-element.95), channel_id=1, source_target_pairs={{0,1},{1,0},{2,3},{3,2},{4,5},{5,4},{6,7},{7,6},{8,9},{9,8},{10,11... | collective-permute-start | bytes 442376 | tf_op jit(solution)/shard_map/ppermute | solution.py:398
  245.1 151.8 %collective-permute-start.48 = (bf16[8,768,384]{2,1,0:T(8,128)(2,1)}, bf16[8,768,384]{2,1,0:T(8,128)(2,1)}, u32[]{:S(2)}, u32[]{:S(2)}) collective-permute-start(bf16[8,768,384]{2,1,0:T(8,128)(2,1)} %get-tuple-element.108), channel_id=1, source_target_pairs={{0,1},{1,0},{2,3},{3,2},{4,5},{5,4},{6,7},{7,6},{8,9},{9,8},{10,11... | collective-permute-start | bytes 14155784 | tf_op jit(solution)/shard_map/ppermute | solution.py:398
  251.7 17.0 %collective-permute-start.30 = (bf16[8,384,384]{2,1,0:T(8,128)(2,1)}, bf16[8,384,384]{2,1,0:T(8,128)(2,1)}, u32[]{:S(2)}, u32[]{:S(2)}) collective-permute-start(bf16[8,384,384]{2,1,0:T(8,128)(2,1)} %get-tuple-element.100), channel_id=1, source_target_pairs={{0,1},{1,0},{2,3},{3,2},{4,5},{5,4},{6,7},{7,6},{8,9},{9,8},{10,11... | collective-permute-start | bytes 7077896 | tf_op jit(solution)/shard_map/ppermute | solution.py:398
  252.7 158.7 %collective-permute-start.36 = (bf16[8,768,384]{2,1,0:T(8,128)(2,1)}, bf16[8,768,384]{2,1,0:T(8,128)(2,1)}, u32[]{:S(2)}, u32[]{:S(2)}) collective-permute-start(bf16[8,768,384]{2,1,0:T(8,128)(2,1)} %get-tuple-element.102), channel_id=1, source_target_pairs={{0,1},{1,0},{2,3},{3,2},{4,5},{5,4},{6,7},{7,6},{8,9},{9,8},{10,11... | collective-permute-start | bytes 14155784 | tf_op jit(solution)/shard_map/ppermute | solution.py:398
  261.3 12.8 %collective-permute-start.42 = (bf16[8,384,384]{2,1,0:T(8,128)(2,1)}, bf16[8,384,384]{2,1,0:T(8,128)(2,1)S(1)}, u32[]{:S(2)}, u32[]{:S(2)}) collective-permute-start(bf16[8,384,384]{2,1,0:T(8,128)(2,1)} %get-tuple-element.106), channel_id=1, source_target_pairs={{0,1},{1,0},{2,3},{3,2},{4,5},{5,4},{6,7},{7,6},{8,9},{9,8},{10,11... | collective-permute-start | bytes 7077896 | tf_op jit(solution)/shard_map/ppermute | solution.py:398
  272.5 88.3 %collective-permute-start.31 = (bf16[4,384,384]{2,1,0:T(8,128)(2,1)S(1)}, bf16[4,384,384]{2,1,0:T(8,128)(2,1)}, u32[]{:S(2)}, u32[]{:S(2)}) collective-permute-start(bf16[4,384,384]{2,1,0:T(8,128)(2,1)S(1)} %slice.393), channel_id=1, source_target_pairs={{0,4},{4,0},{8,12},{12,8},{16,20},{20,16},{24,28},{28,24},{1,5},{5... | collective-permute-start | bytes 3538952 | tf_op jit(solution)/shard_map/ppermute | solution.py:398
  277.4 86.1 %collective-permute-start.43 = (bf16[4,384,384]{2,1,0:T(8,128)(2,1)}, bf16[4,384,384]{2,1,0:T(8,128)(2,1)}, u32[]{:S(2)}, u32[]{:S(2)}) collective-permute-start(bf16[4,384,384]{2,1,0:T(8,128)(2,1)} %slice.423), channel_id=1, source_target_pairs={{0,4},{4,0},{8,12},{12,8},{16,20},{20,16},{24,28},{28,24},{1,5},{5... | collective-permute-start | bytes 3538952 | tf_op jit(solution)/shard_map/ppermute | solution.py:398
  363.1 16.3 %collective-permute-start.32 = (bf16[2,384,384]{2,1,0:T(8,128)(2,1)S(1)}, bf16[2,384,384]{2,1,0:T(8,128)(2,1)S(1)}, u32[]{:S(2)}, u32[]{:S(2)}) collective-permute-start(bf16[2,384,384]{2,1,0:T(8,128)(2,1)S(1)} %slice.395), channel_id=1, source_target_pairs={{0,8},{4,12},{8,0},{12,4},{16,24},{20,28},{24,16},{28,20},{1,9},{5... | collective-permute-start | bytes 1769480 | tf_op jit(solution)/shard_map/ppermute | solution.py:398
  365.4 31.2 %collective-permute-start.44 = (bf16[2,384,384]{2,1,0:T(8,128)(2,1)S(1)}, bf16[2,384,384]{2,1,0:T(8,128)(2,1)S(1)}, u32[]{:S(2)}, u32[]{:S(2)}) collective-permute-start(bf16[2,384,384]{2,1,0:T(8,128)(2,1)S(1)} %slice.425), channel_id=1, source_target_pairs={{0,8},{4,12},{8,0},{12,4},{16,24},{20,28},{24,16},{28,20},{1,9},{5... | collective-permute-start | bytes 1769480 | tf_op jit(solution)/shard_map/ppermute | solution.py:398
  379.6 23.2 %collective-permute-start.33 = (bf16[1,384,384]{2,1,0:T(8,128)(2,1)S(1)}, bf16[1,384,384]{2,1,0:T(8,128)(2,1)S(1)}, u32[]{:S(2)}, u32[]{:S(2)}) collective-permute-start(bf16[1,384,384]{2,1,0:T(8,128)(2,1)S(1)} %slice.397), channel_id=1, source_target_pairs={{0,16},{4,20},{8,24},{12,28},{16,0},{20,4},{24,8},{28,12},{1,17},{... | collective-permute-start | bytes 884744 | tf_op jit(solution)/shard_map/ppermute | solution.py:398
  396.8 13.6 %collective-permute-start.45 = (bf16[1,384,384]{2,1,0:T(8,128)(2,1)S(1)}, bf16[1,384,384]{2,1,0:T(8,128)(2,1)S(1)}, u32[]{:S(2)}, u32[]{:S(2)}) collective-permute-start(bf16[1,384,384]{2,1,0:T(8,128)(2,1)S(1)} %slice.427), channel_id=1, source_target_pairs={{0,16},{4,20},{8,24},{12,28},{16,0},{20,4},{24,8},{28,12},{1,17},{... | collective-permute-start | bytes 884744 | tf_op jit(solution)/shard_map/ppermute | solution.py:398
  402.3 54.5 %collective-permute-start.49 = (bf16[4,768,384]{2,1,0:T(8,128)(2,1)}, bf16[4,768,384]{2,1,0:T(8,128)(2,1)}, u32[]{:S(2)}, u32[]{:S(2)}) collective-permute-start(bf16[4,768,384]{2,1,0:T(8,128)(2,1)} %slice.437), channel_id=1, source_target_pairs={{0,4},{4,0},{8,12},{12,8},{16,20},{20,16},{24,28},{28,24},{1,5},{5... | collective-permute-start | bytes 7077896 | tf_op jit(solution)/shard_map/ppermute | solution.py:398
  402.9 14.3 %collective-permute-start.34 = (bf16[1,384,384]{2,1,0:T(8,128)(2,1)S(1)}, bf16[1,384,384]{2,1,0:T(8,128)(2,1)S(1)}, u32[]{:S(2)}, u32[]{:S(2)}) collective-permute-start(bf16[1,384,384]{2,1,0:T(8,128)(2,1)S(1)} %add_convert_fusion.20), channel_id=1, source_target_pairs={{0,2},{1,3},{2,0},{3,1},{4,6},{5,7},{6,4},{7,5},{8,10},{9,11},{10,... | collective-permute-start | bytes 884744 | tf_op jit(solution)/shard_map/ppermute | solution.py:398
  410.5 9.0 %collective-permute-start.46 = (bf16[1,384,384]{2,1,0:T(8,128)(2,1)S(1)}, bf16[1,384,384]{2,1,0:T(8,128)(2,1)S(1)}, u32[]{:S(2)}, u32[]{:S(2)}) collective-permute-start(bf16[1,384,384]{2,1,0:T(8,128)(2,1)S(1)} %add_convert_fusion.18), channel_id=1, source_target_pairs={{0,2},{1,3},{2,0},{3,1},{4,6},{5,7},{6,4},{7,5},{8,10},{9,11},{10,... | collective-permute-start | bytes 884744 | tf_op jit(solution)/shard_map/ppermute | solution.py:398
  415.2 89.5 %collective-permute-start.37 = (bf16[4,768,384]{2,1,0:T(8,128)(2,1)S(1)}, bf16[4,768,384]{2,1,0:T(8,128)(2,1)S(1)}, u32[]{:S(2)}, u32[]{:S(2)}) collective-permute-start(bf16[4,768,384]{2,1,0:T(8,128)(2,1)S(1)} %slice.407), channel_id=1, source_target_pairs={{0,4},{4,0},{8,12},{12,8},{16,20},{20,16},{24,28},{28,24},{1,5},{5... | collective-permute-start | bytes 7077896 | tf_op jit(solution)/shard_map/ppermute | solution.py:398
  459.2 48.1 %collective-permute-start.50 = (bf16[2,768,384]{2,1,0:T(8,128)(2,1)S(1)}, bf16[2,768,384]{2,1,0:T(8,128)(2,1)S(1)}, u32[]{:S(2)}, u32[]{:S(2)}) collective-permute-start(bf16[2,768,384]{2,1,0:T(8,128)(2,1)S(1)} %slice.439), channel_id=1, source_target_pairs={{0,8},{4,12},{8,0},{12,4},{16,24},{20,28},{24,16},{28,20},{1,9},{5... | collective-permute-start | bytes 3538952 | tf_op jit(solution)/shard_map/ppermute | solution.py:398
  505.3 38.1 %collective-permute-start.38 = (bf16[2,768,384]{2,1,0:T(8,128)(2,1)S(1)}, bf16[2,768,384]{2,1,0:T(8,128)(2,1)S(1)}, u32[]{:S(2)}, u32[]{:S(2)}) collective-permute-start(bf16[2,768,384]{2,1,0:T(8,128)(2,1)S(1)} %slice.409), channel_id=1, source_target_pairs={{0,8},{4,12},{8,0},{12,4},{16,24},{20,28},{24,16},{28,20},{1,9},{5... | collective-permute-start | bytes 3538952 | tf_op jit(solution)/shard_map/ppermute | solution.py:398
  507.7 37.0 %collective-permute-start.51 = (bf16[1,768,384]{2,1,0:T(8,128)(2,1)S(1)}, bf16[1,768,384]{2,1,0:T(8,128)(2,1)S(1)}, u32[]{:S(2)}, u32[]{:S(2)}) collective-permute-start(bf16[1,768,384]{2,1,0:T(8,128)(2,1)S(1)} %slice.441), channel_id=1, source_target_pairs={{0,16},{4,20},{8,24},{12,28},{16,0},{20,4},{24,8},{28,12},{1,17},{... | collective-permute-start | bytes 1769480 | tf_op jit(solution)/shard_map/ppermute | solution.py:398
  543.8 26.7 %collective-permute-start.39 = (bf16[1,768,384]{2,1,0:T(8,128)(2,1)S(1)}, bf16[1,768,384]{2,1,0:T(8,128)(2,1)S(1)}, u32[]{:S(2)}, u32[]{:S(2)}) collective-permute-start(bf16[1,768,384]{2,1,0:T(8,128)(2,1)S(1)} %slice.411), channel_id=1, source_target_pairs={{0,16},{4,20},{8,24},{12,28},{16,0},{20,4},{24,8},{28,12},{1,17},{... | collective-permute-start | bytes 1769480 | tf_op jit(solution)/shard_map/ppermute | solution.py:398
  544.8 27.7 %collective-permute-start.52 = (bf16[1,768,384]{2,1,0:T(8,128)(2,1)S(1)}, bf16[1,768,384]{2,1,0:T(8,128)(2,1)S(1)}, u32[]{:S(2)}, u32[]{:S(2)}) collective-permute-start(bf16[1,768,384]{2,1,0:T(8,128)(2,1)S(1)} %add_convert_fusion.12), channel_id=1, source_target_pairs={{0,2},{1,3},{2,0},{3,1},{4,6},{5,7},{6,4},{7,5},{8,10},{9,11},{10,... | collective-permute-start | bytes 1769480 | tf_op jit(solution)/shard_map/ppermute | solution.py:398
  570.6 15.3 %collective-permute-start.40 = (bf16[1,768,384]{2,1,0:T(8,128)(2,1)S(1)}, bf16[1,768,384]{2,1,0:T(8,128)(2,1)S(1)}, u32[]{:S(2)}, u32[]{:S(2)}) collective-permute-start(bf16[1,768,384]{2,1,0:T(8,128)(2,1)S(1)} %add_convert_fusion.15), channel_id=1, source_target_pairs={{0,2},{1,3},{2,0},{3,1},{4,6},{5,7},{6,4},{7,5},{8,10},{9,11},{10,... | collective-permute-start | bytes 1769480 | tf_op jit(solution)/shard_map/ppermute | solution.py:398
  572.7 13.5 %collective-permute-start.53 = (bf16[1,768,384]{2,1,0:T(8,128)(2,1)S(1)}, bf16[1,768,384]{2,1,0:T(8,128)(2,1)S(1)}, u32[]{:S(2)}, u32[]{:S(2)}) collective-permute-start(bf16[1,768,384]{2,1,0:T(8,128)(2,1)S(1)} %add_convert_fusion.11), channel_id=1, source_target_pairs={{0,1},{1,0},{2,3},{3,2},{4,5},{5,4},{6,7},{7,6},{8,9},{9,8},{10,11... | collective-permute-start | bytes 1769480 | tf_op jit(solution)/shard_map/ppermute | solution.py:398
  (125 other events, 1237.3 us)

commit v2 on v1

--- a/solution.py
+++ b/solution.py
@@ -30,35 +30,43 @@
     return pl.CostEstimate(flops=int(flops), bytes_accessed=int(moved), transcendentals=int(exps))
 
 
-def project_kernel(place, x_ref, gain_ref, w_ref, act_ref, *outs):
-    width = x_ref.shape[-1]
+def project_kernel(tagged, place, x_ref, gain_ref, w_ref, *refs):
+    tag_ref, refs = (refs[0], refs[1:]) if tagged else (None, refs)
+    act_ref, outs = refs[0], refs[1:]
+    rows, width = x_ref.shape[1:]
     half = width // 2
+    gain = gain_ref[...].astype(F32).reshape(1, width)
     for i in range(2):
         x = x_ref[i].astype(F32)
         scale = lax.rsqrt(jnp.mean(x * x, axis=-1, keepdims=True) + EPSILON)
-        act_ref[i] = (x * scale * gain_ref[...].astype(F32)).astype(BF16)
+        act_ref[i] = (x * scale * gain).astype(BF16)
     for r in (3, 2, 1, 0):
         act = act_ref[place[0] ^ (r >> 1)]
         at = (place[1] ^ (r & 1)) * half
         for part in range(3):
             columns = pl.ds(pl.multiple_of(part * width + at, LANES), half)
-            outs[r][part] = dot(act, w_ref[:, columns]).astype(BF16)
-
-
-def project_pieces(place, x, gain, weight):
+            outs[r][part, :rows, :] = dot(act, w_ref[:, columns]).astype(BF16)
+            if tagged:
+                outs[r][part, rows:, :] = tag_ref[place[0] ^ (r >> 1)]
+
+
+def project_pieces(place, x, gain, weight, tag=None):
     seqs, rows, width = x.shape
-    piece = jax.ShapeDtypeStruct((3, rows, width // 2), BF16)
+    tagged = tag is not None
+    extra = [tag] if tagged else []
+    spare = tag.shape[1] if tagged else 0
+    piece = jax.ShapeDtypeStruct((3, rows + spare, width // 2), BF16)
     outs = pl.pallas_call(
-        project_kernel,
+        lambda *refs: project_kernel(tagged, *refs),
         name="project_pieces",
         out_shape=[jax.ShapeDtypeStruct(x.shape, BF16)] + [piece] * OWNERS,
-        in_specs=[SMEM_SPEC] + [VMEM_SPEC] * 3,
+        in_specs=[SMEM_SPEC] + [VMEM_SPEC] * (3 + len(extra)),
         out_specs=[VMEM_SPEC] * (1 + OWNERS),
         compiler_params=pltpu.CompilerParams(vmem_limit_bytes=VMEM_BYTES),
         cost_estimate=cost(
             2 * seqs * rows * width * 3 * width, 6 * width * width + 12 * seqs * rows * width
         ),
-    )(place, x, gain.reshape(1, width), weight)
+    )(place, x, gain, weight, *extra)
     return outs[0], outs[1:]
 
 
@@ -71,9 +79,9 @@
     return jnp.where(lane_head(head), x, jnp.zeros_like(x))
 
 
-def slot_matrix(chosen_ref, counts, owner, rows):
+def slot_matrix(chosen_ref, counts, r, owner, rows):
     slots = chosen_ref.shape[1]
-    spots = chosen_ref[pl.ds(owner, 1), :]
+    spots = chosen_ref[r : r + 1, :]
     row_ids = lax.broadcasted_iota(jnp.int32, (rows, slots), 0)
     slot_ids = lax.broadcasted_iota(jnp.int32, (rows, slots), 1)
     return jnp.where((row_ids == spots) & (slot_ids < counts[owner]), 1.0, 0.0)
@@ -111,7 +119,7 @@
             for part in range(3):
                 merged[part, at, :] = base[r][part]
         else:
-            spots = slot_matrix(chosen_ref, counts, owner, rows)
+            spots = slot_matrix(chosen_ref, counts, r, owner, rows)
             covered = jnp.max(spots, axis=1, keepdims=True) > 0.5
             spots = spots.astype(BF16)
             for part in range(3):
@@ -153,9 +161,9 @@
         outs[r][...] = mixed[at, :]
 
 
-def attend(place, counts, base, chosen=None, slots=None):
+def attend(place, counts, rows, base, chosen=None, slots=None):
     routed = slots is None
-    _, rows, half = base[0].shape
+    half = base[0].shape[2]
     pairs = half // LANES
     length = OWNERS * rows
     inputs = [place, counts]
@@ -163,12 +171,10 @@
     if not routed:
         inputs.append(chosen)
         specs.append(VMEM_SPEC)
-    for group in (base, slots):
+    for group, count in ((base, rows), (slots, None if routed else chosen.shape[1])):
         if group is not None:
             inputs += list(group)
-            specs += [
-                pl.BlockSpec((3, group[0].shape[1], LANES), lambda h: (0, 0, h))
-            ] * OWNERS
+            specs += [pl.BlockSpec((3, count, LANES), lambda h: (0, 0, h))] * OWNERS
     blocks = length // BLOCK
     work = blocks * (blocks + 1) // 2 * BLOCK * BLOCK * 2 * pairs
     outs = pl.pallas_call(
@@ -241,7 +247,7 @@
         owner = me ^ r
         at = pl.ds(pl.multiple_of(owner * rows, rows), rows)
         if not routed:
-            spots = slot_matrix(chosen_ref, counts, owner, rows).astype(BF16)
+            spots = slot_matrix(chosen_ref, counts, r, owner, rows).astype(BF16)
         for part, ref in enumerate((grad_q, grad_k, grad_v)):
             found = ref[at, :].astype(BF16)
             outs[r][part] = found
@@ -286,111 +292,156 @@
     return outs[:OWNERS], outs[OWNERS:]
 
 
-def bit_reverse(number, bits):
-    found = 0
-    for k in range(bits):
-        found = found | (((number >> k) & 1) << (bits - 1 - k))
-    return found
-
-
-def store_slabs(ref, found, first, slab_rows, at, place, bits):
-    for d in range(found.shape[0] // slab_rows):
-        spot = bit_reverse(first + d, bits) ^ place[2]
-        ref[pl.ds(spot, 1), at : at + slab_rows, :] = found[
-            d * slab_rows : (d + 1) * slab_rows
-        ].astype(BF16)[None]
-
-
-def feed_grad_kernel(bits, place, ff_ref, gh_ref, gel_ref, gff_ref, send_ref, own_ref):
-    step, kind, tile = pl.program_id(0), pl.program_id(1), pl.program_id(2)
-    width = ff_ref.shape[1]
-    slabs = 1 << bits
-    narrow, wide = width // slabs, OWNERS * width // slabs
-    for core_step, ref in ((0, send_ref), (1, own_ref)):
-        for t in range(OWNERS):
-
-            @pl.when((step == core_step) & (kind == 0) & (tile == t))
-            def _():
-                found = dot(ff_ref[...], gh_ref[...], TN)
-                store_slabs(ref, found, 0, narrow, t * narrow, place, bits)
-
-            @pl.when((step == core_step) & (kind == 1) & (tile == t))
-            def _():
-                found = dot(gel_ref[...], gff_ref[...], TN)
-                store_slabs(
-                    ref, found, t * slabs // OWNERS, wide, OWNERS * narrow, place, bits
-                )
-
-
-def feed_grad(place, bits, ff_in, grad_hidden, activated, grad_ff):
-    tokens, width = ff_in.shape
+SPARE = 32
+Y_STAGE = -1
+
+
+def send_orders(bits):
+    dp = list(range(bits))
+    rest = dp[2:]
+    return (
+        [dp[0], Y_STAGE, dp[1]] + rest,
+        [dp[1], dp[0], Y_STAGE] + rest,
+        [Y_STAGE, dp[0], dp[1]] + rest,
+    )
+
+
+def position(order, slab, y_half):
+    spot = 0
+    for k in order:
+        spot = 2 * spot + (y_half if k == Y_STAGE else ((slab >> k) & 1))
+    return spot
+
+
+def store_slabs(target, bits, place, first, found, rows):
+    ref, at, which = target
+    order = send_orders(bits)[which]
+    part = rows // 2
+    for d in range(found.shape[0] // rows):
+        for y_half in range(2):
+            spot = position(order, first + d, y_half) ^ place[2 + which]
+            low = d * rows + y_half * part
+            ref[pl.ds(spot, 1), at // 2 : at // 2 + part, :] = found[low : low + part].astype(
+                BF16
+            )[None]
+
+
+def feed_grad_kernel(bits, orders, routed, place, *refs):
+    ff_refs, gel_refs, mix_refs, gh_refs, gff_refs, gatt_refs = (
+        refs[2 * k : 2 * k + 2] for k in range(6)
+    )
+    refs = refs[12:]
+    width = ff_refs[0].shape[1]
     half = width // 2
     slabs = 1 << bits
-    rows = 2 * OWNERS * width // slabs
-
-    def half_of(step, place_ref):
-        return place_ref[1] ^ (1 - step)
-
+    narrow = width // slabs
+    wide = OWNERS * narrow
+    first, second = refs[-2:]
+    if routed:
+        for d in range(slabs):
+            store_slabs((first, wide, orders[0]), bits, place, d, refs[0][d], SPARE)
+    own = pl.ds(pl.multiple_of(place[1] * half, LANES), half)
+    turned = [ref[...].T for ref in ff_refs]
+    for t in range(OWNERS):
+        tile = pl.ds(pl.multiple_of((place[1] * OWNERS + t) * half, LANES), half)
+        found = dot(turned[0], gh_refs[0][:, tile])
+        found = found + dot(turned[1], gh_refs[1][:, t * half : (t + 1) * half])
+        store_slabs((first, t * narrow, orders[0]), bits, place, 0, found, narrow)
+    for t in range(OWNERS):
+        rows = slice(t * width, (t + 1) * width)
+        found = dot(gel_refs[0][:, rows], gff_refs[0][:, own], TN)
+        found = found + dot(gel_refs[1][:, rows], gff_refs[1][...], TN)
+        store_slabs((second, 0, orders[1]), bits, place, t * slabs // OWNERS, found, wide)
+    found = dot(mix_refs[0][...], gatt_refs[0][:, own], TN)
+    found = found + dot(mix_refs[1][...], gatt_refs[1][...], TN)
+    store_slabs((second, wide, orders[1]), bits, place, 0, found, narrow)
+
+
+def feed_grad(place, bits, orders, operands, route=None):
+    tokens, width = operands[0].shape
+    half = width // 2
+    slabs = 1 << bits
+    narrow = width // slabs
+    wide = OWNERS * narrow
+    routed = route is not None
+    rows = (wide + (SPARE if routed else 0), wide + narrow)
+    extra = [route] if routed else []
     return pl.pallas_call(
-        lambda *refs: feed_grad_kernel(bits, *refs),
+        lambda *refs: feed_grad_kernel(bits, orders, routed, *refs),
         name="feed_grad",
-        grid_spec=pltpu.PrefetchScalarGridSpec(
-            num_scalar_prefetch=1,
-            grid=(2, 2, OWNERS),
-            in_specs=[
-                pl.BlockSpec((tokens, width), lambda s, k, t, p: (0, 0)),
-                pl.BlockSpec(
-                    (tokens, half),
-                    lambda s, k, t, p: (
-                        0,
-                        half_of(s, p) * OWNERS + jnp.where(k == 0, t, OWNERS - 1),
-                    ),
-                ),
-                pl.BlockSpec((tokens, width), lambda s, k, t, p: (0, jnp.where(k == 0, 0, t))),
-                pl.BlockSpec((tokens, half), lambda s, k, t, p: (0, half_of(s, p))),
-            ],
-            out_specs=[pl.BlockSpec((slabs, rows, half), lambda s, k, t, p: (0, 0, 0))] * 2,
-        ),
-        out_shape=[jax.ShapeDtypeStruct((slabs, rows, half), BF16)] * 2,
+        in_specs=[SMEM_SPEC] + [VMEM_SPEC] * (12 + len(extra)),
+        out_specs=[VMEM_SPEC] * len(rows),
+        out_shape=[jax.ShapeDtypeStruct((2 * slabs, count // 2, half), BF16) for count in rows],
         compiler_params=pltpu.CompilerParams(vmem_limit_bytes=VMEM_BYTES),
         cost_estimate=cost(
-            16 * tokens * width * width, 16 * width * width + 20 * tokens * width
+            18 * tokens * width * width, 9 * width * width + 40 * tokens * width
         ),
-    )(place, ff_in, grad_hidden, activated, grad_ff)
-
-
-def mix_grad_kernel(bits, place, act_ref, p0, p1, p2, p3, mix_ref, gatt_ref, send_ref, own_ref):
-    width = act_ref.shape[-1]
-    half = width // 2
-    narrow = width // (1 << bits)
-    pieces = (p0, p1, p2, p3)
-    for other, ref in ((1, send_ref), (0, own_ref)):
-        for part in range(3):
-            found = dot(act_ref[place[0]], pieces[other][part], TN)
-            found = found + dot(act_ref[1 - place[0]], pieces[2 + other][part], TN)
-            store_slabs(ref, found, 0, narrow, part * narrow, place, bits)
-        columns = pl.ds(pl.multiple_of((place[1] ^ other) * half, LANES), half)
-        found = dot(mix_ref[0], gatt_ref[0, :, columns], TN)
-        found = found + dot(mix_ref[1], gatt_ref[1, :, columns], TN)
-        store_slabs(ref, found, 0, narrow, 3 * narrow, place, bits)
-
-
-def mix_grad(place, bits, act, pieces, mixture, grad_attended):
-    seqs, rows, width = act.shape
+    )(place, *operands, *extra)
+
+
+def qkv_grad_kernel(bits, order, place, *refs):
+    acts, pieces, out = refs[:OWNERS], refs[OWNERS : 2 * OWNERS], refs[2 * OWNERS]
+    narrow = acts[0].shape[1] // (1 << bits)
+    for part in range(3):
+        found = dot(acts[0][...], pieces[0][part], TN)
+        for r in range(1, OWNERS):
+            found = found + dot(acts[r][...], pieces[r][part], TN)
+        store_slabs((out, part * narrow, order), bits, place, 0, found, narrow)
+
+
+def qkv_grad(place, bits, order, acts, pieces):
+    rows, width = acts[0].shape
     half = width // 2
     slabs = 1 << bits
-    shape = jax.ShapeDtypeStruct((slabs, OWNERS * width // slabs, half), BF16)
+    narrow = width // slabs
     return pl.pallas_call(
-        lambda *refs: mix_grad_kernel(bits, *refs),
-        name="mix_grad",
-        in_specs=[SMEM_SPEC] + [VMEM_SPEC] * 7,
-        out_specs=[VMEM_SPEC] * 2,
-        out_shape=[shape] * 2,
+        lambda *refs: qkv_grad_kernel(bits, order, *refs),
+        name="qkv_grad",
+        in_specs=[SMEM_SPEC] + [VMEM_SPEC] * (2 * OWNERS),
+        out_specs=VMEM_SPEC,
+        out_shape=jax.ShapeDtypeStruct((2 * slabs, 3 * narrow // 2, half), BF16),
         compiler_params=pltpu.CompilerParams(vmem_limit_bytes=VMEM_BYTES),
         cost_estimate=cost(
-            8 * seqs * rows * width * width, 8 * width * width + 12 * seqs * rows * width
+            12 * rows * width * width, 3 * width * width + 20 * rows * width
         ),
-    )(place, act, *pieces, mixture, grad_attended)
+    )(place, *acts, *pieces)
+
+
+def finish_kernel(down_at, place, near_ref, far_ref, qkv_ref, out_ref, up_ref, down_ref):
+    narrow, width = out_ref.shape
+    half = width // 2
+    wide = OWNERS * narrow
+
+    for flip, ref in ((0, near_ref), (1, far_ref)):
+        side = place[1] ^ flip
+
+        def put(out, tile, at, rows):
+            columns = pl.ds(pl.multiple_of(tile * half, LANES), half)
+            for y_half in range(2):
+                part = rows // 2
+                out[y_half * part : (y_half + 1) * part, columns] = ref[
+                    y_half, at // 2 : at // 2 + part, :
+                ].astype(F32)
+
+        for t in range(OWNERS):
+            put(up_ref, side * OWNERS + t, t * narrow, narrow)
+        put(down_ref, side, down_at, wide)
+        put(out_ref, side, down_at + wide, narrow)
+        for p in range(3):
+            put(qkv_ref, 2 * p + side, down_at + wide + (1 + p) * narrow, narrow)
+
+
+def finish(place, down_at, narrow, width, near, far):
+    shapes = [(narrow, 3 * width), (narrow, width), (narrow, 4 * width), (4 * narrow, width)]
+    return pl.pallas_call(
+        lambda *refs: finish_kernel(down_at, *refs),
+        name="finish_grads",
+        in_specs=[SMEM_SPEC] + [VMEM_SPEC] * 2,
+        out_specs=[VMEM_SPEC] * 4,
+        out_shape=[jax.ShapeDtypeStruct(shape, F32) for shape in shapes],
+        compiler_params=pltpu.CompilerParams(vmem_limit_bytes=VMEM_BYTES),
+        cost_estimate=cost(0, 72 * narrow * width),
+    )(place, near, far)
 
 
 def swap(x, axis, bit):
@@ -406,13 +457,42 @@
     return (a.astype(F32) + b.astype(F32)).astype(BF16)
 
 
-def reduce_group(send, own, bits):
-    current = add_low(own, swap(send, "seq", 1))
-    for k in range(bits):
-        n = current.shape[0] // 2
-        current = add_low(current[:n], swap(current[n:], "dp", 1 << k))
-    current = add_low(current, swap(current, "seq", 2))
-    return current[0], swap(current, "seq", 1)[0]
+def halves(unit):
+    n = unit.shape[0] // 2
+    return unit[:n], unit[n:]
+
+
+def combine(keep, received):
+    if keep.shape[0] == 1:
+        return add_low(keep, received)[0]
+    (low, high), (low_in, high_in) = halves(keep), halves(received)
+    return add_low(low, low_in), add_low(high, high_in)
+
+
+def stage_swap(state, order, stage):
+    k = order[stage]
+    return swap(state[1], "seq", 2) if k == Y_STAGE else swap(state[1], "dp", 1 << k)
+
+
+class Chain:
+    def __init__(self, unit, order):
+        self.state, self.order, self.stage = halves(unit), order, 0
+
+    def step(self, after):
+        keep, _ = hold(self.state[0], after)
+        self.state = combine(keep, stage_swap(self.state, self.order, self.stage))
+        self.stage += 1
+        return self.state
+
+
+def gather_halves(own, y_first):
+    other = swap(own, "seq", 2)
+    pair = jnp.stack([jnp.where(y_first, own, other), jnp.where(y_first, other, own)])
+    return pair, swap(pair, "seq", 1)
+
+
+def hold(*values):
+    return lax.optimization_barrier(values)
 
 
 def both_halves(own, other, first):
@@ -430,6 +510,19 @@
 def assemble_packed(pieces, y_first, core_first):
     found = assemble(pieces, y_first, core_first)
     return jnp.concatenate([found[:, 0], found[:, 1], found[:, 2]], axis=-1)
+
+
+def core_half(x, at):
+    half = x.shape[-1] // 2
+    return lax.dynamic_slice_in_dim(x, at * half, half, axis=x.ndim - 1)
+
+
+def with_far(x):
+    return x, swap(x, "seq", 1)
+
+
+def half_with_far(x, core_at):
+    return x, swap(core_half(x, 1 - core_at), "seq", 1)
 
 
 def split_pieces(x, place):
@@ -472,18 +565,16 @@
     unused_value, gelu_pull = jax.vjp(jax.nn.gelu, hidden)
     grad_hidden = gelu_pull(grad_act)[0].astype(BF16)
     grad_ffin = project_back(grad_hidden, w_up)
-    unused_norm, norm_pull = jax.vjp(norm_rows, middle, gain_two.astype(F32))
-    grad_mid_norm, grad_gain_two = norm_pull(grad_ffin)
-    grad_middle = grad_done + grad_mid_norm
+    grad_middle = grad_done + norm_back(middle, gain_two, grad_ffin)
     scaled = grad_middle if router is None else router[..., None] * grad_middle
     grad_attended = scaled.astype(BF16)
     grad_mixture = project_back(grad_attended, w_out).astype(BF16)
-    return grad_ff, grad_hidden, grad_middle, grad_gain_two, grad_attended, grad_mixture
+    return grad_ff, grad_hidden, grad_middle, grad_attended, grad_mixture
 
 
 def norm_back(x, gain, grad_act_in):
-    unused, pull = jax.vjp(norm_rows, x, gain.astype(F32))
-    return pull(grad_act_in)
+    unused, pull = jax.vjp(lambda x: norm_rows(x, gain.astype(F32)), x)
+    return pull(grad_act_in)[0]
 
 
 def per_device(
@@ -510,14 +601,15 @@
     half = width // 2
     dp_size = lax.axis_size("dp")
     bits = dp_size.bit_length() - 1
+    narrow = width // dp_size
     me = lax.axis_index("seq")
+    dp_at = lax.axis_index("dp")
     y_at, core_at = me // 2, me % 2
     y_first, core_first = y_at == 0, core_at == 0
+    orders = send_orders(bits)
     place = jnp.stack(
-        [y_at, core_at, bit_reverse(lax.axis_index("dp"), bits)]
+        [y_at, core_at] + [position(order, dp_at, y_at) for order in orders]
     ).astype(jnp.int32)
-    chosen_all = lax.all_gather(chosen, "seq", axis=0)
-    chosen_mine = lax.dynamic_index_in_dim(chosen_all, y_at, 1, keepdims=False)
     counts_mine = lax.dynamic_index_in_dim(counts, y_at, 0, keepdims=False)
     own_load = lax.dynamic_index_in_dim(counts, me, 1, keepdims=False)
     live = jnp.arange(slots, dtype=jnp.int32)[None, :] < own_load[:, None]
@@ -525,120 +617,185 @@
     gather = hits.astype(BF16)
     live_hits = (hits & live[..., None]).astype(F32)
     covered = jnp.any(hits & live[..., None], axis=1)[..., None]
+    tag = jnp.pad(chosen.astype(BF16), ((0, 0), (0, LANES - slots)))
+    tag = jnp.pad(jnp.tile(tag, (1, half // LANES))[:, None, :], ((0, 0), (0, 15), (0, 0)))
 
     def scatter(values):
         return jnp.einsum("bcr,bcd->brd", live_hits, values, precision=EXACT)
 
-    act_base, base = project_pieces(place, stream_in, gain_b1, qkv_b)
+    def flat(x):
+        return x.reshape(x.shape[0] * x.shape[1], x.shape[2])
 
     picked = jnp.einsum("bcr,brd->bcd", gather, stream_in, preferred_element_type=F32)
     picked_low = picked.astype(BF16)
     router = jnp.einsum("bcd,d->bc", picked_low, route_w, preferred_element_type=F32)
     act_a, pieces = project_pieces(place, picked_low, gain_a1, qkv_a)
-    mixed, merged_a, stats_a = attend(place, counts_mine, exchange(pieces))
-    base = exchange(base)
-    mixture_a = assemble(exchange(mixed), y_first, core_first)
+    pieces = exchange(pieces)
+    act_base, base = project_pieces(place, stream_in, gain_b1, qkv_b, tag)
+    base_two = swap(base[2], "seq", 2)
+    mixed, merged_a, stats_a = attend(place, counts_mine, slots, pieces)
+    mixed = exchange(mixed)
+    mixed, late = hold(mixed, (base[1], base[3]))
+    base = [base[0], swap(late[0], "seq", 1), base_two, swap(late[1], "seq", 3)]
+    mixture_a = assemble(mixed, y_first, core_first)
     done_a, kept_a = feed_forward(picked, router, mixture_a, out_a, gain_a2, up_a, down_a)
     change = jnp.where(live[..., None], done_a - picked, 0.0)
     slot_mid = picked + change
+    base_three, slot_mid = hold(base[3], slot_mid)
+    base = base[:3] + [base_three]
     act_slot, slot_pieces = project_pieces(place, slot_mid, gain_b1, qkv_b)
-    mixed, merged_b, stats_b = attend(
-        place, counts_mine, base, chosen_mine, exchange(slot_pieces)
-    )
-    mixture_b = assemble(exchange(mixed), y_first, core_first)
-    middle = stream_in.astype(F32) + scatter(change)
-    done_b, kept_b = feed_forward(middle, None, mixture_b, out_b, gain_b2, up_b, down_b)
-
-    grad_ff_b, grad_hidden_b, grad_mid_b, g_gb2, grad_att_b, grad_mix_b = feed_backward(
-        cotangent.astype(F32), None, out_b, gain_b2, up_b, down_b, kept_b
-    )
-    grads = exchange(split_pieces(grad_mix_b, place))
-    flat = lambda x: x.reshape(x.shape[0] * x.shape[1], x.shape[2])
-    feed_b = reduce_group(
-        *feed_grad(
-            place, bits, flat(kept_b[2]), flat(grad_hidden_b), flat(kept_b[4]), flat(grad_ff_b)
-        ),
-        bits,
-    )
-    packed_b, packed_slot = attend_back(place, counts_mine, merged_b, stats_b, grads, chosen_mine)
-    packed_slot = exchange(packed_slot)
-    grad_packed_slot = assemble_packed(packed_slot, y_first, core_first)
-    packed_b = exchange(packed_b)
-
-    slot_grad, _ = norm_back(slot_mid, gain_b1, project_back(grad_packed_slot, qkv_b))
-    mid_at_slot = jnp.einsum("bcr,brd->bcd", live_hits, grad_mid_b, precision=EXACT)
-    grad_done = jnp.where(live[..., None], mid_at_slot + slot_grad, 0.0)
-    grad_ff_a, grad_hidden_a, grad_mid_a, g_ga2, grad_att_a, grad_mix_a = feed_backward(
-        grad_done, router, out_a, gain_a2, up_a, down_a, kept_a
-    )
-    grad_router = jnp.sum(kept_a[0] * grad_mid_a, axis=-1)
-    grads = exchange(split_pieces(grad_mix_a, place))
-    feed_a = reduce_group(
-        *feed_grad(
-            place, bits, flat(kept_a[2]), flat(grad_hidden_a), flat(kept_a[4]), flat(grad_ff_a)
-        ),
-        bits,
-    )
-    packed_a, _ = attend_back(place, counts_mine, merged_a, stats_a, grads)
-    packed_a = exchange(packed_a)
-    mix_a = reduce_group(*mix_grad(place, bits, act_a, packed_a, mixture_a, grad_att_a), bits)
-    grad_packed_a = assemble_packed(packed_a, y_first, core_first)
-    res_a, g_ga1 = norm_back(picked, gain_a1, project_back(grad_packed_a, qkv_a))
-    grad_picked = (
-        grad_mid_a + res_a + grad_router[..., None] * route_w.astype(F32) - grad_done
-    )
-    grad_route = jnp.einsum("bc,bcd->d", grad_router, picked, precision=EXACT)
-
+    slot_pieces = exchange(slot_pieces)
+    chosen_mine = jnp.concatenate(
+        [piece[0, rows : rows + 1, :slots] for piece in base], axis=0
+    ).astype(jnp.int32)
     act_b = jnp.where(
         covered,
         jnp.einsum("bcr,bcd->brd", live_hits.astype(BF16), act_slot, preferred_element_type=F32),
         act_base.astype(F32),
     ).astype(BF16)
-    mix_b = reduce_group(*mix_grad(place, bits, act_b, packed_b, mixture_b, grad_att_b), bits)
-    grad_packed_b = assemble_packed(packed_b, y_first, core_first)
-    res_b, g_gb1 = norm_back(middle, gain_b1, project_back(grad_packed_b, qkv_b))
+    acts = jnp.concatenate([act_b, act_a], axis=1)
+    acts_near = lax.dynamic_index_in_dim(acts, y_at, 0, keepdims=False)
+    acts_far = lax.dynamic_index_in_dim(acts, 1 - y_at, 0, keepdims=False)
+    middle = stream_in.astype(F32) + scatter(change)
+    slot_pieces, acts_near, acts_far, middle = hold(slot_pieces, acts_near, acts_far, middle)
+    acts_pair = jnp.stack([acts_near, swap(acts_far, "seq", 2)])
+    mixed, merged_b, stats_b = attend(
+        place, counts_mine, rows, base, chosen_mine, slot_pieces
+    )
+    acts_other = swap(acts_pair, "seq", 1)
+    acts = [acts_pair[0], acts_other[0], acts_pair[1], acts_other[1]]
+    acts_b = [x[:rows] for x in acts]
+    acts_a = [x[rows:] for x in acts]
+    mixture_b = assemble(exchange(mixed), y_first, core_first)
+    done_b, kept_b = feed_forward(middle, None, mixture_b, out_b, gain_b2, up_b, down_b)
+
+    x_first, z_first, y_first_order = orders
+    flat_b = [flat(x) for x in (kept_b[2], kept_b[4], mixture_b)]
+    early = [with_far(x) for x in flat_b]
+    early_grad = half_with_far(flat(cotangent), core_at)
+    grad_ff_b, grad_hidden_b, grad_mid_b, grad_att_b, grad_mix_b = feed_backward(
+        cotangent.astype(F32), None, out_b, gain_b2, up_b, down_b, kept_b
+    )
+    grads = split_pieces(grad_mix_b, place)
+    late = [half_with_far(flat(x), core_at) for x in (grad_hidden_b, grad_att_b)]
+    grads, early = hold(grads, early)
+    grads = exchange(grads)
+    operands = [y for x in early + [late[0], early_grad, late[1]] for y in x]
+    feed_b = feed_grad(place, bits, (0, 1), operands)
+    grads, feed_b = hold(grads, feed_b)
+    up_chain, down_chain = Chain(feed_b[0], x_first), Chain(feed_b[1], z_first)
+    packed_b, packed_slot = attend_back(place, counts_mine, merged_b, stats_b, grads, chosen_mine)
+    packed_slot = exchange(packed_slot)
+    part_b = qkv_grad(place, bits, 0, acts_b, packed_b)
+    token = up_chain.step(part_b)
+    token = down_chain.step(token)
+    packed_slot, part_b, packed_b, token = hold(packed_slot, part_b, packed_b, token)
+    part_chain = Chain(part_b, x_first)
+    packed_b_two = swap(packed_b[2], "seq", 2)
+
+    grad_packed_slot = assemble_packed(packed_slot, y_first, core_first)
+    slot_grad = norm_back(slot_mid, gain_b1, project_back(grad_packed_slot, qkv_b))
+    mid_at_slot = jnp.einsum("bcr,brd->bcd", live_hits, grad_mid_b, precision=EXACT)
+    grad_done = jnp.where(live[..., None], mid_at_slot + slot_grad, 0.0)
+    early = [with_far(flat(x)) for x in (kept_a[2], kept_a[4], mixture_a)]
+    grad_ff_a, grad_hidden_a, grad_mid_a, grad_att_a, grad_mix_a = feed_backward(
+        grad_done, router, out_a, gain_a2, up_a, down_a, kept_a
+    )
+    grads = split_pieces(grad_mix_a, place)
+    late = [
+        half_with_far(flat(x), core_at) for x in (grad_hidden_a, grad_ff_a, grad_att_a)
+    ]
+    grads, early = hold(grads, early)
+    grads = exchange(grads)
+    grad_router = jnp.sum(kept_a[0] * grad_mid_a, axis=-1)
+    grad_route = jnp.einsum("bc,bcd->d", grad_router, picked, precision=EXACT)
+    route = jnp.pad(
+        grad_route.reshape(dp_size, 1, narrow), ((0, 0), (0, SPARE - 1), (0, half - narrow))
+    )
+    operands = [y for x in early + late for y in x]
+    feed_a = feed_grad(place, bits, (0, 1), operands, route)
+    token = up_chain.step(feed_a)
+    token = down_chain.step(token)
+    grads, feed_a, token = hold(grads, feed_a, token)
+    up_chain_a, down_chain_a = Chain(feed_a[0], x_first), Chain(feed_a[1], z_first)
+    packed_a, _ = attend_back(place, counts_mine, merged_a, stats_a, grads)
+    returned_a = exchange(packed_a)
+    part_a = qkv_grad(place, bits, 2, acts_a, packed_a)
+    token = part_chain.step(part_a)
+    token = up_chain.step(token)
+    token = down_chain.step(token)
+    returned_a, part_a, token = hold(returned_a, part_a, token)
+    part_chain_a = Chain(part_a, y_first_order)
+
+    grad_packed_a = assemble_packed(returned_a, y_first, core_first)
+    res_a = norm_back(picked, gain_a1, project_back(grad_packed_a, qkv_a))
+    grad_picked = (
+        grad_mid_a + res_a + grad_router[..., None] * route_w.astype(F32) - grad_done
+    )
+    token = up_chain_a.step((token, grad_picked))
+    token = down_chain_a.step(token)
+    token = part_chain.step(token)
+    token = up_chain.step(token)
+    token = down_chain.step(token)
+    token = part_chain_a.step(token)
+    token = part_chain.step(token)
+    for chain in (up_chain, down_chain):
+        while chain.stage < len(chain.order):
+            token = chain.step(token)
+    token = up_chain_a.step(token)
+    while part_chain.stage < len(part_chain.order):
+        token = part_chain.step(token)
+    late, token = hold((packed_b[1], packed_b[3]), token)
+    returned_b = [packed_b[0], swap(late[0], "seq", 1), packed_b_two, swap(late[1], "seq", 3)]
+    token = down_chain_a.step(token)
+    token = part_chain_a.step(token)
+    near_b, far_b = gather_halves(
+        jnp.concatenate([up_chain.state, down_chain.state, part_chain.state]), y_first
+    )
+    token = up_chain_a.step(token)
+    token = down_chain_a.step(token)
+    token = part_chain_a.step(token)
+    for chain in (up_chain_a, down_chain_a, part_chain_a):
+        while chain.stage < len(chain.order) - 1:
+            token = chain.step(token)
+
+    grad_packed_b = assemble_packed(returned_b, y_first, core_first)
+    res_b = norm_back(middle, gain_b1, project_back(grad_packed_b, qkv_b))
     grad_input = grad_mid_b + res_b + scatter(grad_picked)
-
-    small = lax.psum(jnp.stack([grad_route, g_ga1, g_ga2, g_gb1, g_gb2]), ("dp", "seq"))
-    small = lax.dynamic_slice_in_dim(
-        small, lax.axis_index("dp") * (width // dp_size), width // dp_size, axis=1
-    )
-
-    narrow, wide = width // dp_size, OWNERS * width // dp_size
-
-    def columns(own, other, first, count):
-        def flat_half(x):
-            parts = [x[first + t * narrow : first + (t + 1) * narrow] for t in range(count)]
-            return jnp.concatenate(parts, axis=1).astype(F32)
-
-        return both_halves(flat_half(own), flat_half(other), core_first)
-
-    def qkv_columns(own, other):
-        parts = [columns(own, other, part * narrow, 1) for part in range(3)]
-        return jnp.concatenate(parts, axis=1)
-
-    def down_rows(own, other):
-        at = OWNERS * narrow
-        return both_halves(
-            own[at : at + wide].astype(F32), other[at : at + wide].astype(F32), core_first
-        )
+    qkv_gb, out_gb, up_gb, down_gb = finish(place, OWNERS * narrow, narrow, width, near_b, far_b)
+    token = (token, qkv_gb, grad_input)
+    for chain in (up_chain_a, down_chain_a, part_chain_a):
+        token = chain.step(token)
+    near, far = gather_halves(
+        jnp.concatenate([up_chain_a.state, down_chain_a.state, part_chain_a.state]), y_first
+    )
+    down_at = OWNERS * narrow + SPARE
+    qkv_ga, out_ga, up_ga, down_ga = finish(place, down_at, narrow, width, near, far)
+    at = OWNERS * narrow // 2
+    route = near[0, at, :narrow].astype(F32) + far[0, at, :narrow].astype(F32)
+
+    def gain_grad(found, weight, gain):
+        at = dp_at * narrow
+        weight = lax.dynamic_slice_in_dim(weight, at, narrow, axis=0).astype(F32)
+        gain = lax.dynamic_slice_in_dim(gain, at, narrow, axis=0).astype(F32)
+        return jnp.sum(found * weight, axis=1) / gain
 
     return (
         done_b.astype(BF16),
         grad_input,
-        small[0],
-        small[1],
-        qkv_columns(*mix_a),
-        columns(*mix_a, 3 * narrow, 1),
-        small[2],
-        columns(*feed_a, 0, OWNERS),
-        down_rows(*feed_a),
-        small[3],
-        qkv_columns(*mix_b),
-        columns(*mix_b, 3 * narrow, 1),
-        small[4],
-        columns(*feed_b, 0, OWNERS),
-        down_rows(*feed_b),
+        route,
+        gain_grad(qkv_ga, qkv_a, gain_a1),
+        qkv_ga,
+        out_ga,
+        gain_grad(up_ga, up_a, gain_a2),
+        up_ga,
+        down_ga,
+        gain_grad(qkv_gb, qkv_b, gain_b1),
+        qkv_gb,
+        out_gb,
+        gain_grad(up_gb, up_b, gain_b2),
+        up_gb,
+        down_gb,
     )
 
 

time: 602 us -> 420 us (0.70)
  waiting for transfers between devices: 222 us -> 111 us
  blocking collectives: 101 us -> 0 us
  starting transfers between devices: 42.8 us -> 61.6 us
  local copies, waits for them, and re-layouts: 21.5 us -> 39.3 us
  Pallas kernels: 105 us -> 96.3 us
    ppermute x54 -> x72, waiting for transfers between devices: 222 us -> 111 us  [swap(): return lax.ppermute(x, axis, [(i, i ^ bit) for i in range(size)])]
    psum x1 -> x0, blocking collectives: 78.6 us -> none  [per_device(): lax.psum(jnp.stack([grad_route, g_ga1, g_ga2, g_gb1, g_gb2]), ('dp', 'seq'))]
    all_gather x1 -> x0, blocking collectives: 21.9 us -> none  [per_device(): chosen_all = lax.all_gather(chosen, 'seq', axis=0)]
    ppermute x54 -> x72, starting transfers between devices: 42.8 us -> 61.6 us  [swap(): return lax.ppermute(x, axis, [(i, i ^ bit) for i in range(size)])]
    slice x16 -> x12, local copies, waits for them, and re-layouts: 3.86 us -> 17.4 us  [the longest x6 12 us: halves(): return (unit[:n], unit[n:])]
    pallas_call x7 -> x9, Pallas kernels: 64 us -> 55.2 us  [the longest x2 22.2 us: feed_grad(): pl.pallas_call(lambda *refs: feed_grad_kernel(bits, orders, routed, *refs...]
    dot_general x6, matrix products: 21.2 us -> 27.9 us  [project(): jnp.einsum('bnd,de->bne', left_side, weight, preferred_element_type=F32)]
    convert_element_type x20 -> x18, other arithmetic: 18.6 us -> 14.6 us  [add_low(): return (a.astype(F32) + b.astype(F32)).astype(BF16)]
  transfers between devices with their start and end apart: 54 -> 72, of which waited for: 22 -> 17; matrix products, arithmetic and copies ran while one was open for 11% -> 29% of each run, Pallas kernels for 11% -> 18%
where the time goes in v2:
time: 420 us; the launch traced here: 415 us
  waiting for transfers between devices  111 us (26%)
  Pallas kernels  96.3 us (23%)
  starting transfers between devices  61.6 us (15%)
  matrix products  61.2 us (15%)
  other arithmetic  42.8 us (10%)
  local copies, waits for them, and re-layouts  39.3 us (9%)
    ppermute x72, waiting for transfers between devices, swap(): return lax.ppermute(x, axis, [(i, i ^ bit) for i in range(size)])  111 us
    ppermute x72, starting transfers between devices, swap(): return lax.ppermute(x, axis, [(i, i ^ bit) for i in range(size)])  61.6 us
    dot_general x6, matrix products, project(): jnp.einsum('bnd,de->bne', left_side, weight, preferred_element_type=F32)  27.9 us
    pallas_call x2, Pallas kernels, attend_back(): pl.pallas_call(lambda *refs: attend_back_kernel(rows, routed, *refs), nam...  24 us
    dot_general x9, matrix products, project_back(): jnp.einsum('bne,de->bnd', gradient, weight, preferred_element_type=F32)  23.9 us
    pallas_call x2, Pallas kernels, feed_grad(): pl.pallas_call(lambda *refs: feed_grad_kernel(bits, orders, routed, *refs...  22.2 us
    pallas_call x2, Pallas kernels, attend(): pl.pallas_call(lambda *refs: attend_kernel(rows, routed, *refs), name='at...  17.1 us
    pallas_call x3, Pallas kernels, project_pieces(): pl.pallas_call(lambda *refs: project_kernel(tagged, *refs), name='project...  15.2 us
  transfers between devices with their start and end apart: 72, of which 17 were waited for; matrix products, arithmetic and copies ran while one was open for 29% of the time, Pallas kernels for 18%

profile of v2, /device:TPU:0, one launch (start us, length us, event | category | flops | bytes accessed | tf_op | source)
XLA Modules:
  0.0 415.0 jit_solution(4186135862947460390)
XLA Ops:
  0.7 2.2 fusion.161
  3.6 4.2 %project_pieces.3 = (bf16[2,64,768]{2,1,0:T(8,128)(2,1)}, bf16[3,64,384]{2,1,0:T(8,128)(2,1)}, bf16[3,64,384]{2,1,0:T(8,128)(2,1)}, bf16[3,64,384]{2,1,0:T(8,128)(2,1)}, bf16[3,64,384]{2,1,0:T(8,128)(2,1)}) custom-call(s32[5]{0:T(128)} %stack.75.refs_0_, bf16[2,64,768]{2,1,0:T(8,128)(2,1)} %get-tuple-element.412.refs_1_, bf16[768]{0:T(1024)(128)(2,1)} %refs_2_.3, ...), custom_call_target="tpu_custom_call" | custom-call | flops 452984832 | bytes 4718592 | tf_op jit(solution)/shard_map/project_pieces/pallas_call | solution.py:59
  8.3 2.5 collective-permute-start.1
  11.6 6.8 %project_pieces.4 = (bf16[2,256,768]{2,1,0:T(8,128)(2,1)}, bf16[3,272,384]{2,1,0:T(8,128)(2,1)}, bf16[3,272,384]{2,1,0:T(8,128)(2,1)}, bf16[3,272,384]{2,1,0:T(8,128)(2,1)}, bf16[3,272,384]{2,1,0:T(8,128)(2,1)}) custom-call(s32[5]{0:T(128)} %stack.75.refs_0_, bf16[2,256,768]{2,1,0:T(8,128)(2,1)} %refs_1_.1, bf16[768]{0:T(1024)(128)(2,1)} %refs_2_.5, ...), custom_call_target="tpu_custom_call" | custom-call | flops 1811939328 | bytes 8257536 | tf_op jit(solution)/shard_map/project_pieces/pallas_call | solution.py:59
  23.7 4.4 %attend_routed.1 = (bf16[64,384]{1,0:T(8,128)(2,1)}, bf16[64,384]{1,0:T(8,128)(2,1)}, bf16[64,384]{1,0:T(8,128)(2,1)}, bf16[64,384]{1,0:T(8,128)(2,1)}, bf16[3,2...) custom-call(s32[5]{0:T(128)} %stack.75.refs_0_, s32[4]{0:T(128)} %fusion.146.refs_1_, ...), custom_call_target="tpu_custom_call" | custom-call | flops 402653184 | bytes 1572864 | tf_op jit(solution)/shard_map/attend_routed/pallas_call | solution.py:180
  33.6 2.9 collective-permute-done.4
  39.1 1.8 multiply_reduce_fusion.14
  41.9 5.4 %multiply_convert_fusion.2 = (bf16[2,64,3072]{2,1,0:T(8,128)(2,1)}, f32[2,64,3072]{2,1,0:T(8,128)}) fusion(bf16[2,64,768]{2,1,0:T(8,128)(2,1)} %multiply_convert_fusion.4, bf16[768,3072]{1,0:T(8,128)(2,1)} %param.25), kind=kOutput, calls=%fused_computation.63 | convolution fusion | flops 607518720 | bytes 7274496 | tf_op jit(solution)/shard_map/bnd,de->bne/dot_general | solution.py:544
  47.4 2.8 fusion.162
  53.5 4.2 %project_pieces.5 = (bf16[2,64,768]{2,1,0:T(8,128)(2,1)}, bf16[3,64,384]{2,1,0:T(8,128)(2,1)}, bf16[3,64,384]{2,1,0:T(8,128)(2,1)}, bf16[3,64,384]{2,1,0:T(8,128)(2,1)}, bf16[3,64,384]{2,1,0:T(8,128)(2,1)}) custom-call(s32[5]{0:T(128)} %stack.75.refs_0_, f32[2,64,768]{2,1,0:T(8,128)} %get-tuple-element.167.refs_1_, bf16[768]{0:T(1024)(128)(2,1)} %refs_2_.5, ...), custom_call_target="tpu_custom_call" | custom-call | flops 452984832 | bytes 4718592 | tf_op jit(solution)/shard_map/project_pieces/pallas_call | solution.py:59
  66.9 12.7 %attend_dense.1 = (bf16[256,384]{1,0:T(8,128)(2,1)}, bf16[256,384]{1,0:T(8,128)(2,1)}, bf16[256,384]{1,0:T(8,128)(2,1)}, bf16[256,384]{1,0:T(8,128)(2,1)}, bf16[...) custom-call(s32[5]{0:T(128)} %stack.75.refs_0_, s32[4]{0:T(128)} %fusion.146.refs_1_, ...), custom_call_target="tpu_custom_call" | custom-call | flops 4026531840 | bytes 6291456 | tf_op jit(solution)/shard_map/attend_dense/pallas_call | solution.py:180
  79.6 1.8 collective-permute-start.13
  87.7 3.5 collective-permute-done.14
  92.6 9.8 %multiply_convert_fusion = (bf16[2,256,3072]{2,1,0:T(8,128)(2,1)S(1)}, f32[2,256,3072]{2,1,0:T(8,128)}) fusion(bf16[2,256,768]{2,1,0:T(8,128)(2,1)S(1)} %multiply_convert_fusion.1, bf16[768,3072]{1,0:T(8,128)(2,1)} %param.31), kind=kOutput, calls=%fused_computation.9 | convolution fusion | flops 2430074880 | bytes 14942208 | tf_op jit(solution)/shard_map/bnd,de->bne/dot_general | solution.py:544
  102.9 8.5 %fusion.6 = bf16[2,256,3072]{2,1,0:T(8,128)(2,1)S(1)} fusion(f32[2,256,3072]{2,1,0:T(8,128)} %get-tuple-element.422, bf16[2,256,768]{2,1,0:T(8,128)(2,1)S(1)} %copy-done.27, bf16[3072,768]{1,0:T(8,128)(2,1)S(1)} %bitcast.292), kind=kOutput, calls=%fused_computation.8 | convolution fusion | flops 2447376384 | bytes 14942208 | tf_op jit(solution)/shard_map/bne,de->bnd/dot_general | solution.py:548
  113.1 2.7 multiply_reduce_fusion.2
  128.7 15.3 %feed_grad.2 = (bf16[16,192,384]{2,1,0:T(8,128)(2,1)}, bf16[16,240,384]{2,1,0:T(8,128)(2,1)}) custom-call(s32[5]{0:T(128)} %stack.75.refs_0_, bf16[512,768]{1,0:T(8,128)(2,1)} %bitcast.281, bf16[512,768]{1,0:T(8,128)(2,1)} %copy-done.73, bf16[512,3072]{1,0:T(8,128)(2,1)} %bitcast.294, bf16[512,3072]{1,0:T(8,128)(2,1)} %copy-done.71, ...), custom_call_target="tpu_custom_call" | custom-call | flops 5435817984 | bytes 21037056 | tf_op jit(solution)/shard_map/feed_grad/pallas_call | solution.py:369
  144.9 3.4 fusion.156
  154.6 19.6 %attend_dense_back.1 = (bf16[3,256,384]{2,1,0:T(8,128)(2,1)}, bf16[3,256,384]{2,1,0:T(8,128)(2,1)}, bf16[3,256,384]{2,1,0:T(8,128)(2,1)}, bf16[3,256,384]{2,1,0:...) custom-call(s32[5]{0:T(128)} %stack.75.refs_0_, ...), custom_call_target="tpu_custom_call" | custom-call | flops 10066329600 | bytes 6291456 | tf_op jit(solution)/shard_map/attend_dense_back/pallas_call | solution.py:280
  174.3 6.0 %qkv_grad.2 = bf16[16,144,384]{2,1,0:T(8,128)(2,1)} custom-call(s32[5]{0:T(128)} %stack.75.refs_0_, bf16[256,768]{1,0:T(8,128)(2,1)} %slice.343.refs_1_, bf16[256,768]{1,0:T(8,128)(2,1)} %get-tuple-element.345.refs_2_, bf16[256,768]{1,0:T(8,128)(2,1)} %slice.453.refs_3_, bf16[256,768]{1,0:T(8,128)(2,1)} %get-tuple-element.344.refs_4_, ...), custom_call_target="tpu_custom_call" | custom-call | flops 1811939328 | bytes 5701632 | tf_op jit(solution)/shard_map/qkv_grad/pallas_call | solution.py:397
  180.9 2.9 add_convert_fusion.7
  185.3 2.9 add_convert_fusion.3
  195.9 4.7 %fusion.42 = bf16[2,64,3072]{2,1,0:T(8,128)(2,1)S(1)} fusion(f32[2,64,3072]{2,1,0:T(8,128)S(1)} %copy-done.94, bf16[2,64,768]{2,1,0:T(8,128)(2,1)S(1)} %get-tuple-element.426, bf16[3072,768]{1,0:T(8,128)(2,1)} %param.26), kind=kOutput, calls=%fused_computation.51 | convolution fusion | flops 611844096 | bytes 7274496 | tf_op jit(solution)/shard_map/bne,de->bnd/dot_general | solution.py:548
  211.3 6.9 %feed_grad.3 = (bf16[16,208,384]{2,1,0:T(8,128)(2,1)}, bf16[16,240,384]{2,1,0:T(8,128)(2,1)}) custom-call(s32[5]{0:T(128)} %stack.75.refs_0_, bf16[128,768]{1,0:T(8,128)(2,1)} %bitcast.56.refs_1_, bf16[128,768]{1,0:T(8,128)(2,1)} %collective-permute-done.31.refs_2_, bf16[128,3072]{1,0:T(8,128)(2,1)} %bitcast.57.refs_3_, ...), custom_call_target="tpu_custom_call" | custom-call | flops 1358954496 | bytes 9240576 | tf_op jit(solution)/shard_map/feed_grad/pallas_call | solution.py:369
  219.4 2.2 add_convert_fusion.19
  223.0 2.0 add_convert_fusion.15
  226.1 4.4 %attend_routed_back.1 = (bf16[3,64,384]{2,1,0:T(8,128)(2,1)}, bf16[3,64,384]{2,1,0:T(8,128)(2,1)}, bf16[3,64,384]{2,1,0:T(8,128)(2,1)}, bf16[3,64,384]{2,1,0:T(8,128)(2,1)}) custom-call(s32[5]{0:T(128)} %stack.75.refs_0_, s32[4]{0:T(128)} %fusion.146.refs_1_, bf16[3,256,384]{2,1,0:T(8,128)(2,1)} %get-tuple-element.224.refs_2_, ...), custom_call_target="tpu_custom_call" | custom-call | flops 1006632960 | bytes 1572864 | tf_op jit(solution)/shard_map/attend_routed_back/pallas_call | solution.py:280
  231.6 3.4 fusion.157
  235.0 1.9 fusion.155
  236.9 4.6 %qkv_grad.3 = bf16[16,144,384]{2,1,0:T(8,128)(2,1)} custom-call(s32[5]{0:T(128)} %stack.75.refs_0_, bf16[64,768]{1,0:T(8,128)(2,1)} %slice.362.refs_1_, bf16[64,768]{1,0:T(8,128)(2,1)} %get-tuple-element.343.refs_2_, bf16[64,768]{1,0:T(8,128)(2,1)} %slice.460.refs_3_, bf16[64,768]{1,0:T(8,128)(2,1)} %get-tuple-element.342.refs_4_, ...), custom_call_target="tpu_custom_call" | custom-call | flops 452984832 | bytes 2752512 | tf_op jit(solution)/shard_map/qkv_grad/pallas_call | solution.py:397
  246.1 7.1 %collective-permute-done.47 = bf16[2,240,384]{2,1,0:T(8,128)(2,1)S(1)} collective-permute-done((bf16[2,240,384]{2,1,0:T(8,128)(2,1)}, bf16[2,240,384]{2,1,0:T(8,128)(2,1)S(1)}, u32[]{:S(2)}, u32[]{:S(2)}) %collective-permute-start.47) | collective-permute-done | bytes 368672 | tf_op jit(solution)/shard_map/ppermute | solution.py:449
  257.1 2.6 collective-permute-start.51
  265.1 18.1 %collective-permute-done.48 = bf16[8,208,384]{2,1,0:T(8,128)(2,1)S(1)} collective-permute-done((bf16[8,208,384]{2,1,0:T(8,128)(2,1)S(1)}, bf16[8,208,384]{2,1,0:T(8,128)(2,1)S(1)}, u32[]{:S(2)}, u32[]{:S(2)}) %collective-permute-start.48) | collective-permute-done | bytes 1277984 | tf_op jit(solution)/shard_map/ppermute | solution.py:449
  283.1 2.6 collective-permute-start.52
  286.0 7.1 %collective-permute-done.49 = bf16[8,240,384]{2,1,0:T(8,128)(2,1)S(1)} collective-permute-done((bf16[8,240,384]{2,1,0:T(8,128)(2,1)S(1)}, bf16[8,240,384]{2,1,0:T(8,128)(2,1)S(1)}, u32[]{:S(2)}, u32[]{:S(2)}) %collective-permute-start.49) | collective-permute-done | bytes 1474592 | tf_op jit(solution)/shard_map/ppermute | solution.py:449
  297.5 18.2 %collective-permute-done.53 = bf16[8,144,384]{2,1,0:T(8,128)(2,1)S(1)} collective-permute-done((bf16[8,144,384]{2,1,0:T(8,128)(2,1)S(1)}, bf16[8,144,384]{2,1,0:T(8,128)(2,1)S(1)}, u32[]{:S(2)}, u32[]{:S(2)}) %collective-permute-start.53) | collective-permute-done | bytes 884768 | tf_op jit(solution)/shard_map/ppermute | solution.py:449
  317.7 8.6 %collective-permute-done.55 = bf16[4,208,384]{2,1,0:T(8,128)(2,1)S(1)} collective-permute-done((bf16[4,208,384]{2,1,0:T(8,128)(2,1)S(1)}, bf16[4,208,384]{2,1,0:T(8,128)(2,1)S(1)}, u32[]{:S(2)}, u32[]{:S(2)}) %collective-permute-start.55) | collective-permute-done | bytes 639008 | tf_op jit(solution)/shard_map/ppermute | solution.py:449
  329.3 5.6 %collective-permute-done.62 = bf16[2,208,384]{2,1,0:T(8,128)(2,1)S(1)} collective-permute-done((bf16[2,208,384]{2,1,0:T(8,128)(2,1)S(1)}, bf16[2,208,384]{2,1,0:T(8,128)(2,1)S(1)}, u32[]{:S(2)}, u32[]{:S(2)}) %collective-permute-start.62) | collective-permute-done | bytes 319520 | tf_op jit(solution)/shard_map/ppermute | solution.py:449
  335.0 15.2 %collective-permute-done.65 = bf16[576,384]{1,0:T(8,128)(2,1)S(1)} collective-permute-done((bf16[576,384]{1,0:T(8,128)(2,1)S(1)}, bf16[576,384]{1,0:T(8,128)(2,1)S(1)}, u32[]{:S(2)}, u32[]{:S(2)}) %collective-permute-start.65) | collective-permute-done | bytes 442400 | tf_op jit(solution)/shard_map/ppermute | solution.py:449
  350.2 2.1 collective-permute-start.63
  357.9 2.1 multiply_reduce_fusion.1
  360.1 2.4 fusion.45
  365.7 3.7 finish_grads.2
  369.4 7.8 %collective-permute-done.68 = bf16[1,240,384]{2,1,0:T(8,128)(2,1)S(1)} collective-permute-done((bf16[1,240,384]{2,1,0:T(8,128)(2,1)S(1)}, bf16[1,240,384]{2,1,0:T(8,128)(2,1)S(1)}, u32[]{:S(2)}, u32[]{:S(2)}) %collective-permute-start.68) | collective-permute-done | bytes 184352 | tf_op jit(solution)/shard_map/ppermute | solution.py:449
  377.3 2.0 collective-permute-done.69
  380.9 10.7 %collective-permute-done.70 = bf16[592,384]{1,0:T(8,128)(2,1)S(1)} collective-permute-done((bf16[592,384]{1,0:T(8,128)(2,1)S(1)}, bf16[592,384]{1,0:T(8,128)(2,1)S(1)}, u32[]{:S(2)}, u32[]{:S(2)}) %collective-permute-start.70) | collective-permute-done | bytes 454688 | tf_op jit(solution)/shard_map/ppermute | solution.py:449
  392.0 7.2 %add_convert_fusion = bf16[2,256,768]{2,1,0:T(8,128)(2,1)} fusion(f32[2,256,768]{2,1,0:T(8,128)S(1)} %copy-done.3, bf16[2,256,3072]{2,1,0:T(8,128)(2,1)} %copy-done.70, bf16[3072,768]{1,0:T(8,128)(2,1)} %param.32), kind=kOutput, calls=%fused_computation.58 | convolution fusion | flops 2416705536 | bytes 10223616 | tf_op jit(solution)/shard_map/bnd,de->bne/dot_general | solution.py:544
  404.4 3.5 finish_grads.3
  (457 shorter events, 129.3 us)
Async XLA Ops:
  7.8 15.1 %collective-permute-start = (bf16[3,64,384]{2,1,0:T(8,128)(2,1)}, bf16[3,64,384]{2,1,0:T(8,128)(2,1)S(1)}, u32[]{:S(2)}, u32[]{:S(2)}) collective-permute-start(bf16[3,64,384]{2,1,0:T(8,128)(2,1)} %get-tuple-element.153), channel_id=1, source_target_pairs={{0,1},{1,0},{2,3},{3,2},{4,5},{5,4},{6,7},{7,6},{8,9},{9,8},{10,11... | collective-permute-start | bytes 442376 | tf_op jit(solution)/shard_map/ppermute | solution.py:449
  8.3 14.7 %collective-permute-start.1 = (bf16[3,64,384]{2,1,0:T(8,128)(2,1)}, bf16[3,64,384]{2,1,0:T(8,128)(2,1)S(1)}, u32[]{:S(2)}, u32[]{:S(2)}) collective-permute-start(bf16[3,64,384]{2,1,0:T(8,128)(2,1)} %get-tuple-element.154), channel_id=1, source_target_pairs={{0,2},{1,3},{2,0},{3,1},{4,6},{5,7},{6,4},{7,5},{8,10},{9,11},{10,... | collective-permute-start | bytes 442376 | tf_op jit(solution)/shard_map/ppermute | solution.py:449
  10.8 12.2 %collective-permute-start.2 = (bf16[3,64,384]{2,1,0:T(8,128)(2,1)}, bf16[3,64,384]{2,1,0:T(8,128)(2,1)S(1)}, u32[]{:S(2)}, u32[]{:S(2)}) collective-permute-start(bf16[3,64,384]{2,1,0:T(8,128)(2,1)} %get-tuple-element.155), channel_id=1, source_target_pairs={{0,3},{1,2},{2,1},{3,0},{4,7},{5,6},{6,5},{7,4},{8,11},{9,10},{10,... | collective-permute-start | bytes 442376 | tf_op jit(solution)/shard_map/ppermute | solution.py:449
  18.4 32.8 %collective-permute-start.11 = (bf16[3,272,384]{2,1,0:T(8,128)(2,1)}, bf16[3,272,384]{2,1,0:T(8,128)(2,1)}, u32[]{:S(2)}, u32[]{:S(2)}) collective-permute-start(bf16[3,272,384]{2,1,0:T(8,128)(2,1)} %get-tuple-element.178), channel_id=1, source_target_pairs={{0,2},{1,3},{2,0},{3,1},{4,6},{5,7},{6,4},{7,5},{8,10},{9,11},{10,... | collective-permute-start | bytes 1880072 | tf_op jit(solution)/shard_map/ppermute | solution.py:449
  36.5 16.2 %collective-permute-start.6 = (bf16[3,272,384]{2,1,0:T(8,128)(2,1)}, bf16[3,272,384]{2,1,0:T(8,128)(2,1)S(1)}, u32[]{:S(2)}, u32[]{:S(2)}) collective-permute-start(bf16[3,272,384]{2,1,0:T(8,128)(2,1)} %get-tuple-element.162), channel_id=1, source_target_pairs={{0,3},{1,2},{2,1},{3,0},{4,7},{5,6},{6,5},{7,4},{8,11},{9,10},{10,... | collective-permute-start | bytes 1880072 | tf_op jit(solution)/shard_map/ppermute | solution.py:449
  40.9 21.4 %collective-permute-start.10 = (bf16[3,272,384]{2,1,0:T(8,128)(2,1)}, bf16[3,272,384]{2,1,0:T(8,128)(2,1)}, u32[]{:S(2)}, u32[]{:S(2)}) collective-permute-start(bf16[3,272,384]{2,1,0:T(8,128)(2,1)} %get-tuple-element.177), channel_id=1, source_target_pairs={{0,1},{1,0},{2,3},{3,2},{4,5},{5,4},{6,7},{7,6},{8,9},{9,8},{10,11... | collective-permute-start | bytes 1880072 | tf_op jit(solution)/shard_map/ppermute | solution.py:449
  85.9 26.2 %collective-permute-start.27 = (bf16[320,768]{1,0:T(8,128)(2,1)S(1)}, bf16[320,768]{1,0:T(8,128)(2,1)S(1)}, u32[]{:S(2)}, u32[]{:S(2)}) collective-permute-start(bf16[320,768]{1,0:T(8,128)(2,1)S(1)} %copy-done.46), channel_id=1, source_target_pairs={{0,2},{1,3},{2,0},{3,1},{4,6},{5,7},{6,4},{7,5},{8,10},{9,11},{10,... | collective-permute-start | bytes 1474568 | tf_op jit(solution)/shard_map/ppermute | solution.py:449
  102.4 21.6 %collective-permute-start.16 = (bf16[512,3072]{1,0:T(8,128)(2,1)S(1)}, bf16[512,3072]{1,0:T(8,128)(2,1)S(1)}, u32[]{:S(2)}, u32[]{:S(2)}) collective-permute-start(bf16[512,3072]{1,0:T(8,128)(2,1)S(1)} %bitcast.293), channel_id=1, source_target_pairs={{0,1},{1,0},{2,3},{3,2},{4,5},{5,4},{6,7},{7,6},{8,9},{9,8},{10,11... | collective-permute-start | bytes 9437192 | tf_op jit(solution)/shard_map/ppermute | solution.py:449
  111.5 14.7 %collective-permute-start.21 = (bf16[512,1536]{1,0:T(8,128)(2,1)S(1)}, bf16[512,1536]{1,0:T(8,128)(2,1)S(1)}, u32[]{:S(2)}, u32[]{:S(2)}) collective-permute-start(bf16[512,1536]{1,0:T(8,128)(2,1)S(1)} %constant_dynamic-slice_fusion.5), channel_id=1, source_target_pairs={{0,1},{1,0},{2,3},{3,2},{4,5},{5,4},{6,7},{7,6},{8,9},{9,8},{10,11... | collective-permute-start | bytes 4718600 | tf_op jit(solution)/shard_map/ppermute | solution.py:449
  123.5 81.6 %collective-permute-start.31 = (bf16[128,768]{1,0:T(8,128)(2,1)}, bf16[128,768]{1,0:T(8,128)(2,1)}, u32[]{:S(2)}, u32[]{:S(2)}) collective-permute-start(bf16[128,768]{1,0:T(8,128)(2,1)} %bitcast.56.refs_1_), channel_id=1, source_target_pairs={{0,1},{1,0},{2,3},{3,2},{4,5},{5,4},{6,7},{7,6},{8,9},{9,8},{10,11... | collective-permute-start | bytes 589832 | tf_op jit(solution)/shard_map/ppermute | solution.py:449
  124.0 81.1 %collective-permute-start.32 = (bf16[128,3072]{1,0:T(8,128)(2,1)}, bf16[128,3072]{1,0:T(8,128)(2,1)}, u32[]{:S(2)}, u32[]{:S(2)}) collective-permute-start(bf16[128,3072]{1,0:T(8,128)(2,1)} %bitcast.57.refs_3_), channel_id=1, source_target_pairs={{0,1},{1,0},{2,3},{3,2},{4,5},{5,4},{6,7},{7,6},{8,9},{9,8},{10,11... | collective-permute-start | bytes 2359304 | tf_op jit(solution)/shard_map/ppermute | solution.py:449
  124.1 19.9 %collective-permute-start.18 = (bf16[256,384]{1,0:T(8,128)(2,1)S(1)}, bf16[256,384]{1,0:T(8,128)(2,1)S(1)}, u32[]{:S(2)}, u32[]{:S(2)}) collective-permute-start(bf16[256,384]{1,0:T(8,128)(2,1)S(1)} %get-tuple-element.191), channel_id=1, source_target_pairs={{0,1},{1,0},{2,3},{3,2},{4,5},{5,4},{6,7},{7,6},{8,9},{9,8},{10,11... | collective-permute-start | bytes 589832 | tf_op jit(solution)/shard_map/ppermute | solution.py:449
  124.5 19.5 %collective-permute-start.19 = (bf16[256,384]{1,0:T(8,128)(2,1)S(1)}, bf16[256,384]{1,0:T(8,128)(2,1)S(1)}, u32[]{:S(2)}, u32[]{:S(2)}) collective-permute-start(bf16[256,384]{1,0:T(8,128)(2,1)S(1)} %get-tuple-element.192), channel_id=1, source_target_pairs={{0,2},{1,3},{2,0},{3,1},{4,6},{5,7},{6,4},{7,5},{8,10},{9,11},{10,... | collective-permute-start | bytes 589832 | tf_op jit(solution)/shard_map/ppermute | solution.py:449
  127.4 16.6 %collective-permute-start.20 = (bf16[256,384]{1,0:T(8,128)(2,1)S(1)}, bf16[256,384]{1,0:T(8,128)(2,1)S(1)}, u32[]{:S(2)}, u32[]{:S(2)}) collective-permute-start(bf16[256,384]{1,0:T(8,128)(2,1)S(1)} %get-tuple-element.193), channel_id=1, source_target_pairs={{0,3},{1,2},{2,1},{3,0},{4,7},{5,6},{6,5},{7,4},{8,11},{9,10},{10,... | collective-permute-start | bytes 589832 | tf_op jit(solution)/shard_map/ppermute | solution.py:449
  148.3 35.6 %collective-permute-start.30 = (bf16[8,240,384]{2,1,0:T(8,128)(2,1)}, bf16[8,240,384]{2,1,0:T(8,128)(2,1)}, u32[]{:S(2)}, u32[]{:S(2)}) collective-permute-start(bf16[8,240,384]{2,1,0:T(8,128)(2,1)} %get-tuple-element.308), channel_id=1, source_target_pairs={{0,8},{4,12},{8,0},{12,4},{16,24},{20,28},{24,16},{28,20},{1,9},{5... | collective-permute-start | bytes 4423688 | tf_op jit(solution)/shard_map/ppermute | solution.py:449
  151.5 28.8 %collective-permute-start.29 = (bf16[8,192,384]{2,1,0:T(8,128)(2,1)}, bf16[8,192,384]{2,1,0:T(8,128)(2,1)}, u32[]{:S(2)}, u32[]{:S(2)}) collective-permute-start(bf16[8,192,384]{2,1,0:T(8,128)(2,1)} %get-tuple-element.321), channel_id=1, source_target_pairs={{0,4},{4,0},{8,12},{12,8},{16,20},{20,16},{24,28},{28,24},{1,5},{5... | collective-permute-start | bytes 3538952 | tf_op jit(solution)/shard_map/ppermute | solution.py:449
  174.3 13.9 %collective-permute-start.24 = (bf16[3,64,384]{2,1,0:T(8,128)(2,1)}, bf16[3,64,384]{2,1,0:T(8,128)(2,1)}, u32[]{:S(2)}, u32[]{:S(2)}) collective-permute-start(bf16[3,64,384]{2,1,0:T(8,128)(2,1)} %get-tuple-element.207), channel_id=1, source_target_pairs={{0,1},{1,0},{2,3},{3,2},{4,5},{5,4},{6,7},{7,6},{8,9},{9,8},{10,11... | collective-permute-start | bytes 442376 | tf_op jit(solution)/shard_map/ppermute | solution.py:449
  188.1 17.0 %collective-permute-start.33 = (bf16[128,768]{1,0:T(8,128)(2,1)S(1)}, bf16[128,768]{1,0:T(8,128)(2,1)S(1)}, u32[]{:S(2)}, u32[]{:S(2)}) collective-permute-start(bf16[128,768]{1,0:T(8,128)(2,1)S(1)} %bitcast.285), channel_id=1, source_target_pairs={{0,1},{1,0},{2,3},{3,2},{4,5},{5,4},{6,7},{7,6},{8,9},{9,8},{10,11... | collective-permute-start | bytes 589832 | tf_op jit(solution)/shard_map/ppermute | solution.py:449
  188.4 29.8 %collective-permute-start.40 = (bf16[4,192,384]{2,1,0:T(8,128)(2,1)}, bf16[4,192,384]{2,1,0:T(8,128)(2,1)}, u32[]{:S(2)}, u32[]{:S(2)}) collective-permute-start(bf16[4,192,384]{2,1,0:T(8,128)(2,1)} %get-tuple-element.318), channel_id=1, source_target_pairs={{0,2},{1,3},{2,0},{3,1},{4,6},{5,7},{6,4},{7,5},{8,10},{9,11},{10,... | collective-permute-start | bytes 1769480 | tf_op jit(solution)/shard_map/ppermute | solution.py:449
  189.8 31.7 %collective-permute-start.41 = (bf16[4,240,384]{2,1,0:T(8,128)(2,1)}, bf16[4,240,384]{2,1,0:T(8,128)(2,1)}, u32[]{:S(2)}, u32[]{:S(2)}) collective-permute-start(bf16[4,240,384]{2,1,0:T(8,128)(2,1)} %get-tuple-element.305), channel_id=1, source_target_pairs={{0,4},{4,0},{8,12},{12,8},{16,20},{20,16},{24,28},{28,24},{1,5},{5... | collective-permute-start | bytes 2211848 | tf_op jit(solution)/shard_map/ppermute | solution.py:449
  208.6 16.4 %collective-permute-start.34 = (bf16[64,384]{1,0:T(8,128)(2,1)}, bf16[64,384]{1,0:T(8,128)(2,1)}, u32[]{:S(2)}, u32[]{:S(2)}) collective-permute-start(bf16[64,384]{1,0:T(8,128)(2,1)} %get-tuple-element.231), channel_id=1, source_target_pairs={{0,1},{1,0},{2,3},{3,2},{4,5},{5,4},{6,7},{7,6},{8,9},{9,8},{10,11... | collective-permute-start | bytes 147464 | tf_op jit(solution)/shard_map/ppermute | solution.py:449
  209.1 16.3 %collective-permute-start.35 = (bf16[64,384]{1,0:T(8,128)(2,1)}, bf16[64,384]{1,0:T(8,128)(2,1)S(1)}, u32[]{:S(2)}, u32[]{:S(2)}) collective-permute-start(bf16[64,384]{1,0:T(8,128)(2,1)} %get-tuple-element.232), channel_id=1, source_target_pairs={{0,2},{1,3},{2,0},{3,1},{4,6},{5,7},{6,4},{7,5},{8,10},{9,11},{10,... | collective-permute-start | bytes 147464 | tf_op jit(solution)/shard_map/ppermute | solution.py:449
  211.1 14.3 %collective-permute-start.36 = (bf16[64,384]{1,0:T(8,128)(2,1)S(1)}, bf16[64,384]{1,0:T(8,128)(2,1)S(1)}, u32[]{:S(2)}, u32[]{:S(2)}) collective-permute-start(bf16[64,384]{1,0:T(8,128)(2,1)S(1)} %get-tuple-element.233), channel_id=1, source_target_pairs={{0,3},{1,2},{2,1},{3,0},{4,7},{5,6},{6,5},{7,4},{8,11},{9,10},{10,... | collective-permute-start | bytes 147464 | tf_op jit(solution)/shard_map/ppermute | solution.py:449
  218.2 23.4 %collective-permute-start.42 = (bf16[8,144,384]{2,1,0:T(8,128)(2,1)}, bf16[8,144,384]{2,1,0:T(8,128)(2,1)}, u32[]{:S(2)}, u32[]{:S(2)}) collective-permute-start(bf16[8,144,384]{2,1,0:T(8,128)(2,1)} %get-tuple-element.329), channel_id=1, source_target_pairs={{0,4},{4,0},{8,12},{12,8},{16,20},{20,16},{24,28},{28,24},{1,5},{5... | collective-permute-start | bytes 2654216 | tf_op jit(solution)/shard_map/ppermute | solution.py:449
  221.5 131.1 %collective-permute-start.58 = (bf16[3,256,384]{2,1,0:T(8,128)(2,1)}, bf16[3,256,384]{2,1,0:T(8,128)(2,1)}, u32[]{:S(2)}, u32[]{:S(2)}) collective-permute-start(bf16[3,256,384]{2,1,0:T(8,128)(2,1)} %get-tuple-element.272.refs_7_), channel_id=1, source_target_pairs={{0,2},{1,3},{2,0},{3,1},{4,6},{5,7},{6,4},{7,5},{8,10},{9,11},{10,... | collective-permute-start | bytes 1769480 | tf_op jit(solution)/shard_map/ppermute | solution.py:449
  225.0 19.4 %collective-permute-start.46 = (bf16[2,192,384]{2,1,0:T(8,128)(2,1)}, bf16[2,192,384]{2,1,0:T(8,128)(2,1)}, u32[]{:S(2)}, u32[]{:S(2)}) collective-permute-start(bf16[2,192,384]{2,1,0:T(8,128)(2,1)} %get-tuple-element.340), channel_id=1, source_target_pairs={{0,8},{4,12},{8,0},{12,4},{16,24},{20,28},{24,16},{28,20},{1,9},{5... | collective-permute-start | bytes 884744 | tf_op jit(solution)/shard_map/ppermute | solution.py:449
  230.4 24.4 %collective-permute-start.43 = (bf16[3,64,384]{2,1,0:T(8,128)(2,1)}, bf16[3,64,384]{2,1,0:T(8,128)(2,1)}, u32[]{:S(2)}, u32[]{:S(2)}) collective-permute-start(bf16[3,64,384]{2,1,0:T(8,128)(2,1)} %get-tuple-element.249.refs_6_), channel_id=1, source_target_pairs={{0,1},{1,0},{2,3},{3,2},{4,5},{5,4},{6,7},{7,6},{8,9},{9,8},{10,11... | collective-permute-start | bytes 442376 | tf_op jit(solution)/shard_map/ppermute | solution.py:449
  230.5 25.3 %collective-permute-start.44 = (bf16[3,64,384]{2,1,0:T(8,128)(2,1)}, bf16[3,64,384]{2,1,0:T(8,128)(2,1)}, u32[]{:S(2)}, u32[]{:S(2)}) collective-permute-start(bf16[3,64,384]{2,1,0:T(8,128)(2,1)} %get-tuple-element.250.refs_7_), channel_id=1, source_target_pairs={{0,2},{1,3},{2,0},{3,1},{4,6},{5,7},{6,4},{7,5},{8,10},{9,11},{10,... | collective-permute-start | bytes 442376 | tf_op jit(solution)/shard_map/ppermute | solution.py:449
  244.4 12.7 %collective-permute-start.45 = (bf16[3,64,384]{2,1,0:T(8,128)(2,1)S(1)}, bf16[3,64,384]{2,1,0:T(8,128)(2,1)S(1)}, u32[]{:S(2)}, u32[]{:S(2)}) collective-permute-start(bf16[3,64,384]{2,1,0:T(8,128)(2,1)S(1)} %copy-done.51), channel_id=1, source_target_pairs={{0,3},{1,2},{2,1},{3,0},{4,7},{5,6},{6,5},{7,4},{8,11},{9,10},{10,... | collective-permute-start | bytes 442376 | tf_op jit(solution)/shard_map/ppermute | solution.py:449
  253.3 39.8 %collective-permute-start.49 = (bf16[8,240,384]{2,1,0:T(8,128)(2,1)S(1)}, bf16[8,240,384]{2,1,0:T(8,128)(2,1)S(1)}, u32[]{:S(2)}, u32[]{:S(2)}) collective-permute-start(bf16[8,240,384]{2,1,0:T(8,128)(2,1)S(1)} %copy-done.31), channel_id=1, source_target_pairs={{0,8},{4,12},{8,0},{12,4},{16,24},{20,28},{24,16},{28,20},{1,9},{5... | collective-permute-start | bytes 4423688 | tf_op jit(solution)/shard_map/ppermute | solution.py:449
  254.8 28.3 %collective-permute-start.48 = (bf16[8,208,384]{2,1,0:T(8,128)(2,1)S(1)}, bf16[8,208,384]{2,1,0:T(8,128)(2,1)S(1)}, u32[]{:S(2)}, u32[]{:S(2)}) collective-permute-start(bf16[8,208,384]{2,1,0:T(8,128)(2,1)S(1)} %copy-done.32), channel_id=1, source_target_pairs={{0,4},{4,0},{8,12},{12,8},{16,20},{20,16},{24,28},{28,24},{1,5},{5... | collective-permute-start | bytes 3833864 | tf_op jit(solution)/shard_map/ppermute | solution.py:449
  255.9 38.5 %collective-permute-start.50 = (bf16[4,144,384]{2,1,0:T(8,128)(2,1)S(1)}, bf16[4,144,384]{2,1,0:T(8,128)(2,1)S(1)}, u32[]{:S(2)}, u32[]{:S(2)}) collective-permute-start(bf16[4,144,384]{2,1,0:T(8,128)(2,1)S(1)} %get-tuple-element.326), channel_id=1, source_target_pairs={{0,2},{1,3},{2,0},{3,1},{4,6},{5,7},{6,4},{7,5},{8,10},{9,11},{10,... | collective-permute-start | bytes 1327112 | tf_op jit(solution)/shard_map/ppermute | solution.py:449
  257.1 38.6 %collective-permute-start.51 = (bf16[1,192,384]{2,1,0:T(8,128)(2,1)S(1)}, bf16[1,192,384]{2,1,0:T(8,128)(2,1)S(1)}, u32[]{:S(2)}, u32[]{:S(2)}) collective-permute-start(bf16[1,192,384]{2,1,0:T(8,128)(2,1)S(1)} %get-tuple-element.373), channel_id=1, source_target_pairs={{0,16},{4,20},{8,24},{12,28},{16,0},{20,4},{24,8},{28,12},{1,17},{... | collective-permute-start | bytes 442376 | tf_op jit(solution)/shard_map/ppermute | solution.py:449
  283.1 12.9 %collective-permute-start.52 = (bf16[1,240,384]{2,1,0:T(8,128)(2,1)S(1)}, bf16[1,240,384]{2,1,0:T(8,128)(2,1)S(1)}, u32[]{:S(2)}, u32[]{:S(2)}) collective-permute-start(bf16[1,240,384]{2,1,0:T(8,128)(2,1)S(1)} %get-tuple-element.364), channel_id=1, source_target_pairs={{0,16},{4,20},{8,24},{12,28},{16,0},{20,4},{24,8},{28,12},{1,17},{... | collective-permute-start | bytes 552968 | tf_op jit(solution)/shard_map/ppermute | solution.py:449
  293.1 22.6 %collective-permute-start.53 = (bf16[8,144,384]{2,1,0:T(8,128)(2,1)S(1)}, bf16[8,144,384]{2,1,0:T(8,128)(2,1)S(1)}, u32[]{:S(2)}, u32[]{:S(2)}) collective-permute-start(bf16[8,144,384]{2,1,0:T(8,128)(2,1)S(1)} %get-tuple-element.325), channel_id=1, source_target_pairs={{0,2},{1,3},{2,0},{3,1},{4,6},{5,7},{6,4},{7,5},{8,10},{9,11},{10,... | collective-permute-start | bytes 2654216 | tf_op jit(solution)/shard_map/ppermute | solution.py:449
  294.3 32.0 %collective-permute-start.55 = (bf16[4,208,384]{2,1,0:T(8,128)(2,1)S(1)}, bf16[4,208,384]{2,1,0:T(8,128)(2,1)S(1)}, u32[]{:S(2)}, u32[]{:S(2)}) collective-permute-start(bf16[4,208,384]{2,1,0:T(8,128)(2,1)S(1)} %get-tuple-element.309), channel_id=1, source_target_pairs={{0,2},{1,3},{2,0},{3,1},{4,6},{5,7},{6,4},{7,5},{8,10},{9,11},{10,... | collective-permute-start | bytes 1916936 | tf_op jit(solution)/shard_map/ppermute | solution.py:449
  295.7 21.4 %collective-permute-start.54 = (bf16[2,144,384]{2,1,0:T(8,128)(2,1)S(1)}, bf16[2,144,384]{2,1,0:T(8,128)(2,1)S(1)}, u32[]{:S(2)}, u32[]{:S(2)}) collective-permute-start(bf16[2,144,384]{2,1,0:T(8,128)(2,1)S(1)} %get-tuple-element.355), channel_id=1, source_target_pairs={{0,8},{4,12},{8,0},{12,4},{16,24},{20,28},{24,16},{28,20},{1,9},{5... | collective-permute-start | bytes 663560 | tf_op jit(solution)/shard_map/ppermute | solution.py:449
  296.0 30.7 %collective-permute-start.60 = (bf16[4,240,384]{2,1,0:T(8,128)(2,1)S(1)}, bf16[4,240,384]{2,1,0:T(8,128)(2,1)S(1)}, u32[]{:S(2)}, u32[]{:S(2)}) collective-permute-start(bf16[4,240,384]{2,1,0:T(8,128)(2,1)S(1)} %get-tuple-element.301), channel_id=1, source_target_pairs={{0,4},{4,0},{8,12},{12,8},{16,20},{20,16},{24,28},{28,24},{1,5},{5... | collective-permute-start | bytes 2211848 | tf_op jit(solution)/shard_map/ppermute | solution.py:449
  326.6 27.5 %collective-permute-start.59 = (bf16[3,256,384]{2,1,0:T(8,128)(2,1)S(1)}, bf16[3,256,384]{2,1,0:T(8,128)(2,1)S(1)}, u32[]{:S(2)}, u32[]{:S(2)}) collective-permute-start(bf16[3,256,384]{2,1,0:T(8,128)(2,1)S(1)} %copy-done.77), channel_id=1, source_target_pairs={{0,3},{1,2},{2,1},{3,0},{4,7},{5,6},{6,5},{7,4},{8,11},{9,10},{10,... | collective-permute-start | bytes 1769480 | tf_op jit(solution)/shard_map/ppermute | solution.py:449
  326.8 28.5 %collective-permute-start.57 = (bf16[3,256,384]{2,1,0:T(8,128)(2,1)S(1)}, bf16[3,256,384]{2,1,0:T(8,128)(2,1)S(1)}, u32[]{:S(2)}, u32[]{:S(2)}) collective-permute-start(bf16[3,256,384]{2,1,0:T(8,128)(2,1)S(1)} %copy-done.76), channel_id=1, source_target_pairs={{0,1},{1,0},{2,3},{3,2},{4,5},{5,4},{6,7},{7,6},{8,9},{9,8},{10,11... | collective-permute-start | bytes 1769480 | tf_op jit(solution)/shard_map/ppermute | solution.py:449
  327.8 22.5 %collective-permute-start.65 = (bf16[576,384]{1,0:T(8,128)(2,1)S(1)}, bf16[576,384]{1,0:T(8,128)(2,1)S(1)}, u32[]{:S(2)}, u32[]{:S(2)}) collective-permute-start(bf16[576,384]{1,0:T(8,128)(2,1)S(1)} %pad_maximum_fusion.8), channel_id=1, source_target_pairs={{0,2},{1,3},{2,0},{3,1},{4,6},{5,7},{6,4},{7,5},{8,10},{9,11},{10,... | collective-permute-start | bytes 1327112 | tf_op jit(solution)/shard_map/ppermute | solution.py:449
  335.0 29.4 %collective-permute-start.64 = (bf16[2,144,384]{2,1,0:T(8,128)(2,1)S(1)}, bf16[2,144,384]{2,1,0:T(8,128)(2,1)S(1)}, u32[]{:S(2)}, u32[]{:S(2)}) collective-permute-start(bf16[2,144,384]{2,1,0:T(8,128)(2,1)S(1)} %get-tuple-element.353), channel_id=1, source_target_pairs={{0,8},{4,12},{8,0},{12,4},{16,24},{20,28},{24,16},{28,20},{1,9},{5... | collective-permute-start | bytes 663560 | tf_op jit(solution)/shard_map/ppermute | solution.py:449
  350.2 12.3 %collective-permute-start.63 = (bf16[2,240,384]{2,1,0:T(8,128)(2,1)S(1)}, bf16[2,240,384]{2,1,0:T(8,128)(2,1)S(1)}, u32[]{:S(2)}, u32[]{:S(2)}) collective-permute-start(bf16[2,240,384]{2,1,0:T(8,128)(2,1)S(1)} %get-tuple-element.330), channel_id=1, source_target_pairs={{0,2},{1,3},{2,0},{3,1},{4,6},{5,7},{6,4},{7,5},{8,10},{9,11},{10,... | collective-permute-start | bytes 1105928 | tf_op jit(solution)/shard_map/ppermute | solution.py:449
  352.6 16.8 %collective-permute-start.67 = (bf16[1,208,384]{2,1,0:T(8,128)(2,1)S(1)}, bf16[1,208,384]{2,1,0:T(8,128)(2,1)S(1)}, u32[]{:S(2)}, u32[]{:S(2)}) collective-permute-start(bf16[1,208,384]{2,1,0:T(8,128)(2,1)S(1)} %get-tuple-element.366), channel_id=1, source_target_pairs={{0,16},{4,20},{8,24},{12,28},{16,0},{20,4},{24,8},{28,12},{1,17},{... | collective-permute-start | bytes 479240 | tf_op jit(solution)/shard_map/ppermute | solution.py:449
  362.6 14.6 %collective-permute-start.68 = (bf16[1,240,384]{2,1,0:T(8,128)(2,1)S(1)}, bf16[1,240,384]{2,1,0:T(8,128)(2,1)S(1)}, u32[]{:S(2)}, u32[]{:S(2)}) collective-permute-start(bf16[1,240,384]{2,1,0:T(8,128)(2,1)S(1)} %get-tuple-element.362), channel_id=1, source_target_pairs={{0,16},{4,20},{8,24},{12,28},{16,0},{20,4},{24,8},{28,12},{1,17},{... | collective-permute-start | bytes 552968 | tf_op jit(solution)/shard_map/ppermute | solution.py:449
  364.4 14.9 %collective-permute-start.69 = (bf16[1,144,384]{2,1,0:T(8,128)(2,1)S(1)}, bf16[1,144,384]{2,1,0:T(8,128)(2,1)S(1)}, u32[]{:S(2)}, u32[]{:S(2)}) collective-permute-start(bf16[1,144,384]{2,1,0:T(8,128)(2,1)S(1)} %get-tuple-element.381), channel_id=1, source_target_pairs={{0,16},{4,20},{8,24},{12,28},{16,0},{20,4},{24,8},{28,12},{1,17},{... | collective-permute-start | bytes 331784 | tf_op jit(solution)/shard_map/ppermute | solution.py:449
  379.4 12.2 %collective-permute-start.70 = (bf16[592,384]{1,0:T(8,128)(2,1)S(1)}, bf16[592,384]{1,0:T(8,128)(2,1)S(1)}, u32[]{:S(2)}, u32[]{:S(2)}) collective-permute-start(bf16[592,384]{1,0:T(8,128)(2,1)S(1)} %pad_maximum_fusion.7), channel_id=1, source_target_pairs={{0,2},{1,3},{2,0},{3,1},{4,6},{5,7},{6,4},{7,5},{8,10},{9,11},{10,... | collective-permute-start | bytes 1363976 | tf_op jit(solution)/shard_map/ppermute | solution.py:449
  391.9 12.5 %collective-permute-start.71 = (bf16[2,592,384]{2,1,0:T(8,128)(2,1)S(1)}, bf16[2,592,384]{2,1,0:T(8,128)(2,1)}, u32[]{:S(2)}, u32[]{:S(2)}) collective-permute-start(bf16[2,592,384]{2,1,0:T(8,128)(2,1)S(1)} %pad_maximum_fusion.3.refs_1_), channel_id=1, source_target_pairs={{0,1},{1,0},{2,3},{3,2},{4,5},{5,4},{6,7},{7,6},{8,9},{9,8},{10,11... | collective-permute-start | bytes 2727944 | tf_op jit(solution)/shard_map/ppermute | solution.py:449
  (127 other events, 850.1 us)

commit v3 on v2

--- a/solution.py
+++ b/solution.py
@@ -109,7 +109,7 @@
     else:
         chosen_ref, base, slot_in = refs[0], refs[1 : 1 + OWNERS], refs[1 + OWNERS : 1 + 2 * OWNERS]
         refs = refs[1 + 2 * OWNERS :]
-    outs, (merged, stats, mixed) = refs[:OWNERS], refs[OWNERS:]
+    outs, (merged, mixed, stats) = refs[:OWNERS], refs[OWNERS:]
     me = 2 * place[0] + place[1]
     blocks = OWNERS * rows // BLOCK
     for r in range(OWNERS):
@@ -143,15 +143,14 @@
             for found in scores[1:]:
                 top = jnp.maximum(top, found)
             top = jnp.max(top, axis=1, keepdims=True)
-            total = jnp.zeros((BLOCK, BLOCK), F32)
             part = jnp.zeros((BLOCK, LANES), F32)
             for b in range(a + 1):
-                weight = jnp.exp(scores[b] - top)
-                total = total + weight
-                values = only_head(merged[2, b * BLOCK : (b + 1) * BLOCK, :], head)
-                part = part + dot(weight.astype(BF16), values)
-            total = jnp.sum(total, axis=1, keepdims=True)
-            mixture = mixture + part * (1.0 / total)
+                weight = jnp.exp(scores[b] - top).astype(BF16)
+                values = merged[2, b * BLOCK : (b + 1) * BLOCK, :]
+                part = part + dot(weight, jnp.where(lane_head(head), values, jnp.ones_like(values)))
+            turned = pltpu.roll(part, HEAD_DIM, axis=1)
+            mixture = jnp.where(lane_head(head), part * (1.0 / turned), mixture)
+            total = turned if head == 0 else part
             lane = lax.broadcasted_iota(jnp.int32, (1, LANES), 1)
             stat = jnp.where(lane == head, top + jnp.log(total), stat)
         mixed[a * BLOCK : (a + 1) * BLOCK, :] = mixture.astype(BF16)
@@ -184,26 +183,27 @@
         out_shape=[jax.ShapeDtypeStruct((rows, half), BF16)] * OWNERS
         + [
             jax.ShapeDtypeStruct((3, length, half), BF16),
+            jax.ShapeDtypeStruct((length, half), BF16),
             jax.ShapeDtypeStruct((pairs, 8, length), F32),
         ],
         in_specs=specs,
         out_specs=[pl.BlockSpec((rows, LANES), lambda h: (0, h))] * OWNERS
         + [
             pl.BlockSpec((3, length, LANES), lambda h: (0, 0, h)),
+            pl.BlockSpec((length, LANES), lambda h: (0, h)),
             pl.BlockSpec((1, 8, length), lambda h: (h, 0, 0)),
         ],
-        scratch_shapes=[pltpu.VMEM((length, LANES), BF16)],
         compiler_params=pltpu.CompilerParams(vmem_limit_bytes=VMEM_BYTES),
         cost_estimate=cost(16 * HEAD_DIM * work, 16 * length * half, work),
     )(*inputs)
-    return outs[:OWNERS], outs[OWNERS], outs[OWNERS + 1]
+    return outs[:OWNERS], outs[OWNERS:]
 
 
 def attend_back_kernel(rows, routed, place, counts, *refs):
     if not routed:
         chosen_ref, refs = refs[0], refs[1:]
-    merged, stats, grads = refs[0], refs[1], refs[2 : 2 + OWNERS]
-    outs, refs = refs[2 + OWNERS : 2 + 2 * OWNERS], refs[2 + 2 * OWNERS :]
+    merged, mixed, stats, grads = refs[0], refs[1], refs[2], refs[3 : 3 + OWNERS]
+    outs, refs = refs[3 + OWNERS : 3 + 2 * OWNERS], refs[3 + 2 * OWNERS :]
     if not routed:
         slot_outs, refs = refs[:OWNERS], refs[OWNERS:]
     incoming, grad_q, grad_k, grad_v = refs
@@ -220,12 +220,14 @@
         queries = merged[0, span, :] * jnp.asarray(HEAD_DIM**-0.5, BF16)
         grad_mix = incoming[span, :]
         grad_query = jnp.zeros((BLOCK, LANES), F32)
+        inner = (grad_mix.astype(F32) * mixed[span, :].astype(F32)).T
         for head in range(2):
             own_q = only_head(queries, head)
             own_g = only_head(grad_mix, head)
             level = stats[0, head : head + 1, span]
-            probs, grad_probs = [], []
-            inner = jnp.zeros((1, BLOCK), F32)
+            offset = jnp.sum(
+                inner[head * HEAD_DIM : (head + 1) * HEAD_DIM], axis=0, keepdims=True
+            )
             for b in range(a + 1):
                 keys_at = slice(b * BLOCK, (b + 1) * BLOCK)
                 prob = jnp.exp(dot(merged[1, keys_at, :], own_q, NT) - level)
@@ -233,12 +235,7 @@
                     prob = jnp.where(visible, prob, 0.0)
                 grad_prob = dot(merged[2, keys_at, :], own_g, NT)
                 grad_v[keys_at, :] += dot(prob.astype(BF16), own_g)
-                inner = inner + jnp.sum(prob * grad_prob, axis=0, keepdims=True)
-                probs.append(prob)
-                grad_probs.append(grad_prob)
-            for b in range(a + 1):
-                keys_at = slice(b * BLOCK, (b + 1) * BLOCK)
-                grad_score = (probs[b] * (grad_probs[b] - inner)).astype(BF16)
+                grad_score = (prob * (grad_prob - offset)).astype(BF16)
                 grad_k[keys_at, :] += dot(grad_score, own_q)
                 own_k = only_head(merged[1, keys_at, :], head)
                 grad_query = grad_query + dot(grad_score, own_k, TN)
@@ -255,7 +252,7 @@
                 slot_outs[r][part] = dot(spots, found, TN).astype(BF16)
 
 
-def attend_back(place, counts, merged, stats, grads, chosen=None):
+def attend_back(place, counts, saved, grads, chosen=None):
     routed = chosen is None
     rows, half = grads[0].shape
     pairs = half // LANES
@@ -270,9 +267,10 @@
         slots = chosen.shape[1]
         shapes += [jax.ShapeDtypeStruct((3, slots, half), BF16)] * OWNERS
         out_specs += [pl.BlockSpec((3, slots, LANES), lambda h: (0, 0, h))] * OWNERS
-    inputs += [merged, stats] + list(grads)
+    inputs += list(saved) + list(grads)
     specs += [
         pl.BlockSpec((3, length, LANES), lambda h: (0, 0, h)),
+        pl.BlockSpec((length, LANES), lambda h: (0, h)),
         pl.BlockSpec((1, 8, length), lambda h: (h, 0, 0)),
     ] + [pl.BlockSpec((rows, LANES), lambda h: (0, h))] * OWNERS
     blocks = length // BLOCK
@@ -300,9 +298,11 @@
     dp = list(range(bits))
     rest = dp[2:]
     return (
+        [dp[0], dp[1]] + rest + [Y_STAGE],
+        [dp[1], dp[0]] + rest + [Y_STAGE],
+        [Y_STAGE, dp[0], dp[1]] + rest,
         [dp[0], Y_STAGE, dp[1]] + rest,
-        [dp[1], dp[0], Y_STAGE] + rest,
-        [Y_STAGE, dp[0], dp[1]] + rest,
+        [dp[1], Y_STAGE, dp[0]] + rest,
     )
 
 
@@ -476,13 +476,34 @@
 
 class Chain:
     def __init__(self, unit, order):
-        self.state, self.order, self.stage = halves(unit), order, 0
+        self.unit, self.order, self.stage = unit, order, 0
+        self.state = None, halves(unit)[1]
 
     def step(self, after):
-        keep, _ = hold(self.state[0], after)
+        if self.stage == 0:
+            unit, _ = hold(self.unit, after)
+            keep = halves(unit)[0]
+        else:
+            keep, _ = hold(self.state[0], after)
         self.state = combine(keep, stage_swap(self.state, self.order, self.stage))
         self.stage += 1
         return self.state
+
+
+def merge(chains):
+    found = Chain.__new__(Chain)
+    found.order, found.stage = chains[0].order, chains[0].stage
+    found.state = tuple(
+        jnp.concatenate([chain.state[k] for chain in chains], axis=1) for k in range(2)
+    )
+    return found
+
+
+def advance(chains, stage, token):
+    for chain in chains:
+        while chain.stage < min(stage, len(chain.order)):
+            token = chain.step(token)
+    return token
 
 
 def gather_halves(own, y_first):
@@ -558,18 +579,20 @@
     return done, (attended, middle, ff_in, hidden, activated)
 
 
-def feed_backward(grad_done, router, w_out, gain_two, w_up, w_down, kept):
-    attended, middle, ff_in, hidden, activated = kept
+def hidden_backward(grad_done, w_down, hidden):
     grad_ff = grad_done.astype(BF16)
     grad_act = project_back(grad_ff, w_down)
     unused_value, gelu_pull = jax.vjp(jax.nn.gelu, hidden)
-    grad_hidden = gelu_pull(grad_act)[0].astype(BF16)
+    return grad_ff, gelu_pull(grad_act)[0].astype(BF16)
+
+
+def feed_backward(grad_done, grad_hidden, router, w_out, gain_two, w_up, middle):
     grad_ffin = project_back(grad_hidden, w_up)
     grad_middle = grad_done + norm_back(middle, gain_two, grad_ffin)
     scaled = grad_middle if router is None else router[..., None] * grad_middle
     grad_attended = scaled.astype(BF16)
     grad_mixture = project_back(grad_attended, w_out).astype(BF16)
-    return grad_ff, grad_hidden, grad_middle, grad_attended, grad_mixture
+    return grad_middle, grad_attended, grad_mixture
 
 
 def norm_back(x, gain, grad_act_in):
@@ -633,7 +656,7 @@
     pieces = exchange(pieces)
     act_base, base = project_pieces(place, stream_in, gain_b1, qkv_b, tag)
     base_two = swap(base[2], "seq", 2)
-    mixed, merged_a, stats_a = attend(place, counts_mine, slots, pieces)
+    mixed, saved_a = attend(place, counts_mine, slots, pieces)
     mixed = exchange(mixed)
     mixed, late = hold(mixed, (base[1], base[3]))
     base = [base[0], swap(late[0], "seq", 1), base_two, swap(late[1], "seq", 3)]
@@ -641,7 +664,8 @@
     done_a, kept_a = feed_forward(picked, router, mixture_a, out_a, gain_a2, up_a, down_a)
     change = jnp.where(live[..., None], done_a - picked, 0.0)
     slot_mid = picked + change
-    base_three, slot_mid = hold(base[3], slot_mid)
+    early_a = [with_far(flat(x)) for x in (kept_a[2], kept_a[4], mixture_a)]
+    base_three, early_a, slot_mid = hold(base[3], early_a, slot_mid)
     base = base[:3] + [base_three]
     act_slot, slot_pieces = project_pieces(place, slot_mid, gain_b1, qkv_b)
     slot_pieces = exchange(slot_pieces)
@@ -659,7 +683,7 @@
     middle = stream_in.astype(F32) + scatter(change)
     slot_pieces, acts_near, acts_far, middle = hold(slot_pieces, acts_near, acts_far, middle)
     acts_pair = jnp.stack([acts_near, swap(acts_far, "seq", 2)])
-    mixed, merged_b, stats_b = attend(
+    mixed, saved_b = attend(
         place, counts_mine, rows, base, chosen_mine, slot_pieces
     )
     acts_other = swap(acts_pair, "seq", 1)
@@ -669,12 +693,13 @@
     mixture_b = assemble(exchange(mixed), y_first, core_first)
     done_b, kept_b = feed_forward(middle, None, mixture_b, out_b, gain_b2, up_b, down_b)
 
-    x_first, z_first, y_first_order = orders
     flat_b = [flat(x) for x in (kept_b[2], kept_b[4], mixture_b)]
     early = [with_far(x) for x in flat_b]
     early_grad = half_with_far(flat(cotangent), core_at)
-    grad_ff_b, grad_hidden_b, grad_mid_b, grad_att_b, grad_mix_b = feed_backward(
-        cotangent.astype(F32), None, out_b, gain_b2, up_b, down_b, kept_b
+    grad_done_b = cotangent.astype(F32)
+    grad_ff_b, grad_hidden_b = hidden_backward(grad_done_b, down_b, kept_b[3])
+    grad_mid_b, grad_att_b, grad_mix_b = feed_backward(
+        grad_done_b, grad_hidden_b, None, out_b, gain_b2, up_b, kept_b[1]
     )
     grads = split_pieces(grad_mix_b, place)
     late = [half_with_far(flat(x), core_at) for x in (grad_hidden_b, grad_att_b)]
@@ -683,92 +708,80 @@
     operands = [y for x in early + [late[0], early_grad, late[1]] for y in x]
     feed_b = feed_grad(place, bits, (0, 1), operands)
     grads, feed_b = hold(grads, feed_b)
-    up_chain, down_chain = Chain(feed_b[0], x_first), Chain(feed_b[1], z_first)
-    packed_b, packed_slot = attend_back(place, counts_mine, merged_b, stats_b, grads, chosen_mine)
+    chains_b = [Chain(unit, send_orders(bits)[k]) for k, unit in enumerate(feed_b)]
+    packed_b, packed_slot = attend_back(place, counts_mine, saved_b, grads, chosen_mine)
     packed_slot = exchange(packed_slot)
-    part_b = qkv_grad(place, bits, 0, acts_b, packed_b)
-    token = up_chain.step(part_b)
-    token = down_chain.step(token)
+    part_b = qkv_grad(place, bits, 3, acts_b, packed_b)
+    token = advance(chains_b, 1, part_b)
     packed_slot, part_b, packed_b, token = hold(packed_slot, part_b, packed_b, token)
-    part_chain = Chain(part_b, x_first)
-    packed_b_two = swap(packed_b[2], "seq", 2)
+    feed_chains_b, part_chain_b = chains_b, Chain(part_b, send_orders(bits)[3])
+    packed_two = swap(packed_b[2], "seq", 2)
 
     grad_packed_slot = assemble_packed(packed_slot, y_first, core_first)
     slot_grad = norm_back(slot_mid, gain_b1, project_back(grad_packed_slot, qkv_b))
     mid_at_slot = jnp.einsum("bcr,brd->bcd", live_hits, grad_mid_b, precision=EXACT)
     grad_done = jnp.where(live[..., None], mid_at_slot + slot_grad, 0.0)
-    early = [with_far(flat(x)) for x in (kept_a[2], kept_a[4], mixture_a)]
-    grad_ff_a, grad_hidden_a, grad_mid_a, grad_att_a, grad_mix_a = feed_backward(
-        grad_done, router, out_a, gain_a2, up_a, down_a, kept_a
+    grad_ff_a, grad_hidden_a = hidden_backward(grad_done, down_a, kept_a[3])
+    token = advance(feed_chains_b, 2, (token, grad_hidden_a))
+    grad_hidden_a, token = hold(grad_hidden_a, token)
+    feed_chain_b = merge(feed_chains_b)
+    grad_mid_a, grad_att_a, grad_mix_a = feed_backward(
+        grad_done, grad_hidden_a, router, out_a, gain_a2, up_a, kept_a[1]
     )
     grads = split_pieces(grad_mix_a, place)
     late = [
         half_with_far(flat(x), core_at) for x in (grad_hidden_a, grad_ff_a, grad_att_a)
     ]
-    grads, early = hold(grads, early)
+    grads, packed_two, token = hold(grads, packed_two, token)
     grads = exchange(grads)
     grad_router = jnp.sum(kept_a[0] * grad_mid_a, axis=-1)
     grad_route = jnp.einsum("bc,bcd->d", grad_router, picked, precision=EXACT)
     route = jnp.pad(
         grad_route.reshape(dp_size, 1, narrow), ((0, 0), (0, SPARE - 1), (0, half - narrow))
     )
-    operands = [y for x in early + late for y in x]
-    feed_a = feed_grad(place, bits, (0, 1), operands, route)
-    token = up_chain.step(feed_a)
-    token = down_chain.step(token)
-    grads, feed_a, token = hold(grads, feed_a, token)
-    up_chain_a, down_chain_a = Chain(feed_a[0], x_first), Chain(feed_a[1], z_first)
-    packed_a, _ = attend_back(place, counts_mine, merged_a, stats_a, grads)
+    operands = [y for x in early_a + late for y in x]
+    feed_a = feed_grad(place, bits, (3, 2), operands, route)
+    token = advance([part_chain_b], 1, (token, feed_a))
+    grads, feed_a, late, token = hold(grads, feed_a, (packed_b[1], packed_b[3]), token)
+    packed_three = swap(late[1], "seq", 3)
+    up_chain_a = Chain(feed_a[0], send_orders(bits)[3])
+    packed_a, _ = attend_back(place, counts_mine, saved_a, grads)
     returned_a = exchange(packed_a)
-    part_a = qkv_grad(place, bits, 2, acts_a, packed_a)
-    token = part_chain.step(part_a)
-    token = up_chain.step(token)
-    token = down_chain.step(token)
-    returned_a, part_a, token = hold(returned_a, part_a, token)
-    part_chain_a = Chain(part_a, y_first_order)
+    part_a = qkv_grad(place, bits, 4, acts_a, packed_a)
+    returned_a, part_a, down_a_unit, packed_three, token = hold(
+        returned_a, part_a, feed_a[1], packed_three, token
+    )
+    returned_b = [packed_b[0], swap(late[0], "seq", 1), packed_two, packed_three]
+    down_chain_a = Chain(down_a_unit, send_orders(bits)[2])
+    part_chain_a = Chain(part_a, send_orders(bits)[4])
+    chains_a = [up_chain_a, down_chain_a, part_chain_a]
 
     grad_packed_a = assemble_packed(returned_a, y_first, core_first)
     res_a = norm_back(picked, gain_a1, project_back(grad_packed_a, qkv_a))
     grad_picked = (
         grad_mid_a + res_a + grad_router[..., None] * route_w.astype(F32) - grad_done
     )
-    token = up_chain_a.step((token, grad_picked))
-    token = down_chain_a.step(token)
-    token = part_chain.step(token)
-    token = up_chain.step(token)
-    token = down_chain.step(token)
-    token = part_chain_a.step(token)
-    token = part_chain.step(token)
-    for chain in (up_chain, down_chain):
-        while chain.stage < len(chain.order):
-            token = chain.step(token)
-    token = up_chain_a.step(token)
-    while part_chain.stage < len(part_chain.order):
-        token = part_chain.step(token)
-    late, token = hold((packed_b[1], packed_b[3]), token)
-    returned_b = [packed_b[0], swap(late[0], "seq", 1), packed_b_two, swap(late[1], "seq", 3)]
-    token = down_chain_a.step(token)
-    token = part_chain_a.step(token)
+    token = advance([up_chain_a], 1, (token, grad_picked))
+    token = advance([feed_chain_b], bits, token)
+    token = advance([part_chain_b], 2, token)
+    token = advance([down_chain_a, part_chain_a], 1, token)
+    done_b, returned_b, token = hold(done_b, returned_b, token)
+    token = advance(chains_a, 2, token)
+    token = advance([feed_chain_b], bits + 1, token)
+    token = advance([part_chain_b], 3, token)
+    token = advance(chains_a, 3, token)
+    token = advance([part_chain_b], bits + 1, token)
     near_b, far_b = gather_halves(
-        jnp.concatenate([up_chain.state, down_chain.state, part_chain.state]), y_first
-    )
-    token = up_chain_a.step(token)
-    token = down_chain_a.step(token)
-    token = part_chain_a.step(token)
-    for chain in (up_chain_a, down_chain_a, part_chain_a):
-        while chain.stage < len(chain.order) - 1:
-            token = chain.step(token)
+        jnp.concatenate([feed_chain_b.state, part_chain_b.state]), y_first
+    )
+    token = advance(chains_a, bits, token)
 
     grad_packed_b = assemble_packed(returned_b, y_first, core_first)
     res_b = norm_back(middle, gain_b1, project_back(grad_packed_b, qkv_b))
     grad_input = grad_mid_b + res_b + scatter(grad_picked)
     qkv_gb, out_gb, up_gb, down_gb = finish(place, OWNERS * narrow, narrow, width, near_b, far_b)
-    token = (token, qkv_gb, grad_input)
-    for chain in (up_chain_a, down_chain_a, part_chain_a):
-        token = chain.step(token)
-    near, far = gather_halves(
-        jnp.concatenate([up_chain_a.state, down_chain_a.state, part_chain_a.state]), y_first
-    )
+    token = advance(chains_a, bits + 1, token)
+    near, far = gather_halves(jnp.concatenate([x.state for x in chains_a]), y_first)
     down_at = OWNERS * narrow + SPARE
     qkv_ga, out_ga, up_ga, down_ga = finish(place, down_at, narrow, width, near, far)
     at = OWNERS * narrow // 2

time: 420 us -> 395 us (0.940)
  waiting for transfers between devices: 111 us -> 102 us
  matrix products: 61.2 us -> 53.8 us
  other arithmetic: 42.8 us -> 37.5 us
    ppermute x72 -> x70, waiting for transfers between devices: 111 us -> 102 us  [swap(): return lax.ppermute(x, axis, [(i, i ^ bit) for i in range(size)])]
    ppermute x72 -> x70, starting transfers between devices: 61.6 us -> 57.7 us  [swap(): return lax.ppermute(x, axis, [(i, i ^ bit) for i in range(size)])]
    convert_element_type x18 -> x17, other arithmetic: 14.6 us -> 11.6 us  [add_low(): return (a.astype(F32) + b.astype(F32)).astype(BF16)]
    unnamed x207 -> x227, local copies, waits for them, and re-layouts: 11.7 us -> 10.7 us
  transfers between devices with their start and end apart: 72 -> 70, of which waited for: 17 -> 19; matrix products, arithmetic and copies ran while one was open for 29% -> 28% of each run, Pallas kernels for 18% -> 19%
where the time goes in v3:
time: 395 us; the launch traced here: 390 us
  waiting for transfers between devices  102 us (26%)
  Pallas kernels  98 us (25%)
  starting transfers between devices  57.7 us (15%)
  matrix products  53.8 us (14%)
  local copies, waits for them, and re-layouts  37.7 us (10%)
  other arithmetic  37.5 us (9%)
    ppermute x70, waiting for transfers between devices, swap(): return lax.ppermute(x, axis, [(i, i ^ bit) for i in range(size)])  102 us
    ppermute x70, starting transfers between devices, swap(): return lax.ppermute(x, axis, [(i, i ^ bit) for i in range(size)])  57.7 us
    pallas_call x2, Pallas kernels, attend_back(): pl.pallas_call(lambda *refs: attend_back_kernel(rows, routed, *refs), nam...  25.5 us
    dot_general x6, matrix products, project(): jnp.einsum('bnd,de->bne', left_side, weight, preferred_element_type=F32)  24.2 us
    pallas_call x2, Pallas kernels, feed_grad(): pl.pallas_call(lambda *refs: feed_grad_kernel(bits, orders, routed, *refs...  22.4 us
    dot_general x9, matrix products, project_back(): jnp.einsum('bne,de->bnd', gradient, weight, preferred_element_type=F32)  20.9 us
    pallas_call x2, Pallas kernels, attend(): pl.pallas_call(lambda *refs: attend_kernel(rows, routed, *refs), name='at...  17.3 us
    pallas_call x3, Pallas kernels, project_pieces(): pl.pallas_call(lambda *refs: project_kernel(tagged, *refs), name='project...  15.2 us
  transfers between devices with their start and end apart: 70, of which 19 were waited for; matrix products, arithmetic and copies ran while one was open for 28% of the time, Pallas kernels for 19%

profile of v3, /device:TPU:0, one launch (start us, length us, event | category | flops | bytes accessed | tf_op | source)
XLA Modules:
  0.0 389.6 jit_solution(14405316842369187526)
XLA Ops:
  0.7 2.2 fusion.155
  3.6 4.2 %project_pieces.3 = (bf16[2,64,768]{2,1,0:T(8,128)(2,1)}, bf16[3,64,384]{2,1,0:T(8,128)(2,1)}, bf16[3,64,384]{2,1,0:T(8,128)(2,1)}, bf16[3,64,384]{2,1,0:T(8,128)(2,1)}, bf16[3,64,384]{2,1,0:T(8,128)(2,1)}) custom-call(s32[7]{0:T(128)} %stack.83.refs_0_, bf16[2,64,768]{2,1,0:T(8,128)(2,1)} %get-tuple-element.416.refs_1_, bf16[768]{0:T(1024)(128)(2,1)} %refs_2_.3, ...), custom_call_target="tpu_custom_call" | custom-call | flops 452984832 | bytes 4718592 | tf_op jit(solution)/shard_map/project_pieces/pallas_call | solution.py:59
  8.3 2.5 collective-permute-start.1
  11.6 6.8 %project_pieces.4 = (bf16[2,256,768]{2,1,0:T(8,128)(2,1)}, bf16[3,272,384]{2,1,0:T(8,128)(2,1)}, bf16[3,272,384]{2,1,0:T(8,128)(2,1)}, bf16[3,272,384]{2,1,0:T(8,128)(2,1)}, bf16[3,272,384]{2,1,0:T(8,128)(2,1)}) custom-call(s32[7]{0:T(128)} %stack.83.refs_0_, bf16[2,256,768]{2,1,0:T(8,128)(2,1)} %refs_1_.1, bf16[768]{0:T(1024)(128)(2,1)} %refs_2_.5, ...), custom_call_target="tpu_custom_call" | custom-call | flops 1811939328 | bytes 8257536 | tf_op jit(solution)/shard_map/project_pieces/pallas_call | solution.py:59
  18.3 1.8 collective-permute-start.14
  23.1 4.5 %attend_routed.1 = (bf16[64,384]{1,0:T(8,128)(2,1)}, bf16[64,384]{1,0:T(8,128)(2,1)}, bf16[64,384]{1,0:T(8,128)(2,1)}, bf16[64,384]{1,0:T(8,128)(2,1)}, bf16[3,2...) custom-call(s32[7]{0:T(128)} %stack.83.refs_0_, s32[4]{0:T(128)} %fusion.146.refs_1_, ...), custom_call_target="tpu_custom_call" | custom-call | flops 402653184 | bytes 1572864 | tf_op jit(solution)/shard_map/attend_routed/pallas_call | solution.py:179
  29.6 6.9 %collective-permute-done.4 = bf16[64,384]{1,0:T(8,128)(2,1)S(1)} collective-permute-done((bf16[64,384]{1,0:T(8,128)(2,1)}, bf16[64,384]{1,0:T(8,128)(2,1)S(1)}, u32[]{:S(2)}, u32[]{:S(2)}) %collective-permute-start.4) | collective-permute-done | bytes 49184 | tf_op jit(solution)/shard_map/ppermute | solution.py:449
  40.6 4.8 %multiply_convert_fusion.2 = (bf16[2,64,3072]{2,1,0:T(8,128)(2,1)S(1)}, f32[2,64,3072]{2,1,0:T(8,128)}) fusion(bf16[2,64,768]{2,1,0:T(8,128)(2,1)S(1)} %multiply_convert_fusion.4, bf16[768,3072]{1,0:T(8,128)(2,1)} %param.25), kind=kOutput, calls=%fused_computation.62 | convolution fusion | flops 607518720 | bytes 7274496 | tf_op jit(solution)/shard_map/bnd,de->bne/dot_general | solution.py:565
  50.3 2.4 collective-permute-done.6.refs_6_
  54.4 4.2 %project_pieces.5 = (bf16[2,64,768]{2,1,0:T(8,128)(2,1)}, bf16[3,64,384]{2,1,0:T(8,128)(2,1)}, bf16[3,64,384]{2,1,0:T(8,128)(2,1)}, bf16[3,64,384]{2,1,0:T(8,128)(2,1)}, bf16[3,64,384]{2,1,0:T(8,128)(2,1)}) custom-call(s32[7]{0:T(128)} %stack.83.refs_0_, f32[2,64,768]{2,1,0:T(8,128)} %get-tuple-element.176.refs_1_, bf16[768]{0:T(1024)(128)(2,1)} %refs_2_.5, ...), custom_call_target="tpu_custom_call" | custom-call | flops 452984832 | bytes 4718592 | tf_op jit(solution)/shard_map/project_pieces/pallas_call | solution.py:59
  65.8 1.8 collective-permute-done.12.refs_10_
  68.3 12.9 %attend_dense.1 = (bf16[256,384]{1,0:T(8,128)(2,1)}, bf16[256,384]{1,0:T(8,128)(2,1)}, bf16[256,384]{1,0:T(8,128)(2,1)}, bf16[256,384]{1,0:T(8,128)(2,1)}, bf16[...) custom-call(s32[7]{0:T(128)} %stack.83.refs_0_, s32[4]{0:T(128)} %fusion.146.refs_1_, ...), custom_call_target="tpu_custom_call" | custom-call | flops 4026531840 | bytes 6291456 | tf_op jit(solution)/shard_map/attend_dense/pallas_call | solution.py:179
  90.4 2.3 collective-permute-done.17
  95.1 9.8 %multiply_convert_fusion = (bf16[2,256,3072]{2,1,0:T(8,128)(2,1)S(1)}, f32[2,256,3072]{2,1,0:T(8,128)}) fusion(bf16[2,256,768]{2,1,0:T(8,128)(2,1)S(1)} %multiply_convert_fusion.1, bf16[768,3072]{1,0:T(8,128)(2,1)} %param.31), kind=kOutput, calls=%fused_computation.9 | convolution fusion | flops 2430074880 | bytes 14942208 | tf_op jit(solution)/shard_map/bnd,de->bne/dot_general | solution.py:565
  105.6 8.2 %fusion.6 = bf16[2,256,3072]{2,1,0:T(8,128)(2,1)S(1)} fusion(f32[2,256,3072]{2,1,0:T(8,128)} %get-tuple-element.426, bf16[2,256,768]{2,1,0:T(8,128)(2,1)S(1)} %copy-done.30, bf16[3072,768]{1,0:T(8,128)(2,1)S(1)} %bitcast.298), kind=kOutput, calls=%fused_computation.8 | convolution fusion | flops 2447376384 | bytes 14942208 | tf_op jit(solution)/shard_map/bne,de->bnd/dot_general | solution.py:569
  115.5 2.7 multiply_reduce_fusion.2
  128.3 15.3 %feed_grad.2 = (bf16[16,192,384]{2,1,0:T(8,128)(2,1)}, bf16[16,240,384]{2,1,0:T(8,128)(2,1)}) custom-call(s32[7]{0:T(128)} %stack.83.refs_0_, bf16[512,768]{1,0:T(8,128)(2,1)} %bitcast.285, bf16[512,768]{1,0:T(8,128)(2,1)} %copy-done.78, bf16[512,3072]{1,0:T(8,128)(2,1)} %bitcast.300, bf16[512,3072]{1,0:T(8,128)(2,1)} %copy-done.76, ...), custom_call_target="tpu_custom_call" | custom-call | flops 5435817984 | bytes 21037056 | tf_op jit(solution)/shard_map/feed_grad/pallas_call | solution.py:369
  143.7 2.9 slice.343
  149.9 2.0 slice_bitcast_fusion
  152.0 21.2 %attend_dense_back.1 = (bf16[3,256,384]{2,1,0:T(8,128)(2,1)}, bf16[3,256,384]{2,1,0:T(8,128)(2,1)}, bf16[3,256,384]{2,1,0:T(8,128)(2,1)}, bf16[3,256,384]{2,1,0:...) custom-call(s32[7]{0:T(128)} %stack.83.refs_0_, ...), custom_call_target="tpu_custom_call" | custom-call | flops 10066329600 | bytes 6291456 | tf_op jit(solution)/shard_map/attend_dense_back/pallas_call | solution.py:278
  175.1 6.0 %qkv_grad.2 = bf16[16,144,384]{2,1,0:T(8,128)(2,1)} custom-call(s32[7]{0:T(128)} %stack.83.refs_0_, bf16[256,768]{1,0:T(8,128)(2,1)} %slice.331.refs_1_, bf16[256,768]{1,0:T(8,128)(2,1)} %get-tuple-element.353.refs_2_, bf16[256,768]{1,0:T(8,128)(2,1)} %slice.431.refs_3_, bf16[256,768]{1,0:T(8,128)(2,1)} %get-tuple-element.352.refs_4_, ...), custom_call_target="tpu_custom_call" | custom-call | flops 1811939328 | bytes 5701632 | tf_op jit(solution)/shard_map/qkv_grad/pallas_call | solution.py:397
  181.1 2.0 add_convert_fusion.6
  183.6 1.9 add_convert_fusion.2
  191.3 1.9 fusion.42
  197.0 1.8 collective-permute-done.34
  199.7 5.2 %collective-permute-done.35 = bf16[4,240,384]{2,1,0:T(8,128)(2,1)S(1)} collective-permute-done((bf16[4,240,384]{2,1,0:T(8,128)(2,1)S(1)}, bf16[4,240,384]{2,1,0:T(8,128)(2,1)S(1)}, u32[]{:S(2)}, u32[]{:S(2)}) %collective-permute-start.35) | collective-permute-done | bytes 737312 | tf_op jit(solution)/shard_map/ppermute | solution.py:449
  214.0 7.1 %feed_grad.3 = (bf16[16,208,384]{2,1,0:T(8,128)(2,1)}, bf16[16,240,384]{2,1,0:T(8,128)(2,1)}) custom-call(s32[7]{0:T(128)} %stack.83.refs_0_, bf16[128,768]{1,0:T(8,128)(2,1)} %bitcast.291, bf16[128,768]{1,0:T(8,128)(2,1)} %copy-done.87, bf16[128,3072]{1,0:T(8,128)(2,1)} %bitcast.279, bf16[128,3072]{1,0:T(8,128)(2,1)} %copy-done.77, ...), custom_call_target="tpu_custom_call" | custom-call | flops 1358954496 | bytes 9240576 | tf_op jit(solution)/shard_map/feed_grad/pallas_call | solution.py:369
  221.1 2.2 collective-permute-done.43
  223.3 2.5 add_convert_fusion.10
  230.9 4.3 %attend_routed_back.1 = (bf16[3,64,384]{2,1,0:T(8,128)(2,1)}, bf16[3,64,384]{2,1,0:T(8,128)(2,1)}, bf16[3,64,384]{2,1,0:T(8,128)(2,1)}, bf16[3,64,384]{2,1,0:T(8,128)(2,1)}) custom-call(s32[7]{0:T(128)} %stack.83.refs_0_, s32[4]{0:T(128)} %fusion.146.refs_1_, bf16[3,256,384]{2,1,0:T(8,128)(2,1)} %get-tuple-element.257.refs_2_, ...), custom_call_target="tpu_custom_call" | custom-call | flops 1006632960 | bytes 1572864 | tf_op jit(solution)/shard_map/attend_routed_back/pallas_call | solution.py:278
  237.8 2.7 collective-permute-start.50
  240.5 2.5 slice.373
  243.0 4.6 %qkv_grad.3 = bf16[16,144,384]{2,1,0:T(8,128)(2,1)} custom-call(s32[7]{0:T(128)} %stack.83.refs_0_, bf16[64,768]{1,0:T(8,128)(2,1)} %slice.363.refs_1_, bf16[64,768]{1,0:T(8,128)(2,1)} %get-tuple-element.351.refs_2_, bf16[64,768]{1,0:T(8,128)(2,1)} %slice.448.refs_3_, bf16[64,768]{1,0:T(8,128)(2,1)} %get-tuple-element.350.refs_4_, ...), custom_call_target="tpu_custom_call" | custom-call | flops 452984832 | bytes 2752512 | tf_op jit(solution)/shard_map/qkv_grad/pallas_call | solution.py:397
  255.5 23.5 %collective-permute-done.49 = bf16[8,208,384]{2,1,0:T(8,128)(2,1)S(1)} collective-permute-done((bf16[8,208,384]{2,1,0:T(8,128)(2,1)}, bf16[8,208,384]{2,1,0:T(8,128)(2,1)S(1)}, u32[]{:S(2)}, u32[]{:S(2)}) %collective-permute-start.49) | collective-permute-done | bytes 1277984 | tf_op jit(solution)/shard_map/ppermute | solution.py:449
  280.5 6.0 %fusion.51 = bf16[2,256,768]{2,1,0:T(8,128)(2,1)} fusion(f32[2,256,768]{2,1,0:T(8,128)S(1)} %copy-done.5, bf16[2,256,3072]{2,1,0:T(8,128)(2,1)S(1)} %copy-done.75, bf16[3072,768]{1,0:T(8,128)(2,1)} %param.32), kind=kOutput, calls=%fused_computation.69 | convolution fusion | flops 2416705536 | bytes 10223616 | tf_op jit(solution)/shard_map/bnd,de->bne/dot_general | solution.py:565
  290.3 15.4 %collective-permute-done.54 = bf16[4,208,384]{2,1,0:T(8,128)(2,1)S(1)} collective-permute-done((bf16[4,208,384]{2,1,0:T(8,128)(2,1)S(1)}, bf16[4,208,384]{2,1,0:T(8,128)(2,1)S(1)}, u32[]{:S(2)}, u32[]{:S(2)}) %collective-permute-start.54) | collective-permute-done | bytes 639008 | tf_op jit(solution)/shard_map/ppermute | solution.py:449
  314.9 2.1 multiply_reduce_fusion.1
  317.0 10.0 %collective-permute-done.55 = bf16[4,240,384]{2,1,0:T(8,128)(2,1)S(1)} collective-permute-done((bf16[4,240,384]{2,1,0:T(8,128)(2,1)S(1)}, bf16[4,240,384]{2,1,0:T(8,128)(2,1)S(1)}, u32[]{:S(2)}, u32[]{:S(2)}) %collective-permute-start.55) | collective-permute-done | bytes 737312 | tf_op jit(solution)/shard_map/ppermute | solution.py:449
  329.9 2.6 collective-permute-start.63
  332.6 8.6 %collective-permute-done.60 = bf16[2,240,384]{2,1,0:T(8,128)(2,1)S(1)} collective-permute-done((bf16[2,240,384]{2,1,0:T(8,128)(2,1)S(1)}, bf16[2,240,384]{2,1,0:T(8,128)(2,1)S(1)}, u32[]{:S(2)}, u32[]{:S(2)}) %collective-permute-start.60) | collective-permute-done | bytes 368672 | tf_op jit(solution)/shard_map/ppermute | solution.py:449
  341.4 3.0 collective-permute-start.65
  344.4 4.8 %collective-permute-done.63 = bf16[1,208,384]{2,1,0:T(8,128)(2,1)S(1)} collective-permute-done((bf16[1,208,384]{2,1,0:T(8,128)(2,1)S(1)}, bf16[1,208,384]{2,1,0:T(8,128)(2,1)S(1)}, u32[]{:S(2)}, u32[]{:S(2)}) %collective-permute-start.63) | collective-permute-done | bytes 159776 | tf_op jit(solution)/shard_map/ppermute | solution.py:449
  350.3 2.9 collective-permute-done.64
  353.2 1.9 collective-permute-done.65
  358.4 9.0 %collective-permute-done.66 = bf16[592,384]{1,0:T(8,128)(2,1)S(1)} collective-permute-done((bf16[592,384]{1,0:T(8,128)(2,1)S(1)}, bf16[592,384]{1,0:T(8,128)(2,1)S(1)}, u32[]{:S(2)}, u32[]{:S(2)}) %collective-permute-start.66) | collective-permute-done | bytes 454688 | tf_op jit(solution)/shard_map/ppermute | solution.py:449
  368.4 2.5 fusion.45
  370.8 3.4 finish_grads.3
  379.8 3.5 finish_grads.2
  (474 shorter events, 123.6 us)
Async XLA Ops:
  7.8 14.5 %collective-permute-start = (bf16[3,64,384]{2,1,0:T(8,128)(2,1)}, bf16[3,64,384]{2,1,0:T(8,128)(2,1)S(1)}, u32[]{:S(2)}, u32[]{:S(2)}) collective-permute-start(bf16[3,64,384]{2,1,0:T(8,128)(2,1)} %get-tuple-element.162), channel_id=1, source_target_pairs={{0,1},{1,0},{2,3},{3,2},{4,5},{5,4},{6,7},{7,6},{8,9},{9,8},{10,11... | collective-permute-start | bytes 442376 | tf_op jit(solution)/shard_map/ppermute | solution.py:449
  8.3 14.1 %collective-permute-start.1 = (bf16[3,64,384]{2,1,0:T(8,128)(2,1)}, bf16[3,64,384]{2,1,0:T(8,128)(2,1)S(1)}, u32[]{:S(2)}, u32[]{:S(2)}) collective-permute-start(bf16[3,64,384]{2,1,0:T(8,128)(2,1)} %get-tuple-element.163), channel_id=1, source_target_pairs={{0,2},{1,3},{2,0},{3,1},{4,6},{5,7},{6,4},{7,5},{8,10},{9,11},{10,... | collective-permute-start | bytes 442376 | tf_op jit(solution)/shard_map/ppermute | solution.py:449
  18.3 30.4 %collective-permute-start.14 = (bf16[3,272,384]{2,1,0:T(8,128)(2,1)}, bf16[3,272,384]{2,1,0:T(8,128)(2,1)}, u32[]{:S(2)}, u32[]{:S(2)}) collective-permute-start(bf16[3,272,384]{2,1,0:T(8,128)(2,1)} %get-tuple-element.187), channel_id=1, source_target_pairs={{0,2},{1,3},{2,0},{3,1},{4,6},{5,7},{6,4},{7,5},{8,10},{9,11},{10,... | collective-permute-start | bytes 1880072 | tf_op jit(solution)/shard_map/ppermute | solution.py:449
  36.5 16.2 %collective-permute-start.6 = (bf16[3,272,384]{2,1,0:T(8,128)(2,1)}, bf16[3,272,384]{2,1,0:T(8,128)(2,1)S(1)}, u32[]{:S(2)}, u32[]{:S(2)}) collective-permute-start(bf16[3,272,384]{2,1,0:T(8,128)(2,1)} %get-tuple-element.171), channel_id=1, source_target_pairs={{0,3},{1,2},{2,1},{3,0},{4,7},{5,6},{6,5},{7,4},{8,11},{9,10},{10,... | collective-permute-start | bytes 1880072 | tf_op jit(solution)/shard_map/ppermute | solution.py:449
  88.7 32.1 %collective-permute-start.30 = (bf16[320,768]{1,0:T(8,128)(2,1)S(1)}, bf16[320,768]{1,0:T(8,128)(2,1)S(1)}, u32[]{:S(2)}, u32[]{:S(2)}) collective-permute-start(bf16[320,768]{1,0:T(8,128)(2,1)S(1)} %copy-done.50), channel_id=1, source_target_pairs={{0,2},{1,3},{2,0},{3,1},{4,6},{5,7},{6,4},{7,5},{8,10},{9,11},{10,... | collective-permute-start | bytes 1474568 | tf_op jit(solution)/shard_map/ppermute | solution.py:449
  104.9 20.8 %collective-permute-start.19 = (bf16[512,3072]{1,0:T(8,128)(2,1)S(1)}, bf16[512,3072]{1,0:T(8,128)(2,1)S(1)}, u32[]{:S(2)}, u32[]{:S(2)}) collective-permute-start(bf16[512,3072]{1,0:T(8,128)(2,1)S(1)} %bitcast.299), channel_id=1, source_target_pairs={{0,1},{1,0},{2,3},{3,2},{4,5},{5,4},{6,7},{7,6},{8,9},{9,8},{10,11... | collective-permute-start | bytes 9437192 | tf_op jit(solution)/shard_map/ppermute | solution.py:449
  114.0 14.3 %collective-permute-start.24 = (bf16[512,1536]{1,0:T(8,128)(2,1)S(1)}, bf16[512,1536]{1,0:T(8,128)(2,1)}, u32[]{:S(2)}, u32[]{:S(2)}) collective-permute-start(bf16[512,1536]{1,0:T(8,128)(2,1)S(1)} %constant_dynamic-slice_fusion.5), channel_id=1, source_target_pairs={{0,1},{1,0},{2,3},{3,2},{4,5},{5,4},{6,7},{7,6},{8,9},{9,8},{10,11... | collective-permute-start | bytes 4718600 | tf_op jit(solution)/shard_map/ppermute | solution.py:449
  122.0 28.0 %collective-permute-start.31 = (bf16[2,320,768]{2,1,0:T(8,128)(2,1)}, bf16[2,320,768]{2,1,0:T(8,128)(2,1)}, u32[]{:S(2)}, u32[]{:S(2)}) collective-permute-start(bf16[2,320,768]{2,1,0:T(8,128)(2,1)} %pad_maximum_fusion.2), channel_id=1, source_target_pairs={{0,1},{1,0},{2,3},{3,2},{4,5},{5,4},{6,7},{7,6},{8,9},{9,8},{10,11... | collective-permute-start | bytes 2949128 | tf_op jit(solution)/shard_map/ppermute | solution.py:449
  125.7 17.9 %collective-permute-start.21 = (bf16[256,384]{1,0:T(8,128)(2,1)S(1)}, bf16[256,384]{1,0:T(8,128)(2,1)S(1)}, u32[]{:S(2)}, u32[]{:S(2)}) collective-permute-start(bf16[256,384]{1,0:T(8,128)(2,1)S(1)} %get-tuple-element.201), channel_id=1, source_target_pairs={{0,1},{1,0},{2,3},{3,2},{4,5},{5,4},{6,7},{7,6},{8,9},{9,8},{10,11... | collective-permute-start | bytes 589832 | tf_op jit(solution)/shard_map/ppermute | solution.py:449
  125.8 17.8 %collective-permute-start.22 = (bf16[256,384]{1,0:T(8,128)(2,1)S(1)}, bf16[256,384]{1,0:T(8,128)(2,1)S(1)}, u32[]{:S(2)}, u32[]{:S(2)}) collective-permute-start(bf16[256,384]{1,0:T(8,128)(2,1)S(1)} %get-tuple-element.202), channel_id=1, source_target_pairs={{0,2},{1,3},{2,0},{3,1},{4,6},{5,7},{6,4},{7,5},{8,10},{9,11},{10,... | collective-permute-start | bytes 589832 | tf_op jit(solution)/shard_map/ppermute | solution.py:449
  127.5 16.1 %collective-permute-start.23 = (bf16[256,384]{1,0:T(8,128)(2,1)S(1)}, bf16[256,384]{1,0:T(8,128)(2,1)S(1)}, u32[]{:S(2)}, u32[]{:S(2)}) collective-permute-start(bf16[256,384]{1,0:T(8,128)(2,1)S(1)} %get-tuple-element.203), channel_id=1, source_target_pairs={{0,3},{1,2},{2,1},{3,0},{4,7},{5,6},{6,5},{7,4},{8,11},{9,10},{10,... | collective-permute-start | bytes 589832 | tf_op jit(solution)/shard_map/ppermute | solution.py:449
  146.6 37.0 %collective-permute-start.33 = (bf16[8,240,384]{2,1,0:T(8,128)(2,1)}, bf16[8,240,384]{2,1,0:T(8,128)(2,1)}, u32[]{:S(2)}, u32[]{:S(2)}) collective-permute-start(bf16[8,240,384]{2,1,0:T(8,128)(2,1)} %slice.343), channel_id=1, source_target_pairs={{0,8},{4,12},{8,0},{12,4},{16,24},{20,28},{24,16},{28,20},{1,9},{5... | collective-permute-start | bytes 4423688 | tf_op jit(solution)/shard_map/ppermute | solution.py:449
  148.4 32.7 %collective-permute-start.32 = (bf16[8,192,384]{2,1,0:T(8,128)(2,1)S(1)}, bf16[8,192,384]{2,1,0:T(8,128)(2,1)}, u32[]{:S(2)}, u32[]{:S(2)}) collective-permute-start(bf16[8,192,384]{2,1,0:T(8,128)(2,1)S(1)} %slice.338), channel_id=1, source_target_pairs={{0,4},{4,0},{8,12},{12,8},{16,20},{20,16},{24,28},{28,24},{1,5},{5... | collective-permute-start | bytes 3538952 | tf_op jit(solution)/shard_map/ppermute | solution.py:449
  173.1 13.0 %collective-permute-start.27 = (bf16[3,64,384]{2,1,0:T(8,128)(2,1)}, bf16[3,64,384]{2,1,0:T(8,128)(2,1)}, u32[]{:S(2)}, u32[]{:S(2)}) collective-permute-start(bf16[3,64,384]{2,1,0:T(8,128)(2,1)} %get-tuple-element.217), channel_id=1, source_target_pairs={{0,1},{1,0},{2,3},{3,2},{4,5},{5,4},{6,7},{7,6},{8,9},{9,8},{10,11... | collective-permute-start | bytes 442376 | tf_op jit(solution)/shard_map/ppermute | solution.py:449
  173.2 12.9 %collective-permute-start.28 = (bf16[3,64,384]{2,1,0:T(8,128)(2,1)}, bf16[3,64,384]{2,1,0:T(8,128)(2,1)}, u32[]{:S(2)}, u32[]{:S(2)}) collective-permute-start(bf16[3,64,384]{2,1,0:T(8,128)(2,1)} %get-tuple-element.218), channel_id=1, source_target_pairs={{0,2},{1,3},{2,0},{3,1},{4,6},{5,7},{6,4},{7,5},{8,10},{9,11},{10,... | collective-permute-start | bytes 442376 | tf_op jit(solution)/shard_map/ppermute | solution.py:449
  183.1 15.6 %collective-permute-start.34 = (bf16[4,192,384]{2,1,0:T(8,128)(2,1)S(1)}, bf16[4,192,384]{2,1,0:T(8,128)(2,1)S(1)}, u32[]{:S(2)}, u32[]{:S(2)}) collective-permute-start(bf16[4,192,384]{2,1,0:T(8,128)(2,1)S(1)} %get-tuple-element.325), channel_id=1, source_target_pairs={{0,8},{4,12},{8,0},{12,4},{16,24},{20,28},{24,16},{28,20},{1,9},{5... | collective-permute-start | bytes 1769480 | tf_op jit(solution)/shard_map/ppermute | solution.py:449
  185.5 19.4 %collective-permute-start.35 = (bf16[4,240,384]{2,1,0:T(8,128)(2,1)S(1)}, bf16[4,240,384]{2,1,0:T(8,128)(2,1)S(1)}, u32[]{:S(2)}, u32[]{:S(2)}) collective-permute-start(bf16[4,240,384]{2,1,0:T(8,128)(2,1)S(1)} %get-tuple-element.321), channel_id=1, source_target_pairs={{0,4},{4,0},{8,12},{12,8},{16,20},{20,16},{24,28},{28,24},{1,5},{5... | collective-permute-start | bytes 2211848 | tf_op jit(solution)/shard_map/ppermute | solution.py:449
  193.2 17.2 %collective-permute-start.36 = (bf16[3,256,384]{2,1,0:T(8,128)(2,1)S(1)}, bf16[3,256,384]{2,1,0:T(8,128)(2,1)S(1)}, u32[]{:S(2)}, u32[]{:S(2)}) collective-permute-start(bf16[3,256,384]{2,1,0:T(8,128)(2,1)S(1)} %copy-done.84), channel_id=1, source_target_pairs={{0,2},{1,3},{2,0},{3,1},{4,6},{5,7},{6,4},{7,5},{8,10},{9,11},{10,... | collective-permute-start | bytes 1769480 | tf_op jit(solution)/shard_map/ppermute | solution.py:449
  194.4 17.9 %collective-permute-start.41 = (bf16[128,384]{1,0:T(8,128)(2,1)S(1)}, bf16[128,384]{1,0:T(8,128)(2,1)S(1)}, u32[]{:S(2)}, u32[]{:S(2)}) collective-permute-start(bf16[128,384]{1,0:T(8,128)(2,1)S(1)} %constant_dynamic-slice_fusion.1), channel_id=1, source_target_pairs={{0,1},{1,0},{2,3},{3,2},{4,5},{5,4},{6,7},{7,6},{8,9},{9,8},{10,11... | collective-permute-start | bytes 294920 | tf_op jit(solution)/shard_map/ppermute | solution.py:449
  195.4 27.9 %collective-permute-start.43 = (bf16[8,144,384]{2,1,0:T(8,128)(2,1)}, bf16[8,144,384]{2,1,0:T(8,128)(2,1)}, u32[]{:S(2)}, u32[]{:S(2)}) collective-permute-start(bf16[8,144,384]{2,1,0:T(8,128)(2,1)} %slice.359), channel_id=1, source_target_pairs={{0,4},{4,0},{8,12},{12,8},{16,20},{20,16},{24,28},{28,24},{1,5},{5... | collective-permute-start | bytes 2654216 | tf_op jit(solution)/shard_map/ppermute | solution.py:449
  210.4 15.5 %collective-permute-start.37 = (bf16[64,384]{1,0:T(8,128)(2,1)S(1)}, bf16[64,384]{1,0:T(8,128)(2,1)S(1)}, u32[]{:S(2)}, u32[]{:S(2)}) collective-permute-start(bf16[64,384]{1,0:T(8,128)(2,1)S(1)} %get-tuple-element.240), channel_id=1, source_target_pairs={{0,1},{1,0},{2,3},{3,2},{4,5},{5,4},{6,7},{7,6},{8,9},{9,8},{10,11... | collective-permute-start | bytes 147464 | tf_op jit(solution)/shard_map/ppermute | solution.py:449
  212.2 13.7 %collective-permute-start.38 = (bf16[64,384]{1,0:T(8,128)(2,1)S(1)}, bf16[64,384]{1,0:T(8,128)(2,1)S(1)}, u32[]{:S(2)}, u32[]{:S(2)}) collective-permute-start(bf16[64,384]{1,0:T(8,128)(2,1)S(1)} %get-tuple-element.241), channel_id=1, source_target_pairs={{0,2},{1,3},{2,0},{3,1},{4,6},{5,7},{6,4},{7,5},{8,10},{9,11},{10,... | collective-permute-start | bytes 147464 | tf_op jit(solution)/shard_map/ppermute | solution.py:449
  213.4 12.5 %collective-permute-start.39 = (bf16[64,384]{1,0:T(8,128)(2,1)S(1)}, bf16[64,384]{1,0:T(8,128)(2,1)S(1)}, u32[]{:S(2)}, u32[]{:S(2)}) collective-permute-start(bf16[64,384]{1,0:T(8,128)(2,1)S(1)} %get-tuple-element.242), channel_id=1, source_target_pairs={{0,3},{1,2},{2,1},{3,0},{4,7},{5,6},{6,5},{7,4},{8,11},{9,10},{10,... | collective-permute-start | bytes 147464 | tf_op jit(solution)/shard_map/ppermute | solution.py:449
  225.9 23.2 %collective-permute-start.48 = (bf16[3,256,384]{2,1,0:T(8,128)(2,1)}, bf16[3,256,384]{2,1,0:T(8,128)(2,1)}, u32[]{:S(2)}, u32[]{:S(2)}) collective-permute-start(bf16[3,256,384]{2,1,0:T(8,128)(2,1)} %get-tuple-element.269.refs_8_), channel_id=1, source_target_pairs={{0,3},{1,2},{2,1},{3,0},{4,7},{5,6},{6,5},{7,4},{8,11},{9,10},{10,... | collective-permute-start | bytes 1769480 | tf_op jit(solution)/shard_map/ppermute | solution.py:449
  235.2 12.4 %collective-permute-start.45 = (bf16[3,64,384]{2,1,0:T(8,128)(2,1)}, bf16[3,64,384]{2,1,0:T(8,128)(2,1)S(1)}, u32[]{:S(2)}, u32[]{:S(2)}) collective-permute-start(bf16[3,64,384]{2,1,0:T(8,128)(2,1)} %get-tuple-element.265.refs_6_), channel_id=1, source_target_pairs={{0,1},{1,0},{2,3},{3,2},{4,5},{5,4},{6,7},{7,6},{8,9},{9,8},{10,11... | collective-permute-start | bytes 442376 | tf_op jit(solution)/shard_map/ppermute | solution.py:449
  236.3 12.3 %collective-permute-start.46 = (bf16[3,64,384]{2,1,0:T(8,128)(2,1)}, bf16[3,64,384]{2,1,0:T(8,128)(2,1)S(1)}, u32[]{:S(2)}, u32[]{:S(2)}) collective-permute-start(bf16[3,64,384]{2,1,0:T(8,128)(2,1)} %get-tuple-element.266.refs_7_), channel_id=1, source_target_pairs={{0,2},{1,3},{2,0},{3,1},{4,6},{5,7},{6,4},{7,5},{8,10},{9,11},{10,... | collective-permute-start | bytes 442376 | tf_op jit(solution)/shard_map/ppermute | solution.py:449
  237.3 11.9 %collective-permute-start.47 = (bf16[3,64,384]{2,1,0:T(8,128)(2,1)}, bf16[3,64,384]{2,1,0:T(8,128)(2,1)S(1)}, u32[]{:S(2)}, u32[]{:S(2)}) collective-permute-start(bf16[3,64,384]{2,1,0:T(8,128)(2,1)} %get-tuple-element.267.refs_8_), channel_id=1, source_target_pairs={{0,3},{1,2},{2,1},{3,0},{4,7},{5,6},{6,5},{7,4},{8,11},{9,10},{10,... | collective-permute-start | bytes 442376 | tf_op jit(solution)/shard_map/ppermute | solution.py:449
  237.8 48.9 %collective-permute-start.50 = (bf16[2,432,384]{2,1,0:T(8,128)(2,1)S(1)}, bf16[2,432,384]{2,1,0:T(8,128)(2,1)}, u32[]{:S(2)}, u32[]{:S(2)}) collective-permute-start(bf16[2,432,384]{2,1,0:T(8,128)(2,1)S(1)} %pad_maximum_fusion.8), channel_id=1, source_target_pairs={{0,16},{4,20},{8,24},{12,28},{16,0},{20,4},{24,8},{28,12},{1,17},{... | collective-permute-start | bytes 1990664 | tf_op jit(solution)/shard_map/ppermute | solution.py:449
  247.6 41.8 %collective-permute-start.51 = (bf16[4,144,384]{2,1,0:T(8,128)(2,1)}, bf16[4,144,384]{2,1,0:T(8,128)(2,1)S(1)}, u32[]{:S(2)}, u32[]{:S(2)}) collective-permute-start(bf16[4,144,384]{2,1,0:T(8,128)(2,1)} %get-tuple-element.329), channel_id=1, source_target_pairs={{0,2},{1,3},{2,0},{3,1},{4,6},{5,7},{6,4},{7,5},{8,10},{9,11},{10,... | collective-permute-start | bytes 1327112 | tf_op jit(solution)/shard_map/ppermute | solution.py:449
  248.6 30.4 %collective-permute-start.49 = (bf16[8,208,384]{2,1,0:T(8,128)(2,1)}, bf16[8,208,384]{2,1,0:T(8,128)(2,1)S(1)}, u32[]{:S(2)}, u32[]{:S(2)}) collective-permute-start(bf16[8,208,384]{2,1,0:T(8,128)(2,1)} %slice.373), channel_id=1, source_target_pairs={{0,4},{4,0},{8,12},{12,8},{16,20},{20,16},{24,28},{28,24},{1,5},{5... | collective-permute-start | bytes 3833864 | tf_op jit(solution)/shard_map/ppermute | solution.py:449
  250.7 56.1 %collective-permute-start.52 = (bf16[8,240,384]{2,1,0:T(8,128)(2,1)S(1)}, bf16[8,240,384]{2,1,0:T(8,128)(2,1)S(1)}, u32[]{:S(2)}, u32[]{:S(2)}) collective-permute-start(bf16[8,240,384]{2,1,0:T(8,128)(2,1)S(1)} %slice.386), channel_id=1, source_target_pairs={{0,2},{1,3},{2,0},{3,1},{4,6},{5,7},{6,4},{7,5},{8,10},{9,11},{10,... | collective-permute-start | bytes 4423688 | tf_op jit(solution)/shard_map/ppermute | solution.py:449
  279.4 26.3 %collective-permute-start.54 = (bf16[4,208,384]{2,1,0:T(8,128)(2,1)S(1)}, bf16[4,208,384]{2,1,0:T(8,128)(2,1)S(1)}, u32[]{:S(2)}, u32[]{:S(2)}) collective-permute-start(bf16[4,208,384]{2,1,0:T(8,128)(2,1)S(1)} %get-tuple-element.323), channel_id=1, source_target_pairs={{0,2},{1,3},{2,0},{3,1},{4,6},{5,7},{6,4},{7,5},{8,10},{9,11},{10,... | collective-permute-start | bytes 1916936 | tf_op jit(solution)/shard_map/ppermute | solution.py:449
  286.6 23.5 %collective-permute-start.44 = (bf16[3,256,384]{2,1,0:T(8,128)(2,1)S(1)}, bf16[3,256,384]{2,1,0:T(8,128)(2,1)S(1)}, u32[]{:S(2)}, u32[]{:S(2)}) collective-permute-start(bf16[3,256,384]{2,1,0:T(8,128)(2,1)S(1)} %copy-done.83), channel_id=1, source_target_pairs={{0,1},{1,0},{2,3},{3,2},{4,5},{5,4},{6,7},{7,6},{8,9},{9,8},{10,11... | collective-permute-start | bytes 1769480 | tf_op jit(solution)/shard_map/ppermute | solution.py:449
  286.8 22.5 %collective-permute-start.53 = (bf16[8,144,384]{2,1,0:T(8,128)(2,1)S(1)}, bf16[8,144,384]{2,1,0:T(8,128)(2,1)S(1)}, u32[]{:S(2)}, u32[]{:S(2)}) collective-permute-start(bf16[8,144,384]{2,1,0:T(8,128)(2,1)S(1)} %slice.391), channel_id=1, source_target_pairs={{0,8},{4,12},{8,0},{12,4},{16,24},{20,28},{24,16},{28,20},{1,9},{5... | collective-permute-start | bytes 2654216 | tf_op jit(solution)/shard_map/ppermute | solution.py:449
  289.6 39.8 %collective-permute-start.58 = (bf16[2,144,384]{2,1,0:T(8,128)(2,1)S(1)}, bf16[2,144,384]{2,1,0:T(8,128)(2,1)S(1)}, u32[]{:S(2)}, u32[]{:S(2)}) collective-permute-start(bf16[2,144,384]{2,1,0:T(8,128)(2,1)S(1)} %get-tuple-element.362), channel_id=1, source_target_pairs={{0,8},{4,12},{8,0},{12,4},{16,24},{20,28},{24,16},{28,20},{1,9},{5... | collective-permute-start | bytes 663560 | tf_op jit(solution)/shard_map/ppermute | solution.py:449
  305.7 23.6 %collective-permute-start.57 = (bf16[1,432,384]{2,1,0:T(8,128)(2,1)S(1)}, bf16[1,432,384]{2,1,0:T(8,128)(2,1)S(1)}, u32[]{:S(2)}, u32[]{:S(2)}) collective-permute-start(bf16[1,432,384]{2,1,0:T(8,128)(2,1)S(1)} %get-tuple-element.340), channel_id=1, source_target_pairs={{0,2},{1,3},{2,0},{3,1},{4,6},{5,7},{6,4},{7,5},{8,10},{9,11},{10,... | collective-permute-start | bytes 995336 | tf_op jit(solution)/shard_map/ppermute | solution.py:449
  306.8 23.0 %collective-permute-start.59 = (bf16[2,208,384]{2,1,0:T(8,128)(2,1)S(1)}, bf16[2,208,384]{2,1,0:T(8,128)(2,1)S(1)}, u32[]{:S(2)}, u32[]{:S(2)}) collective-permute-start(bf16[2,208,384]{2,1,0:T(8,128)(2,1)S(1)} %get-tuple-element.342), channel_id=1, source_target_pairs={{0,8},{4,12},{8,0},{12,4},{16,24},{20,28},{24,16},{28,20},{1,9},{5... | collective-permute-start | bytes 958472 | tf_op jit(solution)/shard_map/ppermute | solution.py:449
  309.3 17.7 %collective-permute-start.55 = (bf16[4,240,384]{2,1,0:T(8,128)(2,1)S(1)}, bf16[4,240,384]{2,1,0:T(8,128)(2,1)S(1)}, u32[]{:S(2)}, u32[]{:S(2)}) collective-permute-start(bf16[4,240,384]{2,1,0:T(8,128)(2,1)S(1)} %get-tuple-element.319), channel_id=1, source_target_pairs={{0,4},{4,0},{8,12},{12,8},{16,20},{20,16},{24,28},{28,24},{1,5},{5... | collective-permute-start | bytes 2211848 | tf_op jit(solution)/shard_map/ppermute | solution.py:449
  310.1 18.5 %collective-permute-start.56 = (bf16[4,144,384]{2,1,0:T(8,128)(2,1)S(1)}, bf16[4,144,384]{2,1,0:T(8,128)(2,1)S(1)}, u32[]{:S(2)}, u32[]{:S(2)}) collective-permute-start(bf16[4,144,384]{2,1,0:T(8,128)(2,1)S(1)} %get-tuple-element.327), channel_id=1, source_target_pairs={{0,2},{1,3},{2,0},{3,1},{4,6},{5,7},{6,4},{7,5},{8,10},{9,11},{10,... | collective-permute-start | bytes 1327112 | tf_op jit(solution)/shard_map/ppermute | solution.py:449
  327.2 14.0 %collective-permute-start.60 = (bf16[2,240,384]{2,1,0:T(8,128)(2,1)S(1)}, bf16[2,240,384]{2,1,0:T(8,128)(2,1)S(1)}, u32[]{:S(2)}, u32[]{:S(2)}) collective-permute-start(bf16[2,240,384]{2,1,0:T(8,128)(2,1)S(1)} %get-tuple-element.336), channel_id=1, source_target_pairs={{0,8},{4,12},{8,0},{12,4},{16,24},{20,28},{24,16},{28,20},{1,9},{5... | collective-permute-start | bytes 1105928 | tf_op jit(solution)/shard_map/ppermute | solution.py:449
  328.7 12.7 %collective-permute-start.61 = (bf16[2,144,384]{2,1,0:T(8,128)(2,1)S(1)}, bf16[2,144,384]{2,1,0:T(8,128)(2,1)S(1)}, u32[]{:S(2)}, u32[]{:S(2)}) collective-permute-start(bf16[2,144,384]{2,1,0:T(8,128)(2,1)S(1)} %get-tuple-element.361), channel_id=1, source_target_pairs={{0,4},{4,0},{8,12},{12,8},{16,20},{20,16},{24,28},{28,24},{1,5},{5... | collective-permute-start | bytes 663560 | tf_op jit(solution)/shard_map/ppermute | solution.py:449
  329.5 15.0 %collective-permute-start.62 = (bf16[1,144,384]{2,1,0:T(8,128)(2,1)S(1)}, bf16[1,144,384]{2,1,0:T(8,128)(2,1)S(1)}, u32[]{:S(2)}, u32[]{:S(2)}) collective-permute-start(bf16[1,144,384]{2,1,0:T(8,128)(2,1)S(1)} %get-tuple-element.386), channel_id=1, source_target_pairs={{0,16},{4,20},{8,24},{12,28},{16,0},{20,4},{24,8},{28,12},{1,17},{... | collective-permute-start | bytes 331784 | tf_op jit(solution)/shard_map/ppermute | solution.py:449
  329.9 19.3 %collective-permute-start.63 = (bf16[1,208,384]{2,1,0:T(8,128)(2,1)S(1)}, bf16[1,208,384]{2,1,0:T(8,128)(2,1)S(1)}, u32[]{:S(2)}, u32[]{:S(2)}) collective-permute-start(bf16[1,208,384]{2,1,0:T(8,128)(2,1)S(1)} %get-tuple-element.372), channel_id=1, source_target_pairs={{0,16},{4,20},{8,24},{12,28},{16,0},{20,4},{24,8},{28,12},{1,17},{... | collective-permute-start | bytes 479240 | tf_op jit(solution)/shard_map/ppermute | solution.py:449
  341.3 11.9 %collective-permute-start.64 = (bf16[1,240,384]{2,1,0:T(8,128)(2,1)S(1)}, bf16[1,240,384]{2,1,0:T(8,128)(2,1)S(1)}, u32[]{:S(2)}, u32[]{:S(2)}) collective-permute-start(bf16[1,240,384]{2,1,0:T(8,128)(2,1)S(1)} %get-tuple-element.370), channel_id=1, source_target_pairs={{0,16},{4,20},{8,24},{12,28},{16,0},{20,4},{24,8},{28,12},{1,17},{... | collective-permute-start | bytes 552968 | tf_op jit(solution)/shard_map/ppermute | solution.py:449
  341.4 13.7 %collective-permute-start.65 = (bf16[1,144,384]{2,1,0:T(8,128)(2,1)S(1)}, bf16[1,144,384]{2,1,0:T(8,128)(2,1)S(1)}, u32[]{:S(2)}, u32[]{:S(2)}) collective-permute-start(bf16[1,144,384]{2,1,0:T(8,128)(2,1)S(1)} %get-tuple-element.385), channel_id=1, source_target_pairs={{0,16},{4,20},{8,24},{12,28},{16,0},{20,4},{24,8},{28,12},{1,17},{... | collective-permute-start | bytes 331784 | tf_op jit(solution)/shard_map/ppermute | solution.py:449
  355.2 12.2 %collective-permute-start.66 = (bf16[592,384]{1,0:T(8,128)(2,1)S(1)}, bf16[592,384]{1,0:T(8,128)(2,1)S(1)}, u32[]{:S(2)}, u32[]{:S(2)}) collective-permute-start(bf16[592,384]{1,0:T(8,128)(2,1)S(1)} %pad_maximum_fusion.9), channel_id=1, source_target_pairs={{0,2},{1,3},{2,0},{3,1},{4,6},{5,7},{6,4},{7,5},{8,10},{9,11},{10,... | collective-permute-start | bytes 1363976 | tf_op jit(solution)/shard_map/ppermute | solution.py:449
  358.3 12.6 %collective-permute-start.69 = (bf16[2,576,384]{2,1,0:T(8,128)(2,1)S(1)}, bf16[2,576,384]{2,1,0:T(8,128)(2,1)}, u32[]{:S(2)}, u32[]{:S(2)}) collective-permute-start(bf16[2,576,384]{2,1,0:T(8,128)(2,1)S(1)} %pad_maximum_fusion.4.refs_1_), channel_id=1, source_target_pairs={{0,1},{1,0},{2,3},{3,2},{4,5},{5,4},{6,7},{7,6},{8,9},{9,8},{10,11... | collective-permute-start | bytes 2654216 | tf_op jit(solution)/shard_map/ppermute | solution.py:449
  367.7 12.0 %collective-permute-start.67 = (bf16[2,592,384]{2,1,0:T(8,128)(2,1)S(1)}, bf16[2,592,384]{2,1,0:T(8,128)(2,1)}, u32[]{:S(2)}, u32[]{:S(2)}) collective-permute-start(bf16[2,592,384]{2,1,0:T(8,128)(2,1)S(1)} %pad_maximum_fusion.3.refs_1_), channel_id=1, source_target_pairs={{0,1},{1,0},{2,3},{3,2},{4,5},{5,4},{6,7},{7,6},{8,9},{9,8},{10,11... | collective-permute-start | bytes 2727944 | tf_op jit(solution)/shard_map/ppermute | solution.py:449
  (135 other events, 935.0 us)

commit v4 on v3

--- a/solution.py
+++ b/solution.py
@@ -206,7 +206,8 @@
     outs, refs = refs[3 + OWNERS : 3 + 2 * OWNERS], refs[3 + 2 * OWNERS :]
     if not routed:
         slot_outs, refs = refs[:OWNERS], refs[OWNERS:]
-    incoming, grad_q, grad_k, grad_v = refs
+    incoming, turned_keys, grad_q, grad_k, grad_v = refs
+    turned_keys[...] = merged[1].T
     me = 2 * place[0] + place[1]
     blocks = OWNERS * rows // BLOCK
     for r in range(OWNERS):
@@ -219,15 +220,15 @@
         span = slice(a * BLOCK, (a + 1) * BLOCK)
         queries = merged[0, span, :] * jnp.asarray(HEAD_DIM**-0.5, BF16)
         grad_mix = incoming[span, :]
-        grad_query = jnp.zeros((BLOCK, LANES), F32)
+        grad_queries = []
         inner = (grad_mix.astype(F32) * mixed[span, :].astype(F32)).T
         for head in range(2):
             own_q = only_head(queries, head)
             own_g = only_head(grad_mix, head)
             level = stats[0, head : head + 1, span]
-            offset = jnp.sum(
-                inner[head * HEAD_DIM : (head + 1) * HEAD_DIM], axis=0, keepdims=True
-            )
+            head_rows = slice(head * HEAD_DIM, (head + 1) * HEAD_DIM)
+            grad_query = jnp.zeros((HEAD_DIM, BLOCK), F32)
+            offset = jnp.sum(inner[head_rows], axis=0, keepdims=True)
             for b in range(a + 1):
                 keys_at = slice(b * BLOCK, (b + 1) * BLOCK)
                 prob = jnp.exp(dot(merged[1, keys_at, :], own_q, NT) - level)
@@ -237,9 +238,9 @@
                 grad_v[keys_at, :] += dot(prob.astype(BF16), own_g)
                 grad_score = (prob * (grad_prob - offset)).astype(BF16)
                 grad_k[keys_at, :] += dot(grad_score, own_q)
-                own_k = only_head(merged[1, keys_at, :], head)
-                grad_query = grad_query + dot(grad_score, own_k, TN)
-        grad_q[span, :] = grad_query * HEAD_DIM**-0.5
+                grad_query = grad_query + dot(turned_keys[head_rows, keys_at], grad_score)
+            grad_queries.append(grad_query)
+        grad_q[span, :] = jnp.concatenate(grad_queries, axis=0).T * HEAD_DIM**-0.5
     for r in range(OWNERS):
         owner = me ^ r
         at = pl.ds(pl.multiple_of(owner * rows, rows), rows)
@@ -282,7 +283,10 @@
         out_shape=shapes,
         in_specs=specs,
         out_specs=out_specs,
-        scratch_shapes=[pltpu.VMEM((length, LANES), BF16)]
+        scratch_shapes=[
+            pltpu.VMEM((length, LANES), BF16),
+            pltpu.VMEM((LANES, length), BF16),
+        ]
         + [pltpu.VMEM((length, LANES), F32)] * 3,
         compiler_params=pltpu.CompilerParams(vmem_limit_bytes=VMEM_BYTES),
         cost_estimate=cost(40 * HEAD_DIM * work, 16 * length * half, work),
@@ -298,11 +302,9 @@
     dp = list(range(bits))
     rest = dp[2:]
     return (
-        [dp[0], dp[1]] + rest + [Y_STAGE],
-        [dp[1], dp[0]] + rest + [Y_STAGE],
-        [Y_STAGE, dp[0], dp[1]] + rest,
         [dp[0], Y_STAGE, dp[1]] + rest,
-        [dp[1], Y_STAGE, dp[0]] + rest,
+        [dp[1], dp[0], Y_STAGE] + rest,
+        [Y_STAGE, dp[1], dp[0]] + rest,
     )
 
 
@@ -326,6 +328,28 @@
             )[None]
 
 
+def start_halves(unit, keep, send, sems):
+    n = keep.shape[0]
+    copies = [
+        pltpu.make_async_copy(unit.at[pl.ds(0, n)], keep, sems.at[0]),
+        pltpu.make_async_copy(unit.at[pl.ds(n, n)], send, sems.at[1]),
+    ]
+    for copy in copies:
+        copy.start()
+    return copies
+
+
+def halves_out(slabs, rows, half):
+    return [jax.ShapeDtypeStruct((slabs, rows // 2, half), BF16)] * 2
+
+
+def unit_scratch(slabs, rows, half):
+    return [pltpu.VMEM((2 * slabs, rows // 2, half), BF16), pltpu.SemaphoreType.DMA((2,))]
+
+
+ANY_SPEC = pl.BlockSpec(memory_space=pl.ANY)
+
+
 def feed_grad_kernel(bits, orders, routed, place, *refs):
     ff_refs, gel_refs, mix_refs, gh_refs, gff_refs, gatt_refs = (
         refs[2 * k : 2 * k + 2] for k in range(6)
@@ -336,7 +360,8 @@
     slabs = 1 << bits
     narrow = width // slabs
     wide = OWNERS * narrow
-    first, second = refs[-2:]
+    first, first_sems, second, second_sems = refs[-4:]
+    outs = refs[-8:-4]
     if routed:
         for d in range(slabs):
             store_slabs((first, wide, orders[0]), bits, place, d, refs[0][d], SPARE)
@@ -347,6 +372,7 @@
         found = dot(turned[0], gh_refs[0][:, tile])
         found = found + dot(turned[1], gh_refs[1][:, t * half : (t + 1) * half])
         store_slabs((first, t * narrow, orders[0]), bits, place, 0, found, narrow)
+    copies = start_halves(first, outs[0], outs[1], first_sems)
     for t in range(OWNERS):
         rows = slice(t * width, (t + 1) * width)
         found = dot(gel_refs[0][:, rows], gff_refs[0][:, own], TN)
@@ -355,6 +381,8 @@
     found = dot(mix_refs[0][...], gatt_refs[0][:, own], TN)
     found = found + dot(mix_refs[1][...], gatt_refs[1][...], TN)
     store_slabs((second, wide, orders[1]), bits, place, 0, found, narrow)
+    for copy in copies + start_halves(second, outs[2], outs[3], second_sems):
+        copy.wait()
 
 
 def feed_grad(place, bits, orders, operands, route=None):
@@ -366,27 +394,32 @@
     routed = route is not None
     rows = (wide + (SPARE if routed else 0), wide + narrow)
     extra = [route] if routed else []
-    return pl.pallas_call(
+    up_keep, up_send, down_keep, down_send = pl.pallas_call(
         lambda *refs: feed_grad_kernel(bits, orders, routed, *refs),
         name="feed_grad",
         in_specs=[SMEM_SPEC] + [VMEM_SPEC] * (12 + len(extra)),
-        out_specs=[VMEM_SPEC] * len(rows),
-        out_shape=[jax.ShapeDtypeStruct((2 * slabs, count // 2, half), BF16) for count in rows],
+        out_specs=[ANY_SPEC] * 4,
+        out_shape=halves_out(slabs, rows[0], half) + halves_out(slabs, rows[1], half),
+        scratch_shapes=unit_scratch(slabs, rows[0], half) + unit_scratch(slabs, rows[1], half),
         compiler_params=pltpu.CompilerParams(vmem_limit_bytes=VMEM_BYTES),
         cost_estimate=cost(
             18 * tokens * width * width, 9 * width * width + 40 * tokens * width
         ),
     )(place, *operands, *extra)
+    return (up_keep, up_send), (down_keep, down_send)
 
 
 def qkv_grad_kernel(bits, order, place, *refs):
-    acts, pieces, out = refs[:OWNERS], refs[OWNERS : 2 * OWNERS], refs[2 * OWNERS]
+    acts, pieces = refs[:OWNERS], refs[OWNERS : 2 * OWNERS]
+    keep, send, out, sems = refs[2 * OWNERS :]
     narrow = acts[0].shape[1] // (1 << bits)
     for part in range(3):
         found = dot(acts[0][...], pieces[0][part], TN)
         for r in range(1, OWNERS):
             found = found + dot(acts[r][...], pieces[r][part], TN)
         store_slabs((out, part * narrow, order), bits, place, 0, found, narrow)
+    for copy in start_halves(out, keep, send, sems):
+        copy.wait()
 
 
 def qkv_grad(place, bits, order, acts, pieces):
@@ -398,8 +431,9 @@
         lambda *refs: qkv_grad_kernel(bits, order, *refs),
         name="qkv_grad",
         in_specs=[SMEM_SPEC] + [VMEM_SPEC] * (2 * OWNERS),
-        out_specs=VMEM_SPEC,
-        out_shape=jax.ShapeDtypeStruct((2 * slabs, 3 * narrow // 2, half), BF16),
+        out_specs=[ANY_SPEC] * 2,
+        out_shape=halves_out(slabs, 3 * narrow, half),
+        scratch_shapes=unit_scratch(slabs, 3 * narrow, half),
         compiler_params=pltpu.CompilerParams(vmem_limit_bytes=VMEM_BYTES),
         cost_estimate=cost(
             12 * rows * width * width, 3 * width * width + 20 * rows * width
@@ -476,18 +510,16 @@
 
 class Chain:
     def __init__(self, unit, order):
-        self.unit, self.order, self.stage = unit, order, 0
-        self.state = None, halves(unit)[1]
-
-    def step(self, after):
-        if self.stage == 0:
-            unit, _ = hold(self.unit, after)
-            keep = halves(unit)[0]
-        else:
-            keep, _ = hold(self.state[0], after)
-        self.state = combine(keep, stage_swap(self.state, self.order, self.stage))
+        self.state, self.order, self.stage = unit, order, 0
+
+    def step(self):
+        received = stage_swap(self.state, self.order, self.stage)
+        self.state = combine(self.state[0], received)
         self.stage += 1
-        return self.state
+
+    @property
+    def done(self):
+        return self.stage == len(self.order)
 
 
 def merge(chains):
@@ -499,11 +531,17 @@
     return found
 
 
-def advance(chains, stage, token):
+def meet(chains, *values):
+    held = hold([chain.state for chain in chains], *values)
+    for chain, state in zip(chains, held[0]):
+        chain.state = state
+    return held[1:]
+
+
+def stage(chains, *values):
     for chain in chains:
-        while chain.stage < min(stage, len(chain.order)):
-            token = chain.step(token)
-    return token
+        chain.step()
+    return meet(chains, *values)
 
 
 def gather_halves(own, y_first):
@@ -708,23 +746,20 @@
     operands = [y for x in early + [late[0], early_grad, late[1]] for y in x]
     feed_b = feed_grad(place, bits, (0, 1), operands)
     grads, feed_b = hold(grads, feed_b)
-    chains_b = [Chain(unit, send_orders(bits)[k]) for k, unit in enumerate(feed_b)]
+    x_order, z_order, y_order = send_orders(bits)
+    feed_chains_b = [Chain(unit, order) for unit, order in zip(feed_b, (x_order, z_order))]
     packed_b, packed_slot = attend_back(place, counts_mine, saved_b, grads, chosen_mine)
     packed_slot = exchange(packed_slot)
-    part_b = qkv_grad(place, bits, 3, acts_b, packed_b)
-    token = advance(chains_b, 1, part_b)
-    packed_slot, part_b, packed_b, token = hold(packed_slot, part_b, packed_b, token)
-    feed_chains_b, part_chain_b = chains_b, Chain(part_b, send_orders(bits)[3])
-    packed_two = swap(packed_b[2], "seq", 2)
+    part_chain_b = Chain(qkv_grad(place, bits, 0, acts_b, packed_b), x_order)
+    packed_slot, packed_b, _ = stage(feed_chains_b, packed_slot, packed_b, part_chain_b.state)
 
     grad_packed_slot = assemble_packed(packed_slot, y_first, core_first)
     slot_grad = norm_back(slot_mid, gain_b1, project_back(grad_packed_slot, qkv_b))
     mid_at_slot = jnp.einsum("bcr,brd->bcd", live_hits, grad_mid_b, precision=EXACT)
     grad_done = jnp.where(live[..., None], mid_at_slot + slot_grad, 0.0)
     grad_ff_a, grad_hidden_a = hidden_backward(grad_done, down_a, kept_a[3])
-    token = advance(feed_chains_b, 2, (token, grad_hidden_a))
-    grad_hidden_a, token = hold(grad_hidden_a, token)
-    feed_chain_b = merge(feed_chains_b)
+    (grad_hidden_a,) = stage(feed_chains_b, grad_hidden_a)
+    (grad_hidden_a,) = meet([part_chain_b], grad_hidden_a)
     grad_mid_a, grad_att_a, grad_mix_a = feed_backward(
         grad_done, grad_hidden_a, router, out_a, gain_a2, up_a, kept_a[1]
     )
@@ -732,7 +767,6 @@
     late = [
         half_with_far(flat(x), core_at) for x in (grad_hidden_a, grad_ff_a, grad_att_a)
     ]
-    grads, packed_two, token = hold(grads, packed_two, token)
     grads = exchange(grads)
     grad_router = jnp.sum(kept_a[0] * grad_mid_a, axis=-1)
     grad_route = jnp.einsum("bc,bcd->d", grad_router, picked, precision=EXACT)
@@ -740,73 +774,98 @@
         grad_route.reshape(dp_size, 1, narrow), ((0, 0), (0, SPARE - 1), (0, half - narrow))
     )
     operands = [y for x in early_a + late for y in x]
-    feed_a = feed_grad(place, bits, (3, 2), operands, route)
-    token = advance([part_chain_b], 1, (token, feed_a))
-    grads, feed_a, late, token = hold(grads, feed_a, (packed_b[1], packed_b[3]), token)
-    packed_three = swap(late[1], "seq", 3)
-    up_chain_a = Chain(feed_a[0], send_orders(bits)[3])
+    feed_a = feed_grad(place, bits, (0, 1), operands, route)
+    grads, feed_a = stage(feed_chains_b + [part_chain_b], grads, feed_a)
+    part_chain_b.step()
+    feed_chain_b = merge(feed_chains_b)
+    feed_chains_a = [Chain(unit, order) for unit, order in zip(feed_a, (x_order, z_order))]
     packed_a, _ = attend_back(place, counts_mine, saved_a, grads)
+    (packed_a,) = meet([part_chain_b], packed_a)
     returned_a = exchange(packed_a)
-    part_a = qkv_grad(place, bits, 4, acts_a, packed_a)
-    returned_a, part_a, down_a_unit, packed_three, token = hold(
-        returned_a, part_a, feed_a[1], packed_three, token
-    )
-    returned_b = [packed_b[0], swap(late[0], "seq", 1), packed_two, packed_three]
-    down_chain_a = Chain(down_a_unit, send_orders(bits)[2])
-    part_chain_a = Chain(part_a, send_orders(bits)[4])
-    chains_a = [up_chain_a, down_chain_a, part_chain_a]
+    part_chain_a = Chain(qkv_grad(place, bits, 2, acts_a, packed_a), y_order)
+    returned_a, packed_b, kept_last = meet([part_chain_a], returned_a, packed_b, kept_b[4])
+    done_b = kept_b[1] + project(kept_last, down_b)
+    gains = [
+        lax.dynamic_slice_in_dim(gain, dp_at * narrow, narrow, axis=0).astype(F32)
+        for gain in (gain_a1, gain_a2, gain_b1, gain_b2)
+    ]
 
     grad_packed_a = assemble_packed(returned_a, y_first, core_first)
     res_a = norm_back(picked, gain_a1, project_back(grad_packed_a, qkv_a))
     grad_picked = (
         grad_mid_a + res_a + grad_router[..., None] * route_w.astype(F32) - grad_done
     )
-    token = advance([up_chain_a], 1, (token, grad_picked))
-    token = advance([feed_chain_b], bits, token)
-    token = advance([part_chain_b], 2, token)
-    token = advance([down_chain_a, part_chain_a], 1, token)
-    done_b, returned_b, token = hold(done_b, returned_b, token)
-    token = advance(chains_a, 2, token)
-    token = advance([feed_chain_b], bits + 1, token)
-    token = advance([part_chain_b], 3, token)
-    token = advance(chains_a, 3, token)
-    token = advance([part_chain_b], bits + 1, token)
+    late_weight, packed_b = hold(qkv_b, packed_b)
+    weight_parts = [
+        lax.dynamic_slice_in_dim(late_weight, part * width + core_at * half, half, axis=1)
+        for part in range(3)
+    ]
+    shares = [
+        sum(dot(piece[part], weight_parts[part], NT) for part in range(3)) for piece in packed_b
+    ]
+    tail = feed_chains_a + [part_chain_a]
+    b_side = [feed_chain_b, part_chain_b]
+    for chain in tail:
+        chain.step()
+    given = swap(jnp.stack([shares[1].astype(BF16), shares[3].astype(BF16)]), "seq", 1)
+    act_near = shares[0] + given[0].astype(F32)
+    act_far = (shares[2] + given[1].astype(F32)).astype(BF16)
+    grad_picked, act_near, act_far, done_b, gains = meet(
+        tail + b_side, grad_picked, act_near, act_far, done_b, gains
+    )
+    for chain in b_side:
+        chain.step()
+    stage(tail)
+    meet(b_side, tail[0].state)
+    if not part_chain_b.done:
+        part_chain_b.step()
+    (act_far,) = stage(tail, act_far)
+    act_far = swap(act_far, "seq", 2).astype(F32)
+    last = merge(tail)
+    for chain in [last] + b_side:
+        while not chain.done:
+            chain.step()
+    def gain_grad(found, weight, gain):
+        at = dp_at * narrow
+        weight = lax.dynamic_slice_in_dim(weight, at, narrow, axis=0).astype(F32)
+        return jnp.sum(found * weight, axis=1) / gain
+
     near_b, far_b = gather_halves(
         jnp.concatenate([feed_chain_b.state, part_chain_b.state]), y_first
     )
-    token = advance(chains_a, bits, token)
-
-    grad_packed_b = assemble_packed(returned_b, y_first, core_first)
-    res_b = norm_back(middle, gain_b1, project_back(grad_packed_b, qkv_b))
+
+    grad_act_b = jnp.stack(
+        [jnp.where(y_first, act_near, act_far), jnp.where(y_first, act_far, act_near)]
+    )
+    res_b = norm_back(middle, gain_b1, grad_act_b)
     grad_input = grad_mid_b + res_b + scatter(grad_picked)
     qkv_gb, out_gb, up_gb, down_gb = finish(place, OWNERS * narrow, narrow, width, near_b, far_b)
-    token = advance(chains_a, bits + 1, token)
-    near, far = gather_halves(jnp.concatenate([x.state for x in chains_a]), y_first)
+    own = last.state
+    gains_b = gain_grad(qkv_gb, qkv_b, gains[2]), gain_grad(up_gb, up_b, gains[3])
+    other, gains_b, _ = hold(
+        swap(own, "seq", 2), gains_b, (qkv_gb, out_gb, up_gb, down_gb, grad_input)
+    )
+    near = jnp.stack([jnp.where(y_first, own, other), jnp.where(y_first, other, own)])
+    far = swap(near, "seq", 1)
     down_at = OWNERS * narrow + SPARE
     qkv_ga, out_ga, up_ga, down_ga = finish(place, down_at, narrow, width, near, far)
     at = OWNERS * narrow // 2
     route = near[0, at, :narrow].astype(F32) + far[0, at, :narrow].astype(F32)
 
-    def gain_grad(found, weight, gain):
-        at = dp_at * narrow
-        weight = lax.dynamic_slice_in_dim(weight, at, narrow, axis=0).astype(F32)
-        gain = lax.dynamic_slice_in_dim(gain, at, narrow, axis=0).astype(F32)
-        return jnp.sum(found * weight, axis=1) / gain
-
     return (
         done_b.astype(BF16),
         grad_input,
         route,
-        gain_grad(qkv_ga, qkv_a, gain_a1),
+        gain_grad(qkv_ga, qkv_a, gains[0]),
         qkv_ga,
         out_ga,
-        gain_grad(up_ga, up_a, gain_a2),
+        gain_grad(up_ga, up_a, gains[1]),
         up_ga,
         down_ga,
-        gain_grad(qkv_gb, qkv_b, gain_b1),
+        gains_b[0],
         qkv_gb,
         out_gb,
-        gain_grad(up_gb, up_b, gain_b2),
+        gains_b[1],
         up_gb,
         down_gb,
     )

time: 395 us -> 363 us (0.919)
  waiting for transfers between devices: 102 us -> 77.5 us
  local copies, waits for them, and re-layouts: 37.7 us -> 26.8 us
  matrix products: 53.8 us -> 60.1 us
    ppermute x70 -> x68, waiting for transfers between devices: 102 us -> 77.5 us  [swap(): return lax.ppermute(x, axis, [(i, i ^ bit) for i in range(size)])]
    slice x6 -> x0, local copies, waits for them, and re-layouts: 8.12 us -> none  [halves(): return (unit[:n], unit[n:])]
    dot_general x0 -> x12, matrix products: none -> 5.66 us  [dot(): return lax.dot_general(left, right, dims, preferred_element_type=F32)]
    ppermute x70 -> x68, starting transfers between devices: 57.7 us -> 55 us  [swap(): return lax.ppermute(x, axis, [(i, i ^ bit) for i in range(size)])]
    convert_element_type x17 -> x18, other arithmetic: 11.6 us -> 12.9 us  [add_low(): return (a.astype(F32) + b.astype(F32)).astype(BF16)]
    dot_general x9 -> x8, matrix products: 20.9 us -> 21.5 us  [project_back(): jnp.einsum('bne,de->bnd', gradient, weight, preferred_element_type=F32)]
    unnamed x227 -> x229, local copies, waits for them, and re-layouts: 10.7 us -> 11.3 us
  transfers between devices with their start and end apart: 70 -> 68, of which waited for: 19 -> 26; matrix products, arithmetic and copies ran while one was open for 28% -> 29% of each run, Pallas kernels for 19% -> 20%
where the time goes in v4:
time: 363 us; the launch traced here: 358 us
  Pallas kernels  95 us (26%)
  waiting for transfers between devices  77.5 us (21%)
  matrix products  60.1 us (17%)
  starting transfers between devices  55 us (15%)
  other arithmetic  40.2 us (11%)
  local copies, waits for them, and re-layouts  26.8 us (7%)
    ppermute x68, waiting for transfers between devices, swap(): return lax.ppermute(x, axis, [(i, i ^ bit) for i in range(size)])  77.5 us
    ppermute x68, starting transfers between devices, swap(): return lax.ppermute(x, axis, [(i, i ^ bit) for i in range(size)])  55 us
    dot_general x6, matrix products, project(): jnp.einsum('bnd,de->bne', left_side, weight, preferred_element_type=F32)  24.2 us
    pallas_call x2, Pallas kernels, feed_grad(): pl.pallas_call(lambda *refs: feed_grad_kernel(bits, orders, routed, *refs...  22.9 us
    pallas_call x2, Pallas kernels, attend_back(): pl.pallas_call(lambda *refs: attend_back_kernel(rows, routed, *refs), nam...  21.9 us
    dot_general x8, matrix products, project_back(): jnp.einsum('bne,de->bnd', gradient, weight, preferred_element_type=F32)  21.5 us
    pallas_call x2, Pallas kernels, attend(): pl.pallas_call(lambda *refs: attend_kernel(rows, routed, *refs), name='at...  17.5 us
    pallas_call x3, Pallas kernels, project_pieces(): pl.pallas_call(lambda *refs: project_kernel(tagged, *refs), name='project...  15.3 us
  transfers between devices with their start and end apart: 68, of which 26 were waited for; matrix products, arithmetic and copies ran while one was open for 29% of the time, Pallas kernels for 20%

profile of v4, /device:TPU:0, one launch (start us, length us, event | category | flops | bytes accessed | tf_op | source)
XLA Modules:
  0.0 357.6 jit_solution(15284440858746350336)
XLA Ops:
  0.7 2.2 fusion.203
  3.5 4.2 %project_pieces.3 = (bf16[2,64,768]{2,1,0:T(8,128)(2,1)}, bf16[3,64,384]{2,1,0:T(8,128)(2,1)}, bf16[3,64,384]{2,1,0:T(8,128)(2,1)}, bf16[3,64,384]{2,1,0:T(8,128)(2,1)}, bf16[3,64,384]{2,1,0:T(8,128)(2,1)}) custom-call(s32[5]{0:T(128)} %stack.88.refs_0_, bf16[2,64,768]{2,1,0:T(8,128)(2,1)} %get-tuple-element.505.refs_1_, bf16[768]{0:T(1024)(128)(2,1)} %refs_2_.3, ...), custom_call_target="tpu_custom_call" | custom-call | flops 452984832 | bytes 4718592 | tf_op jit(solution)/shard_map/project_pieces/pallas_call | solution.py:59
  8.2 2.5 collective-permute-start.1
  11.5 6.8 %project_pieces.4 = (bf16[2,256,768]{2,1,0:T(8,128)(2,1)}, bf16[3,272,384]{2,1,0:T(8,128)(2,1)}, bf16[3,272,384]{2,1,0:T(8,128)(2,1)}, bf16[3,272,384]{2,1,0:T(8,128)(2,1)}, bf16[3,272,384]{2,1,0:T(8,128)(2,1)}) custom-call(s32[5]{0:T(128)} %stack.88.refs_0_, bf16[2,256,768]{2,1,0:T(8,128)(2,1)} %refs_1_.1, bf16[768]{0:T(1024)(128)(2,1)} %refs_2_.5, ...), custom_call_target="tpu_custom_call" | custom-call | flops 1811939328 | bytes 8257536 | tf_op jit(solution)/shard_map/project_pieces/pallas_call | solution.py:59
  18.3 1.8 collective-permute-start.14
  23.9 4.6 %attend_routed.1 = (bf16[64,384]{1,0:T(8,128)(2,1)}, bf16[64,384]{1,0:T(8,128)(2,1)}, bf16[64,384]{1,0:T(8,128)(2,1)}, bf16[64,384]{1,0:T(8,128)(2,1)}, bf16[3,2...) custom-call(s32[5]{0:T(128)} %stack.88.refs_0_, s32[4]{0:T(128)} %fusion.195.refs_1_, ...), custom_call_target="tpu_custom_call" | custom-call | flops 402653184 | bytes 1572864 | tf_op jit(solution)/shard_map/attend_routed/pallas_call | solution.py:179
  33.2 3.2 collective-permute-done.4
  40.5 4.9 %multiply_convert_fusion.2 = (bf16[2,64,3072]{2,1,0:T(8,128)(2,1)S(1)}, f32[2,64,3072]{2,1,0:T(8,128)}) fusion(bf16[2,64,768]{2,1,0:T(8,128)(2,1)S(1)} %multiply_convert_fusion.4, bf16[768,3072]{1,0:T(8,128)(2,1)} %param.25), kind=kOutput, calls=%fused_computation.52 | convolution fusion | flops 607518720 | bytes 7274496 | tf_op jit(solution)/shard_map/bnd,de->bne/dot_general | solution.py:603
  50.3 2.4 collective-permute-done.6.refs_6_
  54.4 4.2 %project_pieces.5 = (bf16[2,64,768]{2,1,0:T(8,128)(2,1)}, bf16[3,64,384]{2,1,0:T(8,128)(2,1)}, bf16[3,64,384]{2,1,0:T(8,128)(2,1)}, bf16[3,64,384]{2,1,0:T(8,128)(2,1)}, bf16[3,64,384]{2,1,0:T(8,128)(2,1)}) custom-call(s32[5]{0:T(128)} %stack.88.refs_0_, f32[2,64,768]{2,1,0:T(8,128)} %get-tuple-element.223.refs_1_, bf16[768]{0:T(1024)(128)(2,1)} %refs_2_.5, ...), custom_call_target="tpu_custom_call" | custom-call | flops 452984832 | bytes 4718592 | tf_op jit(solution)/shard_map/project_pieces/pallas_call | solution.py:59
  61.4 1.8 select_convert_fusion
  67.7 12.9 %attend_dense.1 = (bf16[256,384]{1,0:T(8,128)(2,1)}, bf16[256,384]{1,0:T(8,128)(2,1)}, bf16[256,384]{1,0:T(8,128)(2,1)}, bf16[256,384]{1,0:T(8,128)(2,1)}, bf16[...) custom-call(s32[5]{0:T(128)} %stack.88.refs_0_, s32[4]{0:T(128)} %fusion.195.refs_1_, ...), custom_call_target="tpu_custom_call" | custom-call | flops 4026531840 | bytes 6291456 | tf_op jit(solution)/shard_map/attend_dense/pallas_call | solution.py:179
  80.6 1.8 collective-permute-start.16
  88.6 3.6 collective-permute-done.17
  93.6 9.8 %multiply_convert_fusion = (bf16[2,256,3072]{2,1,0:T(8,128)(2,1)S(1)}, f32[2,256,3072]{2,1,0:T(8,128)}) fusion(bf16[2,256,768]{2,1,0:T(8,128)(2,1)S(1)} %multiply_convert_fusion.1, bf16[768,3072]{1,0:T(8,128)(2,1)} %param.31), kind=kOutput, calls=%fused_computation.9 | convolution fusion | flops 2430074880 | bytes 14942208 | tf_op jit(solution)/shard_map/bnd,de->bne/dot_general | solution.py:603
  103.9 8.4 %fusion.6 = bf16[2,256,3072]{2,1,0:T(8,128)(2,1)S(1)} fusion(f32[2,256,3072]{2,1,0:T(8,128)} %get-tuple-element.517, bf16[2,256,768]{2,1,0:T(8,128)(2,1)S(1)} %copy-done.24, bf16[3072,768]{1,0:T(8,128)(2,1)S(1)} %bitcast.322), kind=kOutput, calls=%fused_computation.8 | convolution fusion | flops 2447376384 | bytes 14942208 | tf_op jit(solution)/shard_map/bne,de->bnd/dot_general | solution.py:607
  114.0 2.7 multiply_reduce_fusion.2
  127.3 15.5 %feed_grad.2 = (bf16[8,192,384]{2,1,0:T(8,128)(2,1)}, bf16[8,192,384]{2,1,0:T(8,128)(2,1)}, bf16[8,240,384]{2,1,0:T(8,128)(2,1)}, bf16[8,240,384]{2,1,0:T(8,128)(2,1)}) custom-call(s32[5]{0:T(128)} %stack.88.refs_0_, bf16[512,768]{1,0:T(8,128)(2,1)} %bitcast.309, bf16[512,768]{1,0:T(8,128)(2,1)} %copy-done.82, bf16[512,3072]{1,0:T(8,128)(2,1)} %bitcast.324, ...), custom_call_target="tpu_custom_call" | custom-call | flops 5435817984 | bytes 21037056 | tf_op jit(solution)/shard_map/feed_grad/pallas_call | solution.py:397
  146.1 2.1 slice_bitcast_fusion.2
  148.2 17.7 %attend_dense_back.1 = (bf16[3,256,384]{2,1,0:T(8,128)(2,1)}, bf16[3,256,384]{2,1,0:T(8,128)(2,1)}, bf16[3,256,384]{2,1,0:T(8,128)(2,1)}, bf16[3,256,384]{2,1,0:...) custom-call(s32[5]{0:T(128)} %stack.88.refs_0_, ...), custom_call_target="tpu_custom_call" | custom-call | flops 10066329600 | bytes 6291456 | tf_op jit(solution)/shard_map/attend_dense_back/pallas_call | solution.py:279
  167.8 6.0 %qkv_grad.2 = (bf16[8,144,384]{2,1,0:T(8,128)(2,1)}, bf16[8,144,384]{2,1,0:T(8,128)(2,1)}) custom-call(s32[5]{0:T(128)} %stack.88.refs_0_, bf16[256,768]{1,0:T(8,128)(2,1)} %slice.348.refs_1_, bf16[256,768]{1,0:T(8,128)(2,1)} %get-tuple-element.438.refs_2_, bf16[256,768]{1,0:T(8,128)(2,1)} %slice.453.refs_3_, bf16[256,768]{1,0:T(8,128)(2,1)} %get-tuple-element.437.refs_4_, ...), custom_call_target="tpu_custom_call" | custom-call | flops 1811939328 | bytes 5701632 | tf_op jit(solution)/shard_map/qkv_grad/pallas_call | solution.py:430
  175.5 3.3 collective-permute-done.28
  186.1 4.5 %fusion.35 = bf16[2,64,3072]{2,1,0:T(8,128)(2,1)S(1)} fusion(f32[2,64,3072]{2,1,0:T(8,128)S(1)} %copy-done.105, bf16[2,64,768]{2,1,0:T(8,128)(2,1)S(1)} %get-tuple-element.519, bf16[3072,768]{1,0:T(8,128)(2,1)} %param.26), kind=kOutput, calls=%fused_computation.40 | convolution fusion | flops 611844096 | bytes 7274496 | tf_op jit(solution)/shard_map/bne,de->bnd/dot_general | solution.py:607
  190.6 2.9 collective-permute-done.34
  193.7 4.2 %collective-permute-done.35 = bf16[4,240,384]{2,1,0:T(8,128)(2,1)S(1)} collective-permute-done((bf16[4,240,384]{2,1,0:T(8,128)(2,1)S(1)}, bf16[4,240,384]{2,1,0:T(8,128)(2,1)S(1)}, u32[]{:S(2)}, u32[]{:S(2)}) %collective-permute-start.35) | collective-permute-done | bytes 737312 | tf_op jit(solution)/shard_map/ppermute | solution.py:483
  211.7 7.3 %feed_grad.3 = (bf16[8,208,384]{2,1,0:T(8,128)(2,1)}, bf16[8,208,384]{2,1,0:T(8,128)(2,1)}, bf16[8,240,384]{2,1,0:T(8,128)(2,1)}, bf16[8,240,384]{2,1,0:T(8,128)(2,1)}) custom-call(s32[5]{0:T(128)} %stack.88.refs_0_, bf16[128,768]{1,0:T(8,128)(2,1)} %bitcast.315, bf16[128,768]{1,0:T(8,128)(2,1)} %copy-done.89, bf16[128,3072]{1,0:T(8,128)(2,1)} %bitcast.303, ...), custom_call_target="tpu_custom_call" | custom-call | flops 1358954496 | bytes 9240576 | tf_op jit(solution)/shard_map/feed_grad/pallas_call | solution.py:397
  220.1 2.5 add_convert_fusion.11
  226.3 4.3 %attend_routed_back.1 = (bf16[3,64,384]{2,1,0:T(8,128)(2,1)}, bf16[3,64,384]{2,1,0:T(8,128)(2,1)}, bf16[3,64,384]{2,1,0:T(8,128)(2,1)}, bf16[3,64,384]{2,1,0:T(8,128)(2,1)}) custom-call(s32[5]{0:T(128)} %stack.88.refs_0_, s32[4]{0:T(128)} %fusion.195.refs_1_, bf16[3,256,384]{2,1,0:T(8,128)(2,1)} %get-tuple-element.313.refs_2_, ...), custom_call_target="tpu_custom_call" | custom-call | flops 1006632960 | bytes 1572864 | tf_op jit(solution)/shard_map/attend_routed_back/pallas_call | solution.py:279
  230.6 1.8 pad_maximum_fusion.9
  232.4 1.9 collective-permute-done.47
  234.3 2.1 add_convert_fusion.24
  239.1 4.6 %qkv_grad.3 = (bf16[8,144,384]{2,1,0:T(8,128)(2,1)}, bf16[8,144,384]{2,1,0:T(8,128)(2,1)}) custom-call(s32[5]{0:T(128)} %stack.88.refs_0_, bf16[64,768]{1,0:T(8,128)(2,1)} %slice.385.refs_1_, bf16[64,768]{1,0:T(8,128)(2,1)} %get-tuple-element.436.refs_2_, bf16[64,768]{1,0:T(8,128)(2,1)} %slice.474.refs_3_, bf16[64,768]{1,0:T(8,128)(2,1)} %get-tuple-element.435.refs_4_, ...), custom_call_target="tpu_custom_call" | custom-call | flops 452984832 | bytes 2752512 | tf_op jit(solution)/shard_map/qkv_grad/pallas_call | solution.py:430
  243.7 2.1 collective-permute-done.50
  257.2 5.9 %fusion.44 = bf16[2,256,768]{2,1,0:T(8,128)(2,1)} fusion(f32[2,256,768]{2,1,0:T(8,128)S(1)} %copy-done.8, bf16[2,256,3072]{2,1,0:T(8,128)(2,1)S(1)} %copy-done.79, bf16[3072,768]{1,0:T(8,128)(2,1)} %param.32), kind=kOutput, calls=%fused_computation.59 | convolution fusion | flops 2416705536 | bytes 10223616 | tf_op jit(solution)/shard_map/bnd,de->bne/dot_general | solution.py:603
  270.9 2.6 collective-permute-start.62
  277.5 6.9 %collective-permute-done.63 = bf16[2,144,384]{2,1,0:T(8,128)(2,1)S(1)} collective-permute-done((bf16[2,144,384]{2,1,0:T(8,128)(2,1)S(1)}, bf16[2,144,384]{2,1,0:T(8,128)(2,1)S(1)}, u32[]{:S(2)}, u32[]{:S(2)}) %collective-permute-start.63) | collective-permute-done | bytes 221216 | tf_op jit(solution)/shard_map/ppermute | solution.py:483
  284.6 4.2 %collective-permute-done.62 = bf16[1,432,384]{2,1,0:T(8,128)(2,1)S(1)} collective-permute-done((bf16[1,432,384]{2,1,0:T(8,128)(2,1)S(1)}, bf16[1,432,384]{2,1,0:T(8,128)(2,1)S(1)}, u32[]{:S(2)}, u32[]{:S(2)}) %collective-permute-start.62) | collective-permute-done | bytes 331808 | tf_op jit(solution)/shard_map/ppermute | solution.py:483
  288.8 5.8 %collective-permute-done.55 = bf16[4,144,384]{2,1,0:T(8,128)(2,1)S(1)} collective-permute-done((bf16[4,144,384]{2,1,0:T(8,128)(2,1)S(1)}, bf16[4,144,384]{2,1,0:T(8,128)(2,1)S(1)}, u32[]{:S(2)}, u32[]{:S(2)}) %collective-permute-start.55) | collective-permute-done | bytes 442400 | tf_op jit(solution)/shard_map/ppermute | solution.py:483
  295.1 2.7 collective-permute-start.64
  300.6 2.2 collective-permute-done.64
  305.1 3.3 collective-permute-done.56
  311.6 7.7 %collective-permute-done.65 = bf16[576,384]{1,0:T(8,128)(2,1)S(1)} collective-permute-done((bf16[576,384]{1,0:T(8,128)(2,1)S(1)}, bf16[576,384]{1,0:T(8,128)(2,1)S(1)}, u32[]{:S(2)}, u32[]{:S(2)}) %collective-permute-start.65) | collective-permute-done | bytes 442400 | tf_op jit(solution)/shard_map/ppermute | solution.py:483
  319.6 5.8 %collective-permute-done.59 = bf16[256,768]{1,0:T(8,128)(2,1)S(1)} collective-permute-done((bf16[256,768]{1,0:T(8,128)(2,1)S(1)}, bf16[256,768]{1,0:T(8,128)(2,1)S(1)}, u32[]{:S(2)}, u32[]{:S(2)}) %collective-permute-start.59) | collective-permute-done | bytes 393248 | tf_op jit(solution)/shard_map/ppermute | solution.py:483
  326.0 5.1 %collective-permute-done.60 = bf16[1,592,384]{2,1,0:T(8,128)(2,1)S(1)} collective-permute-done((bf16[1,592,384]{2,1,0:T(8,128)(2,1)S(1)}, bf16[1,592,384]{2,1,0:T(8,128)(2,1)S(1)}, u32[]{:S(2)}, u32[]{:S(2)}) %collective-permute-start.60) | collective-permute-done | bytes 454688 | tf_op jit(solution)/shard_map/ppermute | solution.py:483
  332.6 2.5 fusion.38
  335.0 3.4 finish_grads.2
  345.1 2.4 collective-permute-done.67.refs_2_
  348.5 3.5 finish_grads.3
  (478 shorter events, 130.0 us)
Async XLA Ops:
  7.7 15.4 %collective-permute-start = (bf16[3,64,384]{2,1,0:T(8,128)(2,1)}, bf16[3,64,384]{2,1,0:T(8,128)(2,1)S(1)}, u32[]{:S(2)}, u32[]{:S(2)}) collective-permute-start(bf16[3,64,384]{2,1,0:T(8,128)(2,1)} %get-tuple-element.209), channel_id=1, source_target_pairs={{0,1},{1,0},{2,3},{3,2},{4,5},{5,4},{6,7},{7,6},{8,9},{9,8},{10,11... | collective-permute-start | bytes 442376 | tf_op jit(solution)/shard_map/ppermute | solution.py:483
  8.2 14.9 %collective-permute-start.1 = (bf16[3,64,384]{2,1,0:T(8,128)(2,1)}, bf16[3,64,384]{2,1,0:T(8,128)(2,1)S(1)}, u32[]{:S(2)}, u32[]{:S(2)}) collective-permute-start(bf16[3,64,384]{2,1,0:T(8,128)(2,1)} %get-tuple-element.210), channel_id=1, source_target_pairs={{0,2},{1,3},{2,0},{3,1},{4,6},{5,7},{6,4},{7,5},{8,10},{9,11},{10,... | collective-permute-start | bytes 442376 | tf_op jit(solution)/shard_map/ppermute | solution.py:483
  10.7 12.5 %collective-permute-start.2 = (bf16[3,64,384]{2,1,0:T(8,128)(2,1)}, bf16[3,64,384]{2,1,0:T(8,128)(2,1)S(1)}, u32[]{:S(2)}, u32[]{:S(2)}) collective-permute-start(bf16[3,64,384]{2,1,0:T(8,128)(2,1)} %get-tuple-element.211), channel_id=1, source_target_pairs={{0,3},{1,2},{2,1},{3,0},{4,7},{5,6},{6,5},{7,4},{8,11},{9,10},{10,... | collective-permute-start | bytes 442376 | tf_op jit(solution)/shard_map/ppermute | solution.py:483
  18.3 30.4 %collective-permute-start.14 = (bf16[3,272,384]{2,1,0:T(8,128)(2,1)}, bf16[3,272,384]{2,1,0:T(8,128)(2,1)}, u32[]{:S(2)}, u32[]{:S(2)}) collective-permute-start(bf16[3,272,384]{2,1,0:T(8,128)(2,1)} %get-tuple-element.234), channel_id=1, source_target_pairs={{0,2},{1,3},{2,0},{3,1},{4,6},{5,7},{6,4},{7,5},{8,10},{9,11},{10,... | collective-permute-start | bytes 1880072 | tf_op jit(solution)/shard_map/ppermute | solution.py:483
  28.5 7.9 %collective-permute-start.4 = (bf16[64,384]{1,0:T(8,128)(2,1)}, bf16[64,384]{1,0:T(8,128)(2,1)S(1)}, u32[]{:S(2)}, u32[]{:S(2)}) collective-permute-start(bf16[64,384]{1,0:T(8,128)(2,1)} %get-tuple-element.214), channel_id=1, source_target_pairs={{0,2},{1,3},{2,0},{3,1},{4,6},{5,7},{6,4},{7,5},{8,10},{9,11},{10,... | collective-permute-start | bytes 147464 | tf_op jit(solution)/shard_map/ppermute | solution.py:483
  36.4 16.2 %collective-permute-start.6 = (bf16[3,272,384]{2,1,0:T(8,128)(2,1)}, bf16[3,272,384]{2,1,0:T(8,128)(2,1)S(1)}, u32[]{:S(2)}, u32[]{:S(2)}) collective-permute-start(bf16[3,272,384]{2,1,0:T(8,128)(2,1)} %get-tuple-element.218), channel_id=1, source_target_pairs={{0,3},{1,2},{2,1},{3,0},{4,7},{5,6},{6,5},{7,4},{8,11},{9,10},{10,... | collective-permute-start | bytes 1880072 | tf_op jit(solution)/shard_map/ppermute | solution.py:483
  40.3 9.6 %collective-permute-start.7 = (bf16[128,768]{1,0:T(8,128)(2,1)S(1)}, bf16[128,768]{1,0:T(8,128)(2,1)S(1)}, u32[]{:S(2)}, u32[]{:S(2)}) collective-permute-start(bf16[128,768]{1,0:T(8,128)(2,1)S(1)} %bitcast.314), channel_id=1, source_target_pairs={{0,1},{1,0},{2,3},{3,2},{4,5},{5,4},{6,7},{7,6},{8,9},{9,8},{10,11... | collective-permute-start | bytes 589832 | tf_op jit(solution)/shard_map/ppermute | solution.py:483
  80.6 8.0 %collective-permute-start.16 = (bf16[256,384]{1,0:T(8,128)(2,1)}, bf16[256,384]{1,0:T(8,128)(2,1)S(1)}, u32[]{:S(2)}, u32[]{:S(2)}) collective-permute-start(bf16[256,384]{1,0:T(8,128)(2,1)} %get-tuple-element.242), channel_id=1, source_target_pairs={{0,2},{1,3},{2,0},{3,1},{4,6},{5,7},{6,4},{7,5},{8,10},{9,11},{10,... | collective-permute-start | bytes 589832 | tf_op jit(solution)/shard_map/ppermute | solution.py:483
  82.4 9.7 %collective-permute-start.17 = (bf16[256,384]{1,0:T(8,128)(2,1)}, bf16[256,384]{1,0:T(8,128)(2,1)S(1)}, u32[]{:S(2)}, u32[]{:S(2)}) collective-permute-start(bf16[256,384]{1,0:T(8,128)(2,1)} %get-tuple-element.243), channel_id=1, source_target_pairs={{0,3},{1,2},{2,1},{3,0},{4,7},{5,6},{6,5},{7,4},{8,11},{9,10},{10,... | collective-permute-start | bytes 589832 | tf_op jit(solution)/shard_map/ppermute | solution.py:483
  85.9 33.3 %collective-permute-start.32 = (bf16[320,768]{1,0:T(8,128)(2,1)S(1)}, bf16[320,768]{1,0:T(8,128)(2,1)S(1)}, u32[]{:S(2)}, u32[]{:S(2)}) collective-permute-start(bf16[320,768]{1,0:T(8,128)(2,1)S(1)} %copy-done.48), channel_id=1, source_target_pairs={{0,2},{1,3},{2,0},{3,1},{4,6},{5,7},{6,4},{7,5},{8,10},{9,11},{10,... | collective-permute-start | bytes 1474568 | tf_op jit(solution)/shard_map/ppermute | solution.py:483
  103.5 21.2 %collective-permute-start.19 = (bf16[512,3072]{1,0:T(8,128)(2,1)S(1)}, bf16[512,3072]{1,0:T(8,128)(2,1)S(1)}, u32[]{:S(2)}, u32[]{:S(2)}) collective-permute-start(bf16[512,3072]{1,0:T(8,128)(2,1)S(1)} %bitcast.323), channel_id=1, source_target_pairs={{0,1},{1,0},{2,3},{3,2},{4,5},{5,4},{6,7},{7,6},{8,9},{9,8},{10,11... | collective-permute-start | bytes 9437192 | tf_op jit(solution)/shard_map/ppermute | solution.py:483
  112.5 14.9 %collective-permute-start.24 = (bf16[512,1536]{1,0:T(8,128)(2,1)S(1)}, bf16[512,1536]{1,0:T(8,128)(2,1)}, u32[]{:S(2)}, u32[]{:S(2)}) collective-permute-start(bf16[512,1536]{1,0:T(8,128)(2,1)S(1)} %constant_dynamic-slice_fusion.5), channel_id=1, source_target_pairs={{0,1},{1,0},{2,3},{3,2},{4,5},{5,4},{6,7},{7,6},{8,9},{9,8},{10,11... | collective-permute-start | bytes 4718600 | tf_op jit(solution)/shard_map/ppermute | solution.py:483
  120.3 25.8 %collective-permute-start.33 = (bf16[2,320,768]{2,1,0:T(8,128)(2,1)}, bf16[2,320,768]{2,1,0:T(8,128)(2,1)}, u32[]{:S(2)}, u32[]{:S(2)}) collective-permute-start(bf16[2,320,768]{2,1,0:T(8,128)(2,1)} %pad_maximum_fusion), channel_id=1, source_target_pairs={{0,1},{1,0},{2,3},{3,2},{4,5},{5,4},{6,7},{7,6},{8,9},{9,8},{10,11... | collective-permute-start | bytes 2949128 | tf_op jit(solution)/shard_map/ppermute | solution.py:483
  124.7 18.2 %collective-permute-start.21 = (bf16[256,384]{1,0:T(8,128)(2,1)S(1)}, bf16[256,384]{1,0:T(8,128)(2,1)S(1)}, u32[]{:S(2)}, u32[]{:S(2)}) collective-permute-start(bf16[256,384]{1,0:T(8,128)(2,1)S(1)} %get-tuple-element.245), channel_id=1, source_target_pairs={{0,1},{1,0},{2,3},{3,2},{4,5},{5,4},{6,7},{7,6},{8,9},{9,8},{10,11... | collective-permute-start | bytes 589832 | tf_op jit(solution)/shard_map/ppermute | solution.py:483
  124.8 18.1 %collective-permute-start.22 = (bf16[256,384]{1,0:T(8,128)(2,1)S(1)}, bf16[256,384]{1,0:T(8,128)(2,1)S(1)}, u32[]{:S(2)}, u32[]{:S(2)}) collective-permute-start(bf16[256,384]{1,0:T(8,128)(2,1)S(1)} %get-tuple-element.246), channel_id=1, source_target_pairs={{0,2},{1,3},{2,0},{3,1},{4,6},{5,7},{6,4},{7,5},{8,10},{9,11},{10,... | collective-permute-start | bytes 589832 | tf_op jit(solution)/shard_map/ppermute | solution.py:483
  126.6 16.4 %collective-permute-start.23 = (bf16[256,384]{1,0:T(8,128)(2,1)S(1)}, bf16[256,384]{1,0:T(8,128)(2,1)S(1)}, u32[]{:S(2)}, u32[]{:S(2)}) collective-permute-start(bf16[256,384]{1,0:T(8,128)(2,1)S(1)} %get-tuple-element.247), channel_id=1, source_target_pairs={{0,3},{1,2},{2,1},{3,0},{4,7},{5,6},{6,5},{7,4},{8,11},{9,10},{10,... | collective-permute-start | bytes 589832 | tf_op jit(solution)/shard_map/ppermute | solution.py:483
  142.9 30.9 %collective-permute-start.27 = (bf16[8,192,384]{2,1,0:T(8,128)(2,1)}, bf16[8,192,384]{2,1,0:T(8,128)(2,1)}, u32[]{:S(2)}, u32[]{:S(2)}) collective-permute-start(bf16[8,192,384]{2,1,0:T(8,128)(2,1)} %get-tuple-element.259), channel_id=1, source_target_pairs={{0,4},{4,0},{8,12},{12,8},{16,20},{20,16},{24,28},{28,24},{1,5},{5... | collective-permute-start | bytes 3538952 | tf_op jit(solution)/shard_map/ppermute | solution.py:483
  144.5 34.3 %collective-permute-start.28 = (bf16[8,240,384]{2,1,0:T(8,128)(2,1)}, bf16[8,240,384]{2,1,0:T(8,128)(2,1)S(1)}, u32[]{:S(2)}, u32[]{:S(2)}) collective-permute-start(bf16[8,240,384]{2,1,0:T(8,128)(2,1)} %get-tuple-element.261), channel_id=1, source_target_pairs={{0,8},{4,12},{8,0},{12,4},{16,24},{20,28},{24,16},{28,20},{1,9},{5... | collective-permute-start | bytes 4423688 | tf_op jit(solution)/shard_map/ppermute | solution.py:483
  165.9 13.3 %collective-permute-start.29 = (bf16[3,64,384]{2,1,0:T(8,128)(2,1)}, bf16[3,64,384]{2,1,0:T(8,128)(2,1)S(1)}, u32[]{:S(2)}, u32[]{:S(2)}) collective-permute-start(bf16[3,64,384]{2,1,0:T(8,128)(2,1)} %get-tuple-element.270), channel_id=1, source_target_pairs={{0,1},{1,0},{2,3},{3,2},{4,5},{5,4},{6,7},{7,6},{8,9},{9,8},{10,11... | collective-permute-start | bytes 442376 | tf_op jit(solution)/shard_map/ppermute | solution.py:483
  165.9 13.3 %collective-permute-start.30 = (bf16[3,64,384]{2,1,0:T(8,128)(2,1)}, bf16[3,64,384]{2,1,0:T(8,128)(2,1)S(1)}, u32[]{:S(2)}, u32[]{:S(2)}) collective-permute-start(bf16[3,64,384]{2,1,0:T(8,128)(2,1)} %get-tuple-element.271), channel_id=1, source_target_pairs={{0,2},{1,3},{2,0},{3,1},{4,6},{5,7},{6,4},{7,5},{8,10},{9,11},{10,... | collective-permute-start | bytes 442376 | tf_op jit(solution)/shard_map/ppermute | solution.py:483
  167.1 12.1 %collective-permute-start.31 = (bf16[3,64,384]{2,1,0:T(8,128)(2,1)}, bf16[3,64,384]{2,1,0:T(8,128)(2,1)S(1)}, u32[]{:S(2)}, u32[]{:S(2)}) collective-permute-start(bf16[3,64,384]{2,1,0:T(8,128)(2,1)} %get-tuple-element.272), channel_id=1, source_target_pairs={{0,3},{1,2},{2,1},{3,0},{4,7},{5,6},{6,5},{7,4},{8,11},{9,10},{10,... | collective-permute-start | bytes 442376 | tf_op jit(solution)/shard_map/ppermute | solution.py:483
  179.2 14.3 %collective-permute-start.34 = (bf16[4,192,384]{2,1,0:T(8,128)(2,1)S(1)}, bf16[4,192,384]{2,1,0:T(8,128)(2,1)S(1)}, u32[]{:S(2)}, u32[]{:S(2)}) collective-permute-start(bf16[4,192,384]{2,1,0:T(8,128)(2,1)S(1)} %get-tuple-element.282), channel_id=1, source_target_pairs={{0,2},{1,3},{2,0},{3,1},{4,6},{5,7},{6,4},{7,5},{8,10},{9,11},{10,... | collective-permute-start | bytes 1769480 | tf_op jit(solution)/shard_map/ppermute | solution.py:483
  180.6 17.4 %collective-permute-start.35 = (bf16[4,240,384]{2,1,0:T(8,128)(2,1)S(1)}, bf16[4,240,384]{2,1,0:T(8,128)(2,1)S(1)}, u32[]{:S(2)}, u32[]{:S(2)}) collective-permute-start(bf16[4,240,384]{2,1,0:T(8,128)(2,1)S(1)} %get-tuple-element.284), channel_id=1, source_target_pairs={{0,4},{4,0},{8,12},{12,8},{16,20},{20,16},{24,28},{28,24},{1,5},{5... | collective-permute-start | bytes 2211848 | tf_op jit(solution)/shard_map/ppermute | solution.py:483
  185.5 23.7 %collective-permute-start.43 = (bf16[128,384]{1,0:T(8,128)(2,1)S(1)}, bf16[128,384]{1,0:T(8,128)(2,1)S(1)}, u32[]{:S(2)}, u32[]{:S(2)}) collective-permute-start(bf16[128,384]{1,0:T(8,128)(2,1)S(1)} %constant_dynamic-slice_fusion.1), channel_id=1, source_target_pairs={{0,1},{1,0},{2,3},{3,2},{4,5},{5,4},{6,7},{7,6},{8,9},{9,8},{10,11... | collective-permute-start | bytes 294920 | tf_op jit(solution)/shard_map/ppermute | solution.py:483
  198.1 8.9 %collective-permute-start.36 = (bf16[2,192,384]{2,1,0:T(8,128)(2,1)S(1)}, bf16[2,192,384]{2,1,0:T(8,128)(2,1)S(1)}, u32[]{:S(2)}, u32[]{:S(2)}) collective-permute-start(bf16[2,192,384]{2,1,0:T(8,128)(2,1)S(1)} %get-tuple-element.290), channel_id=1, source_target_pairs={{0,8},{4,12},{8,0},{12,4},{16,24},{20,28},{24,16},{28,20},{1,9},{5... | collective-permute-start | bytes 884744 | tf_op jit(solution)/shard_map/ppermute | solution.py:483
  199.7 8.6 %collective-permute-start.37 = (bf16[2,240,384]{2,1,0:T(8,128)(2,1)S(1)}, bf16[2,240,384]{2,1,0:T(8,128)(2,1)S(1)}, u32[]{:S(2)}, u32[]{:S(2)}) collective-permute-start(bf16[2,240,384]{2,1,0:T(8,128)(2,1)S(1)} %get-tuple-element.292), channel_id=1, source_target_pairs={{0,2},{1,3},{2,0},{3,1},{4,6},{5,7},{6,4},{7,5},{8,10},{9,11},{10,... | collective-permute-start | bytes 1105928 | tf_op jit(solution)/shard_map/ppermute | solution.py:483
  200.6 19.4 %collective-permute-start.38 = (bf16[8,144,384]{2,1,0:T(8,128)(2,1)}, bf16[8,144,384]{2,1,0:T(8,128)(2,1)}, u32[]{:S(2)}, u32[]{:S(2)}) collective-permute-start(bf16[8,144,384]{2,1,0:T(8,128)(2,1)} %get-tuple-element.295), channel_id=1, source_target_pairs={{0,4},{4,0},{8,12},{12,8},{16,20},{20,16},{24,28},{28,24},{1,5},{5... | collective-permute-start | bytes 2654216 | tf_op jit(solution)/shard_map/ppermute | solution.py:483
  205.7 16.9 %collective-permute-start.39 = (bf16[64,384]{1,0:T(8,128)(2,1)}, bf16[64,384]{1,0:T(8,128)(2,1)}, u32[]{:S(2)}, u32[]{:S(2)}) collective-permute-start(bf16[64,384]{1,0:T(8,128)(2,1)} %get-tuple-element.491), channel_id=1, source_target_pairs={{0,1},{1,0},{2,3},{3,2},{4,5},{5,4},{6,7},{7,6},{8,9},{9,8},{10,11... | collective-permute-start | bytes 147464 | tf_op jit(solution)/shard_map/ppermute | solution.py:483
  209.2 13.5 %collective-permute-start.40 = (bf16[64,384]{1,0:T(8,128)(2,1)}, bf16[64,384]{1,0:T(8,128)(2,1)}, u32[]{:S(2)}, u32[]{:S(2)}) collective-permute-start(bf16[64,384]{1,0:T(8,128)(2,1)} %get-tuple-element.490), channel_id=1, source_target_pairs={{0,2},{1,3},{2,0},{3,1},{4,6},{5,7},{6,4},{7,5},{8,10},{9,11},{10,... | collective-permute-start | bytes 147464 | tf_op jit(solution)/shard_map/ppermute | solution.py:483
  210.9 11.7 %collective-permute-start.41 = (bf16[64,384]{1,0:T(8,128)(2,1)}, bf16[64,384]{1,0:T(8,128)(2,1)}, u32[]{:S(2)}, u32[]{:S(2)}) collective-permute-start(bf16[64,384]{1,0:T(8,128)(2,1)} %get-tuple-element.489), channel_id=1, source_target_pairs={{0,3},{1,2},{2,1},{3,0},{4,7},{5,6},{6,5},{7,4},{8,11},{9,10},{10,... | collective-permute-start | bytes 147464 | tf_op jit(solution)/shard_map/ppermute | solution.py:483
  222.6 11.7 %collective-permute-start.47 = (bf16[4,144,384]{2,1,0:T(8,128)(2,1)}, bf16[4,144,384]{2,1,0:T(8,128)(2,1)}, u32[]{:S(2)}, u32[]{:S(2)}) collective-permute-start(bf16[4,144,384]{2,1,0:T(8,128)(2,1)} %get-tuple-element.312), channel_id=1, source_target_pairs={{0,2},{1,3},{2,0},{3,1},{4,6},{5,7},{6,4},{7,5},{8,10},{9,11},{10,... | collective-permute-start | bytes 1327112 | tf_op jit(solution)/shard_map/ppermute | solution.py:483
  225.4 38.5 %collective-permute-start.45 = (bf16[8,208,384]{2,1,0:T(8,128)(2,1)}, bf16[8,208,384]{2,1,0:T(8,128)(2,1)}, u32[]{:S(2)}, u32[]{:S(2)}) collective-permute-start(bf16[8,208,384]{2,1,0:T(8,128)(2,1)} %get-tuple-element.308), channel_id=1, source_target_pairs={{0,4},{4,0},{8,12},{12,8},{16,20},{20,16},{24,28},{28,24},{1,5},{5... | collective-permute-start | bytes 3833864 | tf_op jit(solution)/shard_map/ppermute | solution.py:483
  225.9 42.5 %collective-permute-start.46 = (bf16[8,240,384]{2,1,0:T(8,128)(2,1)}, bf16[8,240,384]{2,1,0:T(8,128)(2,1)}, u32[]{:S(2)}, u32[]{:S(2)}) collective-permute-start(bf16[8,240,384]{2,1,0:T(8,128)(2,1)} %get-tuple-element.310), channel_id=1, source_target_pairs={{0,8},{4,12},{8,0},{12,4},{16,24},{20,28},{24,16},{28,20},{1,9},{5... | collective-permute-start | bytes 4423688 | tf_op jit(solution)/shard_map/ppermute | solution.py:483
  237.6 8.2 %collective-permute-start.50 = (bf16[3,64,384]{2,1,0:T(8,128)(2,1)}, bf16[3,64,384]{2,1,0:T(8,128)(2,1)}, u32[]{:S(2)}, u32[]{:S(2)}) collective-permute-start(bf16[3,64,384]{2,1,0:T(8,128)(2,1)} %get-tuple-element.327.refs_8_), channel_id=1, source_target_pairs={{0,3},{1,2},{2,1},{3,0},{4,7},{5,6},{6,5},{7,4},{8,11},{9,10},{10,... | collective-permute-start | bytes 442376 | tf_op jit(solution)/shard_map/ppermute | solution.py:483
  245.8 22.3 %collective-permute-start.51 = (bf16[8,144,384]{2,1,0:T(8,128)(2,1)}, bf16[8,144,384]{2,1,0:T(8,128)(2,1)S(1)}, u32[]{:S(2)}, u32[]{:S(2)}) collective-permute-start(bf16[8,144,384]{2,1,0:T(8,128)(2,1)} %get-tuple-element.335), channel_id=1, source_target_pairs={{0,2},{1,3},{2,0},{3,1},{4,6},{5,7},{6,4},{7,5},{8,10},{9,11},{10,... | collective-permute-start | bytes 2654216 | tf_op jit(solution)/shard_map/ppermute | solution.py:483
  250.4 16.0 %collective-permute-start.52 = (bf16[2,256,768]{2,1,0:T(8,128)(2,1)S(1)}, bf16[2,256,768]{2,1,0:T(8,128)(2,1)S(1)}, u32[]{:S(2)}, u32[]{:S(2)}) collective-permute-start(bf16[2,256,768]{2,1,0:T(8,128)(2,1)S(1)} %pad_maximum_fusion.4), channel_id=1, source_target_pairs={{0,1},{1,0},{2,3},{3,2},{4,5},{5,4},{6,7},{7,6},{8,9},{9,8},{10,11... | collective-permute-start | bytes 2359304 | tf_op jit(solution)/shard_map/ppermute | solution.py:483
  270.4 14.1 %collective-permute-start.63 = (bf16[2,144,384]{2,1,0:T(8,128)(2,1)S(1)}, bf16[2,144,384]{2,1,0:T(8,128)(2,1)S(1)}, u32[]{:S(2)}, u32[]{:S(2)}) collective-permute-start(bf16[2,144,384]{2,1,0:T(8,128)(2,1)S(1)} %copy-done.51), channel_id=1, source_target_pairs={{0,8},{4,12},{8,0},{12,4},{16,24},{20,28},{24,16},{28,20},{1,9},{5... | collective-permute-start | bytes 663560 | tf_op jit(solution)/shard_map/ppermute | solution.py:483
  270.9 17.8 %collective-permute-start.62 = (bf16[1,432,384]{2,1,0:T(8,128)(2,1)S(1)}, bf16[1,432,384]{2,1,0:T(8,128)(2,1)S(1)}, u32[]{:S(2)}, u32[]{:S(2)}) collective-permute-start(bf16[1,432,384]{2,1,0:T(8,128)(2,1)S(1)} %copy-done.50), channel_id=1, source_target_pairs={{0,16},{4,20},{8,24},{12,28},{16,0},{20,4},{24,8},{28,12},{1,17},{... | collective-permute-start | bytes 995336 | tf_op jit(solution)/shard_map/ppermute | solution.py:483
  273.5 21.2 %collective-permute-start.53 = (bf16[4,208,384]{2,1,0:T(8,128)(2,1)S(1)}, bf16[4,208,384]{2,1,0:T(8,128)(2,1)S(1)}, u32[]{:S(2)}, u32[]{:S(2)}) collective-permute-start(bf16[4,208,384]{2,1,0:T(8,128)(2,1)S(1)} %get-tuple-element.359), channel_id=1, source_target_pairs={{0,2},{1,3},{2,0},{3,1},{4,6},{5,7},{6,4},{7,5},{8,10},{9,11},{10,... | collective-permute-start | bytes 1916936 | tf_op jit(solution)/shard_map/ppermute | solution.py:483
  274.5 20.4 %collective-permute-start.54 = (bf16[4,240,384]{2,1,0:T(8,128)(2,1)S(1)}, bf16[4,240,384]{2,1,0:T(8,128)(2,1)S(1)}, u32[]{:S(2)}, u32[]{:S(2)}) collective-permute-start(bf16[4,240,384]{2,1,0:T(8,128)(2,1)S(1)} %get-tuple-element.361), channel_id=1, source_target_pairs={{0,4},{4,0},{8,12},{12,8},{16,20},{20,16},{24,28},{28,24},{1,5},{5... | collective-permute-start | bytes 2211848 | tf_op jit(solution)/shard_map/ppermute | solution.py:483
  276.0 18.6 %collective-permute-start.55 = (bf16[4,144,384]{2,1,0:T(8,128)(2,1)S(1)}, bf16[4,144,384]{2,1,0:T(8,128)(2,1)S(1)}, u32[]{:S(2)}, u32[]{:S(2)}) collective-permute-start(bf16[4,144,384]{2,1,0:T(8,128)(2,1)S(1)} %get-tuple-element.363), channel_id=1, source_target_pairs={{0,8},{4,12},{8,0},{12,4},{16,24},{20,28},{24,16},{28,20},{1,9},{5... | collective-permute-start | bytes 1327112 | tf_op jit(solution)/shard_map/ppermute | solution.py:483
  297.8 10.6 %collective-permute-start.56 = (bf16[2,208,384]{2,1,0:T(8,128)(2,1)S(1)}, bf16[2,208,384]{2,1,0:T(8,128)(2,1)S(1)}, u32[]{:S(2)}, u32[]{:S(2)}) collective-permute-start(bf16[2,208,384]{2,1,0:T(8,128)(2,1)S(1)} %get-tuple-element.365), channel_id=1, source_target_pairs={{0,8},{4,12},{8,0},{12,4},{16,24},{20,28},{24,16},{28,20},{1,9},{5... | collective-permute-start | bytes 958472 | tf_op jit(solution)/shard_map/ppermute | solution.py:483
  298.2 11.5 %collective-permute-start.57 = (bf16[2,240,384]{2,1,0:T(8,128)(2,1)S(1)}, bf16[2,240,384]{2,1,0:T(8,128)(2,1)S(1)}, u32[]{:S(2)}, u32[]{:S(2)}) collective-permute-start(bf16[2,240,384]{2,1,0:T(8,128)(2,1)S(1)} %get-tuple-element.367), channel_id=1, source_target_pairs={{0,2},{1,3},{2,0},{3,1},{4,6},{5,7},{6,4},{7,5},{8,10},{9,11},{10,... | collective-permute-start | bytes 1105928 | tf_op jit(solution)/shard_map/ppermute | solution.py:483
  302.9 16.3 %collective-permute-start.65 = (bf16[576,384]{1,0:T(8,128)(2,1)S(1)}, bf16[576,384]{1,0:T(8,128)(2,1)S(1)}, u32[]{:S(2)}, u32[]{:S(2)}) collective-permute-start(bf16[576,384]{1,0:T(8,128)(2,1)S(1)} %pad_maximum_fusion.6), channel_id=1, source_target_pairs={{0,2},{1,3},{2,0},{3,1},{4,6},{5,7},{6,4},{7,5},{8,10},{9,11},{10,... | collective-permute-start | bytes 1327112 | tf_op jit(solution)/shard_map/ppermute | solution.py:483
  309.9 15.6 %collective-permute-start.59 = (bf16[256,768]{1,0:T(8,128)(2,1)S(1)}, bf16[256,768]{1,0:T(8,128)(2,1)S(1)}, u32[]{:S(2)}, u32[]{:S(2)}) collective-permute-start(bf16[256,768]{1,0:T(8,128)(2,1)S(1)} %fusion.80), channel_id=1, source_target_pairs={{0,2},{1,3},{2,0},{3,1},{4,6},{5,7},{6,4},{7,5},{8,10},{9,11},{10,... | collective-permute-start | bytes 1179656 | tf_op jit(solution)/shard_map/ppermute | solution.py:483
  311.1 20.0 %collective-permute-start.60 = (bf16[1,592,384]{2,1,0:T(8,128)(2,1)S(1)}, bf16[1,592,384]{2,1,0:T(8,128)(2,1)S(1)}, u32[]{:S(2)}, u32[]{:S(2)}) collective-permute-start(bf16[1,592,384]{2,1,0:T(8,128)(2,1)S(1)} %pad_maximum_fusion.5), channel_id=1, source_target_pairs={{0,16},{4,20},{8,24},{12,28},{16,0},{20,4},{24,8},{28,12},{1,17},{... | collective-permute-start | bytes 1363976 | tf_op jit(solution)/shard_map/ppermute | solution.py:483
  319.5 15.5 %collective-permute-start.66 = (bf16[2,576,384]{2,1,0:T(8,128)(2,1)S(1)}, bf16[2,576,384]{2,1,0:T(8,128)(2,1)}, u32[]{:S(2)}, u32[]{:S(2)}) collective-permute-start(bf16[2,576,384]{2,1,0:T(8,128)(2,1)S(1)} %pad_maximum_fusion.2.refs_1_), channel_id=1, source_target_pairs={{0,1},{1,0},{2,3},{3,2},{4,5},{5,4},{6,7},{7,6},{8,9},{9,8},{10,11... | collective-permute-start | bytes 2654216 | tf_op jit(solution)/shard_map/ppermute | solution.py:483
  331.2 12.5 %collective-permute-start.61 = (bf16[592,384]{1,0:T(8,128)(2,1)S(1)}, bf16[592,384]{1,0:T(8,128)(2,1)}, u32[]{:S(2)}, u32[]{:S(2)}) collective-permute-start(bf16[592,384]{1,0:T(8,128)(2,1)S(1)} %fusion.96), channel_id=1, source_target_pairs={{0,2},{1,3},{2,0},{3,1},{4,6},{5,7},{6,4},{7,5},{8,10},{9,11},{10,... | collective-permute-start | bytes 1363976 | tf_op jit(solution)/shard_map/ppermute | solution.py:483
  (134 other events, 1176.2 us)

commit v5 on v4

--- a/solution.py
+++ b/solution.py
@@ -410,9 +410,10 @@
 
 
 def qkv_grad_kernel(bits, order, place, *refs):
-    acts, pieces = refs[:OWNERS], refs[OWNERS : 2 * OWNERS]
-    keep, send, out, sems = refs[2 * OWNERS :]
-    narrow = acts[0].shape[1] // (1 << bits)
+    (pair, other), pieces = refs[:2], refs[2 : 2 + OWNERS]
+    keep, send, out, sems = refs[2 + OWNERS :]
+    acts = (pair.at[0], other.at[0], pair.at[1], other.at[1])
+    narrow = pair.shape[2] // (1 << bits)
     for part in range(3):
         found = dot(acts[0][...], pieces[0][part], TN)
         for r in range(1, OWNERS):
@@ -422,15 +423,18 @@
         copy.wait()
 
 
-def qkv_grad(place, bits, order, acts, pieces):
-    rows, width = acts[0].shape
+def qkv_grad(place, bits, order, acts, at, pieces):
+    rows, width = pieces[0].shape[1], acts[0].shape[2]
     half = width // 2
     slabs = 1 << bits
     narrow = width // slabs
     return pl.pallas_call(
         lambda *refs: qkv_grad_kernel(bits, order, *refs),
         name="qkv_grad",
-        in_specs=[SMEM_SPEC] + [VMEM_SPEC] * (2 * OWNERS),
+        grid=(1,),
+        in_specs=[SMEM_SPEC]
+        + [pl.BlockSpec((2, rows, width), lambda i: (0, at // rows, 0))] * 2
+        + [VMEM_SPEC] * OWNERS,
         out_specs=[ANY_SPEC] * 2,
         out_shape=halves_out(slabs, 3 * narrow, half),
         scratch_shapes=unit_scratch(slabs, 3 * narrow, half),
@@ -725,9 +729,7 @@
         place, counts_mine, rows, base, chosen_mine, slot_pieces
     )
     acts_other = swap(acts_pair, "seq", 1)
-    acts = [acts_pair[0], acts_other[0], acts_pair[1], acts_other[1]]
-    acts_b = [x[:rows] for x in acts]
-    acts_a = [x[rows:] for x in acts]
+    acts = (acts_pair, acts_other)
     mixture_b = assemble(exchange(mixed), y_first, core_first)
     done_b, kept_b = feed_forward(middle, None, mixture_b, out_b, gain_b2, up_b, down_b)
 
@@ -750,7 +752,7 @@
     feed_chains_b = [Chain(unit, order) for unit, order in zip(feed_b, (x_order, z_order))]
     packed_b, packed_slot = attend_back(place, counts_mine, saved_b, grads, chosen_mine)
     packed_slot = exchange(packed_slot)
-    part_chain_b = Chain(qkv_grad(place, bits, 0, acts_b, packed_b), x_order)
+    part_chain_b = Chain(qkv_grad(place, bits, 0, acts, 0, packed_b), x_order)
     packed_slot, packed_b, _ = stage(feed_chains_b, packed_slot, packed_b, part_chain_b.state)
 
     grad_packed_slot = assemble_packed(packed_slot, y_first, core_first)
@@ -782,13 +784,17 @@
     packed_a, _ = attend_back(place, counts_mine, saved_a, grads)
     (packed_a,) = meet([part_chain_b], packed_a)
     returned_a = exchange(packed_a)
-    part_chain_a = Chain(qkv_grad(place, bits, 2, acts_a, packed_a), y_order)
-    returned_a, packed_b, kept_last = meet([part_chain_a], returned_a, packed_b, kept_b[4])
+    part_chain_a = Chain(qkv_grad(place, bits, 2, acts, rows, packed_a), y_order)
+    returned_a, packed_b, kept_last, gains = meet(
+        [part_chain_a, feed_chain_b],
+        returned_a,
+        packed_b,
+        kept_b[4],
+        (gain_a1, gain_a2, gain_b1, gain_b2),
+    )
     done_b = kept_b[1] + project(kept_last, down_b)
-    gains = [
-        lax.dynamic_slice_in_dim(gain, dp_at * narrow, narrow, axis=0).astype(F32)
-        for gain in (gain_a1, gain_a2, gain_b1, gain_b2)
-    ]
+    gains = lax.dynamic_slice_in_dim(jnp.stack(gains), dp_at * narrow, narrow, axis=1)
+    gains = gains.astype(F32)
 
     grad_packed_a = assemble_packed(returned_a, y_first, core_first)
     res_a = norm_back(picked, gain_a1, project_back(grad_packed_a, qkv_a))
@@ -807,16 +813,16 @@
     b_side = [feed_chain_b, part_chain_b]
     for chain in tail:
         chain.step()
+    feed_chain_b.step()
     given = swap(jnp.stack([shares[1].astype(BF16), shares[3].astype(BF16)]), "seq", 1)
     act_near = shares[0] + given[0].astype(F32)
     act_far = (shares[2] + given[1].astype(F32)).astype(BF16)
     grad_picked, act_near, act_far, done_b, gains = meet(
         tail + b_side, grad_picked, act_near, act_far, done_b, gains
     )
-    for chain in b_side:
-        chain.step()
+    part_chain_b.step()
     stage(tail)
-    meet(b_side, tail[0].state)
+    meet([part_chain_b], tail[0].state)
     if not part_chain_b.done:
         part_chain_b.step()
     (act_far,) = stage(tail, act_far)

time: 363 us -> 355 us (0.978)
  matrix products: 60.1 us -> 54.9 us
    slice x6 -> x0, local copies, waits for them, and re-layouts: 6.54 us -> none  [the longest x3 3.63 us: per_device(): acts_b = [x[:rows] for x in acts]]
    unnamed x229 -> x247, local copies, waits for them, and re-layouts: 11.3 us -> 15.6 us
  transfers between devices with their start and end apart: 68 -> 68, of which waited for: 26 -> 27; matrix products, arithmetic and copies ran while one was open for 29% -> 26% of each run, Pallas kernels for 20% -> 20%
where the time goes in v5:
time: 355 us; the launch traced here: 350 us
  Pallas kernels  94.9 us (27%)
  waiting for transfers between devices  78.7 us (22%)
  matrix products  54.9 us (15%)
  starting transfers between devices  54.8 us (15%)
  other arithmetic  38.7 us (11%)
  local copies, waits for them, and re-layouts  24.7 us (7%)
    ppermute x68, waiting for transfers between devices, swap(): return lax.ppermute(x, axis, [(i, i ^ bit) for i in range(size)])  78.7 us
    ppermute x68, starting transfers between devices, swap(): return lax.ppermute(x, axis, [(i, i ^ bit) for i in range(size)])  54.8 us
    pallas_call x2, Pallas kernels, feed_grad(): pl.pallas_call(lambda *refs: feed_grad_kernel(bits, orders, routed, *refs...  22.7 us
    pallas_call x2, Pallas kernels, attend_back(): pl.pallas_call(lambda *refs: attend_back_kernel(rows, routed, *refs), nam...  22.2 us
    dot_general x6, matrix products, project(): jnp.einsum('bnd,de->bne', left_side, weight, preferred_element_type=F32)  21.3 us
    dot_general x8, matrix products, project_back(): jnp.einsum('bne,de->bnd', gradient, weight, preferred_element_type=F32)  19.2 us
    pallas_call x2, Pallas kernels, attend(): pl.pallas_call(lambda *refs: attend_kernel(rows, routed, *refs), name='at...  17.3 us
    unnamed x247, local copies, waits for them, and re-layouts  15.6 us
  transfers between devices with their start and end apart: 68, of which 27 were waited for; matrix products, arithmetic and copies ran while one was open for 26% of the time, Pallas kernels for 20%

profile of v5, /device:TPU:0, one launch (start us, length us, event | category | flops | bytes accessed | tf_op | source)
XLA Modules:
  0.0 349.8 jit_solution(5416365576441611238)
XLA Ops:
  0.7 2.2 fusion.207
  3.5 4.2 %project_pieces.3 = (bf16[2,64,768]{2,1,0:T(8,128)(2,1)}, bf16[3,64,384]{2,1,0:T(8,128)(2,1)}, bf16[3,64,384]{2,1,0:T(8,128)(2,1)}, bf16[3,64,384]{2,1,0:T(8,128)(2,1)}, bf16[3,64,384]{2,1,0:T(8,128)(2,1)}) custom-call(s32[5]{0:T(128)} %stack.103.refs_0_, bf16[2,64,768]{2,1,0:T(8,128)(2,1)} %get-tuple-element.507.refs_1_, bf16[768]{0:T(1024)(128)(2,1)} %refs_2_.3, ...), custom_call_target="tpu_custom_call" | custom-call | flops 452984832 | bytes 4718592 | tf_op jit(solution)/shard_map/project_pieces/pallas_call | solution.py:59
  8.2 2.5 collective-permute-start.1
  11.5 6.8 %project_pieces.4 = (bf16[2,256,768]{2,1,0:T(8,128)(2,1)}, bf16[3,272,384]{2,1,0:T(8,128)(2,1)}, bf16[3,272,384]{2,1,0:T(8,128)(2,1)}, bf16[3,272,384]{2,1,0:T(8,128)(2,1)}, bf16[3,272,384]{2,1,0:T(8,128)(2,1)}) custom-call(s32[5]{0:T(128)} %stack.103.refs_0_, bf16[2,256,768]{2,1,0:T(8,128)(2,1)} %refs_1_.1, bf16[768]{0:T(1024)(128)(2,1)} %refs_2_.5, ...), custom_call_target="tpu_custom_call" | custom-call | flops 1811939328 | bytes 8257536 | tf_op jit(solution)/shard_map/project_pieces/pallas_call | solution.py:59
  22.5 4.5 %attend_routed.1 = (bf16[64,384]{1,0:T(8,128)(2,1)}, bf16[64,384]{1,0:T(8,128)(2,1)}, bf16[64,384]{1,0:T(8,128)(2,1)}, bf16[64,384]{1,0:T(8,128)(2,1)}, bf16[3,2...) custom-call(s32[5]{0:T(128)} %stack.103.refs_0_, s32[4]{0:T(128)} %fusion.199.refs_1_, ...), custom_call_target="tpu_custom_call" | custom-call | flops 402653184 | bytes 1572864 | tf_op jit(solution)/shard_map/attend_routed/pallas_call | solution.py:179
  29.1 7.3 %collective-permute-done.4 = bf16[64,384]{1,0:T(8,128)(2,1)S(1)} collective-permute-done((bf16[64,384]{1,0:T(8,128)(2,1)}, bf16[64,384]{1,0:T(8,128)(2,1)S(1)}, u32[]{:S(2)}, u32[]{:S(2)}) %collective-permute-start.4) | collective-permute-done | bytes 49184 | tf_op jit(solution)/shard_map/ppermute | solution.py:487
  40.5 4.9 %multiply_convert_fusion.2 = (bf16[2,64,3072]{2,1,0:T(8,128)(2,1)S(1)}, f32[2,64,3072]{2,1,0:T(8,128)}) fusion(bf16[2,64,768]{2,1,0:T(8,128)(2,1)S(1)} %multiply_convert_fusion.4, bf16[768,3072]{1,0:T(8,128)(2,1)} %param.25), kind=kOutput, calls=%fused_computation.52 | convolution fusion | flops 607518720 | bytes 7274496 | tf_op jit(solution)/shard_map/bnd,de->bne/dot_general | solution.py:607
  50.4 2.2 collective-permute-done.6.refs_6_
  54.4 4.2 %project_pieces.5 = (bf16[2,64,768]{2,1,0:T(8,128)(2,1)}, bf16[3,64,384]{2,1,0:T(8,128)(2,1)}, bf16[3,64,384]{2,1,0:T(8,128)(2,1)}, bf16[3,64,384]{2,1,0:T(8,128)(2,1)}, bf16[3,64,384]{2,1,0:T(8,128)(2,1)}) custom-call(s32[5]{0:T(128)} %stack.103.refs_0_, f32[2,64,768]{2,1,0:T(8,128)} %get-tuple-element.224.refs_1_, bf16[768]{0:T(1024)(128)(2,1)} %refs_2_.5, ...), custom_call_target="tpu_custom_call" | custom-call | flops 452984832 | bytes 4718592 | tf_op jit(solution)/shard_map/project_pieces/pallas_call | solution.py:59
  65.8 1.8 collective-permute-done.12.refs_10_
  68.3 12.8 %attend_dense.1 = (bf16[256,384]{1,0:T(8,128)(2,1)}, bf16[256,384]{1,0:T(8,128)(2,1)}, bf16[256,384]{1,0:T(8,128)(2,1)}, bf16[256,384]{1,0:T(8,128)(2,1)}, bf16[...) custom-call(s32[5]{0:T(128)} %stack.103.refs_0_, s32[4]{0:T(128)} %fusion.199.refs_1_, ...), custom_call_target="tpu_custom_call" | custom-call | flops 4026531840 | bytes 6291456 | tf_op jit(solution)/shard_map/attend_dense/pallas_call | solution.py:179
  84.7 4.5 %collective-permute-done.16 = bf16[256,384]{1,0:T(8,128)(2,1)} collective-permute-done((bf16[256,384]{1,0:T(8,128)(2,1)}, bf16[256,384]{1,0:T(8,128)(2,1)}, u32[]{:S(2)}, u32[]{:S(2)}) %collective-permute-start.16) | collective-permute-done | bytes 196640 | tf_op jit(solution)/shard_map/ppermute | solution.py:487
  89.2 3.3 collective-permute-done.17
  95.9 7.0 %multiply_convert_fusion = (bf16[2,256,3072]{2,1,0:T(8,128)(2,1)S(1)}, f32[2,256,3072]{2,1,0:T(8,128)S(1)}) fusion(bf16[2,256,768]{2,1,0:T(8,128)(2,1)S(1)} %multiply_convert_fusion.1, bf16[768,3072]{1,0:T(8,128)(2,1)} %param.31), kind=kOutput, calls=%fused_computation.9 | convolution fusion | flops 2430074880 | bytes 14942208 | tf_op jit(solution)/shard_map/bnd,de->bne/dot_general | solution.py:607
  103.3 6.1 %fusion.6 = bf16[2,256,3072]{2,1,0:T(8,128)(2,1)S(1)} fusion(f32[2,256,3072]{2,1,0:T(8,128)S(1)} %get-tuple-element.519, bf16[2,256,768]{2,1,0:T(8,128)(2,1)S(1)} %copy-done.29, bf16[3072,768]{1,0:T(8,128)(2,1)S(1)} %bitcast.322), kind=kOutput, calls=%fused_computation.8 | convolution fusion | flops 2447376384 | bytes 14942208 | tf_op jit(solution)/shard_map/bne,de->bnd/dot_general | solution.py:611
  111.2 2.7 multiply_reduce_fusion.2
  118.6 1.9 collective-permute-start.32
  122.4 15.4 %feed_grad.2 = (bf16[8,192,384]{2,1,0:T(8,128)(2,1)}, bf16[8,192,384]{2,1,0:T(8,128)(2,1)}, bf16[8,240,384]{2,1,0:T(8,128)(2,1)}, bf16[8,240,384]{2,1,0:T(8,128)(2,1)}) custom-call(s32[5]{0:T(128)} %stack.103.refs_0_, bf16[512,768]{1,0:T(8,128)(2,1)} %bitcast.308, bf16[512,768]{1,0:T(8,128)(2,1)} %copy-done.94, bf16[512,3072]{1,0:T(8,128)(2,1)} %bitcast.324, ...), custom_call_target="tpu_custom_call" | custom-call | flops 5435817984 | bytes 21037056 | tf_op jit(solution)/shard_map/feed_grad/pallas_call | solution.py:397
  137.9 1.9 collective-permute-done.23.refs_9_
  146.2 17.9 %attend_dense_back.1 = (bf16[3,256,384]{2,1,0:T(8,128)(2,1)}, bf16[3,256,384]{2,1,0:T(8,128)(2,1)}, bf16[3,256,384]{2,1,0:T(8,128)(2,1)}, bf16[3,256,384]{2,1,0:...) custom-call(s32[5]{0:T(128)} %stack.103.refs_0_, ...), custom_call_target="tpu_custom_call" | custom-call | flops 10066329600 | bytes 6291456 | tf_op jit(solution)/shard_map/attend_dense_back/pallas_call | solution.py:279
  166.1 6.0 %qkv_grad.2 = (bf16[8,144,384]{2,1,0:T(8,128)(2,1)}, bf16[8,144,384]{2,1,0:T(8,128)(2,1)}) custom-call(s32[5]{0:T(128)} %stack.103.refs_0_, bf16[2,320,768]{2,1,0:T(8,128)(2,1)} %copy-done.16, bf16[2,320,768]{2,1,0:T(8,128)(2,1)} %collective-permute-done.33.refs_2_, bf16[3,256,384]{2,1,0:T(8,128)(2,1)} %get-tuple-element.353.refs_3_, ...), custom_call_target="tpu_custom_call" | custom-call | flops 1811939328 | bytes 5701632 | tf_op jit(solution)/shard_map/qkv_grad/pallas_call | solution.py:431
  173.8 2.4 collective-permute-done.28
  184.0 4.5 %fusion.35 = bf16[2,64,3072]{2,1,0:T(8,128)(2,1)S(1)} fusion(f32[2,64,3072]{2,1,0:T(8,128)S(1)} %copy-done.114, bf16[2,64,768]{2,1,0:T(8,128)(2,1)S(1)} %get-tuple-element.521, bf16[3072,768]{1,0:T(8,128)(2,1)} %param.26), kind=kOutput, calls=%fused_computation.40 | convolution fusion | flops 611844096 | bytes 7274496 | tf_op jit(solution)/shard_map/bne,de->bnd/dot_general | solution.py:611
  188.6 2.9 collective-permute-done.34
  191.6 4.3 %collective-permute-done.35 = bf16[4,240,384]{2,1,0:T(8,128)(2,1)S(1)} collective-permute-done((bf16[4,240,384]{2,1,0:T(8,128)(2,1)S(1)}, bf16[4,240,384]{2,1,0:T(8,128)(2,1)S(1)}, u32[]{:S(2)}, u32[]{:S(2)}) %collective-permute-start.35) | collective-permute-done | bytes 737312 | tf_op jit(solution)/shard_map/ppermute | solution.py:487
  209.0 7.3 %feed_grad.3 = (bf16[8,208,384]{2,1,0:T(8,128)(2,1)}, bf16[8,208,384]{2,1,0:T(8,128)(2,1)}, bf16[8,240,384]{2,1,0:T(8,128)(2,1)}, bf16[8,240,384]{2,1,0:T(8,128)(2,1)}) custom-call(s32[5]{0:T(128)} %stack.103.refs_0_, bf16[128,768]{1,0:T(8,128)(2,1)} %bitcast.315, bf16[128,768]{1,0:T(8,128)(2,1)} %copy-done.100, bf16[128,3072]{1,0:T(8,128)(2,1)} %bitcast.302, ...), custom_call_target="tpu_custom_call" | custom-call | flops 1358954496 | bytes 9240576 | tf_op jit(solution)/shard_map/feed_grad/pallas_call | solution.py:397
  216.4 2.1 collective-permute-done.38
  218.5 2.5 add_convert_fusion.11
  225.3 4.3 %attend_routed_back.1 = (bf16[3,64,384]{2,1,0:T(8,128)(2,1)}, bf16[3,64,384]{2,1,0:T(8,128)(2,1)}, bf16[3,64,384]{2,1,0:T(8,128)(2,1)}, bf16[3,64,384]{2,1,0:T(8,128)(2,1)}) custom-call(s32[5]{0:T(128)} %stack.103.refs_0_, s32[4]{0:T(128)} %fusion.199.refs_1_, bf16[3,256,384]{2,1,0:T(8,128)(2,1)} %get-tuple-element.314.refs_2_, ...), custom_call_target="tpu_custom_call" | custom-call | flops 1006632960 | bytes 1572864 | tf_op jit(solution)/shard_map/attend_routed_back/pallas_call | solution.py:279
  232.8 1.9 add_convert_fusion.24
  236.7 4.6 %qkv_grad.3 = (bf16[8,144,384]{2,1,0:T(8,128)(2,1)}, bf16[8,144,384]{2,1,0:T(8,128)(2,1)}) custom-call(s32[5]{0:T(128)} %stack.103.refs_0_, bf16[2,320,768]{2,1,0:T(8,128)(2,1)} %copy-done.16, bf16[2,320,768]{2,1,0:T(8,128)(2,1)} %collective-permute-done.33.refs_2_, bf16[3,64,384]{2,1,0:T(8,128)(2,1)} %get-tuple-element.345.refs_3_, ...), custom_call_target="tpu_custom_call" | custom-call | flops 452984832 | bytes 2752512 | tf_op jit(solution)/shard_map/qkv_grad/pallas_call | solution.py:431
  241.7 2.4 collective-permute-done.50
  245.3 2.6 collective-permute-start.52
  259.1 5.9 %fusion.44 = bf16[2,256,768]{2,1,0:T(8,128)(2,1)} fusion(f32[2,256,768]{2,1,0:T(8,128)S(1)} %copy-done.8, bf16[2,256,3072]{2,1,0:T(8,128)(2,1)S(1)} %copy-done.91, bf16[3072,768]{1,0:T(8,128)(2,1)} %param.32), kind=kOutput, calls=%fused_computation.59 | convolution fusion | flops 2416705536 | bytes 10223616 | tf_op jit(solution)/shard_map/bnd,de->bne/dot_general | solution.py:607
  276.5 3.9 %collective-permute-done.63 = bf16[2,144,384]{2,1,0:T(8,128)(2,1)S(1)} collective-permute-done((bf16[2,144,384]{2,1,0:T(8,128)(2,1)S(1)}, bf16[2,144,384]{2,1,0:T(8,128)(2,1)S(1)}, u32[]{:S(2)}, u32[]{:S(2)}) %collective-permute-start.63) | collective-permute-done | bytes 221216 | tf_op jit(solution)/shard_map/ppermute | solution.py:487
  280.5 8.5 %collective-permute-done.56 = bf16[4,144,384]{2,1,0:T(8,128)(2,1)S(1)} collective-permute-done((bf16[4,144,384]{2,1,0:T(8,128)(2,1)S(1)}, bf16[4,144,384]{2,1,0:T(8,128)(2,1)S(1)}, u32[]{:S(2)}, u32[]{:S(2)}) %collective-permute-start.56) | collective-permute-done | bytes 442400 | tf_op jit(solution)/shard_map/ppermute | solution.py:487
  290.0 2.5 collective-permute-done.55
  296.2 3.5 collective-permute-done.64
  301.1 1.8 collective-permute-done.57
  303.0 1.9 collective-permute-done.58
  306.6 2.8 collective-permute-start.61
  309.4 5.0 %collective-permute-done.65 = bf16[576,384]{1,0:T(8,128)(2,1)S(1)} collective-permute-done((bf16[576,384]{1,0:T(8,128)(2,1)S(1)}, bf16[576,384]{1,0:T(8,128)(2,1)S(1)}, u32[]{:S(2)}, u32[]{:S(2)}) %collective-permute-start.65) | collective-permute-done | bytes 442400 | tf_op jit(solution)/shard_map/ppermute | solution.py:487
  314.8 4.8 %collective-permute-done.60 = bf16[256,768]{1,0:T(8,128)(2,1)S(1)} collective-permute-done((bf16[256,768]{1,0:T(8,128)(2,1)S(1)}, bf16[256,768]{1,0:T(8,128)(2,1)S(1)}, u32[]{:S(2)}, u32[]{:S(2)}) %collective-permute-start.60) | collective-permute-done | bytes 393248 | tf_op jit(solution)/shard_map/ppermute | solution.py:487
  321.1 2.5 fusion.38
  325.7 3.4 finish_grads.2
  332.5 3.8 %collective-permute-done.62 = bf16[592,384]{1,0:T(8,128)(2,1)} collective-permute-done((bf16[592,384]{1,0:T(8,128)(2,1)S(1)}, bf16[592,384]{1,0:T(8,128)(2,1)}, u32[]{:S(2)}, u32[]{:S(2)}) %collective-permute-start.62) | collective-permute-done | bytes 454688 | tf_op jit(solution)/shard_map/ppermute | solution.py:487
  337.8 2.4 collective-permute-done.67.refs_2_
  341.2 3.5 %finish_grads.3 = (f32[96,2304]{1,0:T(8,128)}, f32[96,768]{1,0:T(8,128)}, f32[96,3072]{1,0:T(8,128)}, f32[384,768]{1,0:T(8,128)}) custom-call(s32[5]{0:T(128)} %stack.103.refs_0_, bf16[2,592,384]{2,1,0:T(8,128)(2,1)} %copy-done.17, bf16[2,592,384]{2,1,0:T(8,128)(2,1)} %copy-done.42), custom_call_target="tpu_custom_call" | custom-call | bytes 5308416 | tf_op jit(solution)/shard_map/finish_grads/pallas_call | solution.py:474
  (489 shorter events, 128.5 us)
Async XLA Ops:
  7.8 14.0 %collective-permute-start = (bf16[3,64,384]{2,1,0:T(8,128)(2,1)}, bf16[3,64,384]{2,1,0:T(8,128)(2,1)S(1)}, u32[]{:S(2)}, u32[]{:S(2)}) collective-permute-start(bf16[3,64,384]{2,1,0:T(8,128)(2,1)} %get-tuple-element.210), channel_id=1, source_target_pairs={{0,1},{1,0},{2,3},{3,2},{4,5},{5,4},{6,7},{7,6},{8,9},{9,8},{10,11... | collective-permute-start | bytes 442376 | tf_op jit(solution)/shard_map/ppermute | solution.py:487
  8.2 13.6 %collective-permute-start.1 = (bf16[3,64,384]{2,1,0:T(8,128)(2,1)}, bf16[3,64,384]{2,1,0:T(8,128)(2,1)S(1)}, u32[]{:S(2)}, u32[]{:S(2)}) collective-permute-start(bf16[3,64,384]{2,1,0:T(8,128)(2,1)} %get-tuple-element.211), channel_id=1, source_target_pairs={{0,2},{1,3},{2,0},{3,1},{4,6},{5,7},{6,4},{7,5},{8,10},{9,11},{10,... | collective-permute-start | bytes 442376 | tf_op jit(solution)/shard_map/ppermute | solution.py:487
  10.7 11.1 %collective-permute-start.2 = (bf16[3,64,384]{2,1,0:T(8,128)(2,1)}, bf16[3,64,384]{2,1,0:T(8,128)(2,1)}, u32[]{:S(2)}, u32[]{:S(2)}) collective-permute-start(bf16[3,64,384]{2,1,0:T(8,128)(2,1)} %get-tuple-element.212), channel_id=1, source_target_pairs={{0,3},{1,2},{2,1},{3,0},{4,7},{5,6},{6,5},{7,4},{8,11},{9,10},{10,... | collective-permute-start | bytes 442376 | tf_op jit(solution)/shard_map/ppermute | solution.py:487
  18.3 30.5 %collective-permute-start.14 = (bf16[3,272,384]{2,1,0:T(8,128)(2,1)}, bf16[3,272,384]{2,1,0:T(8,128)(2,1)}, u32[]{:S(2)}, u32[]{:S(2)}) collective-permute-start(bf16[3,272,384]{2,1,0:T(8,128)(2,1)} %get-tuple-element.235), channel_id=1, source_target_pairs={{0,2},{1,3},{2,0},{3,1},{4,6},{5,7},{6,4},{7,5},{8,10},{9,11},{10,... | collective-permute-start | bytes 1880072 | tf_op jit(solution)/shard_map/ppermute | solution.py:487
  27.0 9.4 %collective-permute-start.4 = (bf16[64,384]{1,0:T(8,128)(2,1)}, bf16[64,384]{1,0:T(8,128)(2,1)S(1)}, u32[]{:S(2)}, u32[]{:S(2)}) collective-permute-start(bf16[64,384]{1,0:T(8,128)(2,1)} %get-tuple-element.215), channel_id=1, source_target_pairs={{0,2},{1,3},{2,0},{3,1},{4,6},{5,7},{6,4},{7,5},{8,10},{9,11},{10,... | collective-permute-start | bytes 147464 | tf_op jit(solution)/shard_map/ppermute | solution.py:487
  27.4 9.0 %collective-permute-start.5 = (bf16[64,384]{1,0:T(8,128)(2,1)}, bf16[64,384]{1,0:T(8,128)(2,1)S(1)}, u32[]{:S(2)}, u32[]{:S(2)}) collective-permute-start(bf16[64,384]{1,0:T(8,128)(2,1)} %get-tuple-element.216), channel_id=1, source_target_pairs={{0,3},{1,2},{2,1},{3,0},{4,7},{5,6},{6,5},{7,4},{8,11},{9,10},{10,... | collective-permute-start | bytes 147464 | tf_op jit(solution)/shard_map/ppermute | solution.py:487
  36.4 16.2 %collective-permute-start.6 = (bf16[3,272,384]{2,1,0:T(8,128)(2,1)}, bf16[3,272,384]{2,1,0:T(8,128)(2,1)S(1)}, u32[]{:S(2)}, u32[]{:S(2)}) collective-permute-start(bf16[3,272,384]{2,1,0:T(8,128)(2,1)} %get-tuple-element.219), channel_id=1, source_target_pairs={{0,3},{1,2},{2,1},{3,0},{4,7},{5,6},{6,5},{7,4},{8,11},{9,10},{10,... | collective-permute-start | bytes 1880072 | tf_op jit(solution)/shard_map/ppermute | solution.py:487
  40.3 9.6 %collective-permute-start.7 = (bf16[128,768]{1,0:T(8,128)(2,1)S(1)}, bf16[128,768]{1,0:T(8,128)(2,1)S(1)}, u32[]{:S(2)}, u32[]{:S(2)}) collective-permute-start(bf16[128,768]{1,0:T(8,128)(2,1)S(1)} %bitcast.314), channel_id=1, source_target_pairs={{0,1},{1,0},{2,3},{3,2},{4,5},{5,4},{6,7},{7,6},{8,9},{9,8},{10,11... | collective-permute-start | bytes 589832 | tf_op jit(solution)/shard_map/ppermute | solution.py:487
  82.8 9.7 %collective-permute-start.17 = (bf16[256,384]{1,0:T(8,128)(2,1)}, bf16[256,384]{1,0:T(8,128)(2,1)}, u32[]{:S(2)}, u32[]{:S(2)}) collective-permute-start(bf16[256,384]{1,0:T(8,128)(2,1)} %get-tuple-element.244), channel_id=1, source_target_pairs={{0,3},{1,2},{2,1},{3,0},{4,7},{5,6},{6,5},{7,4},{8,11},{9,10},{10,... | collective-permute-start | bytes 589832 | tf_op jit(solution)/shard_map/ppermute | solution.py:487
  84.1 36.5 %collective-permute-start.25 = (bf16[512,384]{1,0:T(8,128)(2,1)S(1)}, bf16[512,384]{1,0:T(8,128)(2,1)}, u32[]{:S(2)}, u32[]{:S(2)}) collective-permute-start(bf16[512,384]{1,0:T(8,128)(2,1)S(1)} %constant_dynamic-slice_fusion.6), channel_id=1, source_target_pairs={{0,1},{1,0},{2,3},{3,2},{4,5},{5,4},{6,7},{7,6},{8,9},{9,8},{10,11... | collective-permute-start | bytes 1179656 | tf_op jit(solution)/shard_map/ppermute | solution.py:487
  84.4 9.2 %collective-permute-start.15 = (bf16[256,384]{1,0:T(8,128)(2,1)}, bf16[256,384]{1,0:T(8,128)(2,1)S(1)}, u32[]{:S(2)}, u32[]{:S(2)}) collective-permute-start(bf16[256,384]{1,0:T(8,128)(2,1)} %get-tuple-element.242), channel_id=1, source_target_pairs={{0,1},{1,0},{2,3},{3,2},{4,5},{5,4},{6,7},{7,6},{8,9},{9,8},{10,11... | collective-permute-start | bytes 589832 | tf_op jit(solution)/shard_map/ppermute | solution.py:487
  102.9 17.6 %collective-permute-start.19 = (bf16[512,3072]{1,0:T(8,128)(2,1)S(1)}, bf16[512,3072]{1,0:T(8,128)(2,1)S(1)}, u32[]{:S(2)}, u32[]{:S(2)}) collective-permute-start(bf16[512,3072]{1,0:T(8,128)(2,1)S(1)} %bitcast.323), channel_id=1, source_target_pairs={{0,1},{1,0},{2,3},{3,2},{4,5},{5,4},{6,7},{7,6},{8,9},{9,8},{10,11... | collective-permute-start | bytes 9437192 | tf_op jit(solution)/shard_map/ppermute | solution.py:487
  109.5 12.9 %collective-permute-start.24 = (bf16[512,1536]{1,0:T(8,128)(2,1)S(1)}, bf16[512,1536]{1,0:T(8,128)(2,1)}, u32[]{:S(2)}, u32[]{:S(2)}) collective-permute-start(bf16[512,1536]{1,0:T(8,128)(2,1)S(1)} %constant_dynamic-slice_fusion.7), channel_id=1, source_target_pairs={{0,1},{1,0},{2,3},{3,2},{4,5},{5,4},{6,7},{7,6},{8,9},{9,8},{10,11... | collective-permute-start | bytes 4718600 | tf_op jit(solution)/shard_map/ppermute | solution.py:487
  118.6 24.4 %collective-permute-start.32 = (bf16[320,768]{1,0:T(8,128)(2,1)S(1)}, bf16[320,768]{1,0:T(8,128)(2,1)S(1)}, u32[]{:S(2)}, u32[]{:S(2)}) collective-permute-start(bf16[320,768]{1,0:T(8,128)(2,1)S(1)} %copy-done.56), channel_id=1, source_target_pairs={{0,2},{1,3},{2,0},{3,1},{4,6},{5,7},{6,4},{7,5},{8,10},{9,11},{10,... | collective-permute-start | bytes 1474568 | tf_op jit(solution)/shard_map/ppermute | solution.py:487
  120.5 17.4 %collective-permute-start.21 = (bf16[256,384]{1,0:T(8,128)(2,1)}, bf16[256,384]{1,0:T(8,128)(2,1)S(1)}, u32[]{:S(2)}, u32[]{:S(2)}) collective-permute-start(bf16[256,384]{1,0:T(8,128)(2,1)} %get-tuple-element.246), channel_id=1, source_target_pairs={{0,1},{1,0},{2,3},{3,2},{4,5},{5,4},{6,7},{7,6},{8,9},{9,8},{10,11... | collective-permute-start | bytes 589832 | tf_op jit(solution)/shard_map/ppermute | solution.py:487
  120.5 17.4 %collective-permute-start.22 = (bf16[256,384]{1,0:T(8,128)(2,1)}, bf16[256,384]{1,0:T(8,128)(2,1)S(1)}, u32[]{:S(2)}, u32[]{:S(2)}) collective-permute-start(bf16[256,384]{1,0:T(8,128)(2,1)} %get-tuple-element.247), channel_id=1, source_target_pairs={{0,2},{1,3},{2,0},{3,1},{4,6},{5,7},{6,4},{7,5},{8,10},{9,11},{10,... | collective-permute-start | bytes 589832 | tf_op jit(solution)/shard_map/ppermute | solution.py:487
  120.8 19.0 %collective-permute-start.23 = (bf16[256,384]{1,0:T(8,128)(2,1)S(1)}, bf16[256,384]{1,0:T(8,128)(2,1)S(1)}, u32[]{:S(2)}, u32[]{:S(2)}) collective-permute-start(bf16[256,384]{1,0:T(8,128)(2,1)S(1)} %get-tuple-element.248), channel_id=1, source_target_pairs={{0,3},{1,2},{2,1},{3,0},{4,7},{5,6},{6,5},{7,4},{8,11},{9,10},{10,... | collective-permute-start | bytes 589832 | tf_op jit(solution)/shard_map/ppermute | solution.py:487
  139.9 32.3 %collective-permute-start.27 = (bf16[8,192,384]{2,1,0:T(8,128)(2,1)}, bf16[8,192,384]{2,1,0:T(8,128)(2,1)}, u32[]{:S(2)}, u32[]{:S(2)}) collective-permute-start(bf16[8,192,384]{2,1,0:T(8,128)(2,1)} %get-tuple-element.260), channel_id=1, source_target_pairs={{0,4},{4,0},{8,12},{12,8},{16,20},{20,16},{24,28},{28,24},{1,5},{5... | collective-permute-start | bytes 3538952 | tf_op jit(solution)/shard_map/ppermute | solution.py:487
  141.5 34.7 %collective-permute-start.28 = (bf16[8,240,384]{2,1,0:T(8,128)(2,1)}, bf16[8,240,384]{2,1,0:T(8,128)(2,1)S(1)}, u32[]{:S(2)}, u32[]{:S(2)}) collective-permute-start(bf16[8,240,384]{2,1,0:T(8,128)(2,1)} %get-tuple-element.262), channel_id=1, source_target_pairs={{0,8},{4,12},{8,0},{12,4},{16,24},{20,28},{24,16},{28,20},{1,9},{5... | collective-permute-start | bytes 4423688 | tf_op jit(solution)/shard_map/ppermute | solution.py:487
  145.0 21.1 %collective-permute-start.33 = (bf16[2,320,768]{2,1,0:T(8,128)(2,1)S(1)}, bf16[2,320,768]{2,1,0:T(8,128)(2,1)}, u32[]{:S(2)}, u32[]{:S(2)}) collective-permute-start(bf16[2,320,768]{2,1,0:T(8,128)(2,1)S(1)} %pad_maximum_fusion.refs_1_), channel_id=1, source_target_pairs={{0,1},{1,0},{2,3},{3,2},{4,5},{5,4},{6,7},{7,6},{8,9},{9,8},{10,11... | collective-permute-start | bytes 2949128 | tf_op jit(solution)/shard_map/ppermute | solution.py:487
  164.0 12.5 %collective-permute-start.29 = (bf16[3,64,384]{2,1,0:T(8,128)(2,1)}, bf16[3,64,384]{2,1,0:T(8,128)(2,1)S(1)}, u32[]{:S(2)}, u32[]{:S(2)}) collective-permute-start(bf16[3,64,384]{2,1,0:T(8,128)(2,1)} %get-tuple-element.271), channel_id=1, source_target_pairs={{0,1},{1,0},{2,3},{3,2},{4,5},{5,4},{6,7},{7,6},{8,9},{9,8},{10,11... | collective-permute-start | bytes 442376 | tf_op jit(solution)/shard_map/ppermute | solution.py:487
  164.6 12.0 %collective-permute-start.30 = (bf16[3,64,384]{2,1,0:T(8,128)(2,1)}, bf16[3,64,384]{2,1,0:T(8,128)(2,1)S(1)}, u32[]{:S(2)}, u32[]{:S(2)}) collective-permute-start(bf16[3,64,384]{2,1,0:T(8,128)(2,1)} %get-tuple-element.272), channel_id=1, source_target_pairs={{0,2},{1,3},{2,0},{3,1},{4,6},{5,7},{6,4},{7,5},{8,10},{9,11},{10,... | collective-permute-start | bytes 442376 | tf_op jit(solution)/shard_map/ppermute | solution.py:487
  166.1 10.5 %collective-permute-start.31 = (bf16[3,64,384]{2,1,0:T(8,128)(2,1)}, bf16[3,64,384]{2,1,0:T(8,128)(2,1)S(1)}, u32[]{:S(2)}, u32[]{:S(2)}) collective-permute-start(bf16[3,64,384]{2,1,0:T(8,128)(2,1)} %get-tuple-element.273), channel_id=1, source_target_pairs={{0,3},{1,2},{2,1},{3,0},{4,7},{5,6},{6,5},{7,4},{8,11},{9,10},{10,... | collective-permute-start | bytes 442376 | tf_op jit(solution)/shard_map/ppermute | solution.py:487
  176.6 14.8 %collective-permute-start.34 = (bf16[4,192,384]{2,1,0:T(8,128)(2,1)S(1)}, bf16[4,192,384]{2,1,0:T(8,128)(2,1)S(1)}, u32[]{:S(2)}, u32[]{:S(2)}) collective-permute-start(bf16[4,192,384]{2,1,0:T(8,128)(2,1)S(1)} %get-tuple-element.283), channel_id=1, source_target_pairs={{0,2},{1,3},{2,0},{3,1},{4,6},{5,7},{6,4},{7,5},{8,10},{9,11},{10,... | collective-permute-start | bytes 1769480 | tf_op jit(solution)/shard_map/ppermute | solution.py:487
  178.2 17.7 %collective-permute-start.35 = (bf16[4,240,384]{2,1,0:T(8,128)(2,1)S(1)}, bf16[4,240,384]{2,1,0:T(8,128)(2,1)S(1)}, u32[]{:S(2)}, u32[]{:S(2)}) collective-permute-start(bf16[4,240,384]{2,1,0:T(8,128)(2,1)S(1)} %get-tuple-element.285), channel_id=1, source_target_pairs={{0,4},{4,0},{8,12},{12,8},{16,20},{20,16},{24,28},{28,24},{1,5},{5... | collective-permute-start | bytes 2211848 | tf_op jit(solution)/shard_map/ppermute | solution.py:487
  183.5 23.7 %collective-permute-start.43 = (bf16[128,384]{1,0:T(8,128)(2,1)S(1)}, bf16[128,384]{1,0:T(8,128)(2,1)S(1)}, u32[]{:S(2)}, u32[]{:S(2)}) collective-permute-start(bf16[128,384]{1,0:T(8,128)(2,1)S(1)} %constant_dynamic-slice_fusion.3), channel_id=1, source_target_pairs={{0,1},{1,0},{2,3},{3,2},{4,5},{5,4},{6,7},{7,6},{8,9},{9,8},{10,11... | collective-permute-start | bytes 294920 | tf_op jit(solution)/shard_map/ppermute | solution.py:487
  196.1 8.8 %collective-permute-start.36 = (bf16[2,192,384]{2,1,0:T(8,128)(2,1)S(1)}, bf16[2,192,384]{2,1,0:T(8,128)(2,1)S(1)}, u32[]{:S(2)}, u32[]{:S(2)}) collective-permute-start(bf16[2,192,384]{2,1,0:T(8,128)(2,1)S(1)} %get-tuple-element.291), channel_id=1, source_target_pairs={{0,8},{4,12},{8,0},{12,4},{16,24},{20,28},{24,16},{28,20},{1,9},{5... | collective-permute-start | bytes 884744 | tf_op jit(solution)/shard_map/ppermute | solution.py:487
  197.8 8.5 %collective-permute-start.37 = (bf16[2,240,384]{2,1,0:T(8,128)(2,1)S(1)}, bf16[2,240,384]{2,1,0:T(8,128)(2,1)S(1)}, u32[]{:S(2)}, u32[]{:S(2)}) collective-permute-start(bf16[2,240,384]{2,1,0:T(8,128)(2,1)S(1)} %get-tuple-element.293), channel_id=1, source_target_pairs={{0,2},{1,3},{2,0},{3,1},{4,6},{5,7},{6,4},{7,5},{8,10},{9,11},{10,... | collective-permute-start | bytes 1105928 | tf_op jit(solution)/shard_map/ppermute | solution.py:487
  198.6 19.9 %collective-permute-start.38 = (bf16[8,144,384]{2,1,0:T(8,128)(2,1)}, bf16[8,144,384]{2,1,0:T(8,128)(2,1)}, u32[]{:S(2)}, u32[]{:S(2)}) collective-permute-start(bf16[8,144,384]{2,1,0:T(8,128)(2,1)} %get-tuple-element.296), channel_id=1, source_target_pairs={{0,4},{4,0},{8,12},{12,8},{16,20},{20,16},{24,28},{28,24},{1,5},{5... | collective-permute-start | bytes 2654216 | tf_op jit(solution)/shard_map/ppermute | solution.py:487
  203.6 17.4 %collective-permute-start.39 = (bf16[64,384]{1,0:T(8,128)(2,1)}, bf16[64,384]{1,0:T(8,128)(2,1)}, u32[]{:S(2)}, u32[]{:S(2)}) collective-permute-start(bf16[64,384]{1,0:T(8,128)(2,1)} %get-tuple-element.489), channel_id=1, source_target_pairs={{0,1},{1,0},{2,3},{3,2},{4,5},{5,4},{6,7},{7,6},{8,9},{9,8},{10,11... | collective-permute-start | bytes 147464 | tf_op jit(solution)/shard_map/ppermute | solution.py:487
  207.2 13.9 %collective-permute-start.40 = (bf16[64,384]{1,0:T(8,128)(2,1)}, bf16[64,384]{1,0:T(8,128)(2,1)S(1)}, u32[]{:S(2)}, u32[]{:S(2)}) collective-permute-start(bf16[64,384]{1,0:T(8,128)(2,1)} %get-tuple-element.488), channel_id=1, source_target_pairs={{0,2},{1,3},{2,0},{3,1},{4,6},{5,7},{6,4},{7,5},{8,10},{9,11},{10,... | collective-permute-start | bytes 147464 | tf_op jit(solution)/shard_map/ppermute | solution.py:487
  208.3 12.7 %collective-permute-start.41 = (bf16[64,384]{1,0:T(8,128)(2,1)S(1)}, bf16[64,384]{1,0:T(8,128)(2,1)S(1)}, u32[]{:S(2)}, u32[]{:S(2)}) collective-permute-start(bf16[64,384]{1,0:T(8,128)(2,1)S(1)} %get-tuple-element.487), channel_id=1, source_target_pairs={{0,3},{1,2},{2,1},{3,0},{4,7},{5,6},{6,5},{7,4},{8,11},{9,10},{10,... | collective-permute-start | bytes 147464 | tf_op jit(solution)/shard_map/ppermute | solution.py:487
  222.3 10.6 %collective-permute-start.47 = (bf16[4,144,384]{2,1,0:T(8,128)(2,1)}, bf16[4,144,384]{2,1,0:T(8,128)(2,1)}, u32[]{:S(2)}, u32[]{:S(2)}) collective-permute-start(bf16[4,144,384]{2,1,0:T(8,128)(2,1)} %get-tuple-element.313), channel_id=1, source_target_pairs={{0,2},{1,3},{2,0},{3,1},{4,6},{5,7},{6,4},{7,5},{8,10},{9,11},{10,... | collective-permute-start | bytes 1327112 | tf_op jit(solution)/shard_map/ppermute | solution.py:487
  224.3 41.7 %collective-permute-start.45 = (bf16[8,208,384]{2,1,0:T(8,128)(2,1)}, bf16[8,208,384]{2,1,0:T(8,128)(2,1)}, u32[]{:S(2)}, u32[]{:S(2)}) collective-permute-start(bf16[8,208,384]{2,1,0:T(8,128)(2,1)} %get-tuple-element.309), channel_id=1, source_target_pairs={{0,4},{4,0},{8,12},{12,8},{16,20},{20,16},{24,28},{28,24},{1,5},{5... | collective-permute-start | bytes 3833864 | tf_op jit(solution)/shard_map/ppermute | solution.py:487
  224.9 45.0 %collective-permute-start.46 = (bf16[8,240,384]{2,1,0:T(8,128)(2,1)}, bf16[8,240,384]{2,1,0:T(8,128)(2,1)}, u32[]{:S(2)}, u32[]{:S(2)}) collective-permute-start(bf16[8,240,384]{2,1,0:T(8,128)(2,1)} %get-tuple-element.311), channel_id=1, source_target_pairs={{0,8},{4,12},{8,0},{12,4},{16,24},{20,28},{24,16},{28,20},{1,9},{5... | collective-permute-start | bytes 4423688 | tf_op jit(solution)/shard_map/ppermute | solution.py:487
  244.1 24.8 %collective-permute-start.51 = (bf16[8,144,384]{2,1,0:T(8,128)(2,1)}, bf16[8,144,384]{2,1,0:T(8,128)(2,1)S(1)}, u32[]{:S(2)}, u32[]{:S(2)}) collective-permute-start(bf16[8,144,384]{2,1,0:T(8,128)(2,1)} %get-tuple-element.340), channel_id=1, source_target_pairs={{0,2},{1,3},{2,0},{3,1},{4,6},{5,7},{6,4},{7,5},{8,10},{9,11},{10,... | collective-permute-start | bytes 2654216 | tf_op jit(solution)/shard_map/ppermute | solution.py:487
  245.3 20.5 %collective-permute-start.52 = (bf16[1,432,384]{2,1,0:T(8,128)(2,1)S(1)}, bf16[1,432,384]{2,1,0:T(8,128)(2,1)S(1)}, u32[]{:S(2)}, u32[]{:S(2)}) collective-permute-start(bf16[1,432,384]{2,1,0:T(8,128)(2,1)S(1)} %pad_maximum_fusion.10), channel_id=1, source_target_pairs={{0,16},{4,20},{8,24},{12,28},{16,0},{20,4},{24,8},{28,12},{1,17},{... | collective-permute-start | bytes 995336 | tf_op jit(solution)/shard_map/ppermute | solution.py:487
  251.3 16.7 %collective-permute-start.53 = (bf16[2,256,768]{2,1,0:T(8,128)(2,1)S(1)}, bf16[2,256,768]{2,1,0:T(8,128)(2,1)S(1)}, u32[]{:S(2)}, u32[]{:S(2)}) collective-permute-start(bf16[2,256,768]{2,1,0:T(8,128)(2,1)S(1)} %pad_maximum_fusion.4), channel_id=1, source_target_pairs={{0,1},{1,0},{2,3},{3,2},{4,5},{5,4},{6,7},{7,6},{8,9},{9,8},{10,11... | collective-permute-start | bytes 2359304 | tf_op jit(solution)/shard_map/ppermute | solution.py:487
  273.6 15.3 %collective-permute-start.56 = (bf16[4,144,384]{2,1,0:T(8,128)(2,1)S(1)}, bf16[4,144,384]{2,1,0:T(8,128)(2,1)S(1)}, u32[]{:S(2)}, u32[]{:S(2)}) collective-permute-start(bf16[4,144,384]{2,1,0:T(8,128)(2,1)S(1)} %get-tuple-element.370), channel_id=1, source_target_pairs={{0,8},{4,12},{8,0},{12,4},{16,24},{20,28},{24,16},{28,20},{1,9},{5... | collective-permute-start | bytes 1327112 | tf_op jit(solution)/shard_map/ppermute | solution.py:487
  274.1 15.7 %collective-permute-start.54 = (bf16[4,208,384]{2,1,0:T(8,128)(2,1)S(1)}, bf16[4,208,384]{2,1,0:T(8,128)(2,1)S(1)}, u32[]{:S(2)}, u32[]{:S(2)}) collective-permute-start(bf16[4,208,384]{2,1,0:T(8,128)(2,1)S(1)} %get-tuple-element.366), channel_id=1, source_target_pairs={{0,2},{1,3},{2,0},{3,1},{4,6},{5,7},{6,4},{7,5},{8,10},{9,11},{10,... | collective-permute-start | bytes 1916936 | tf_op jit(solution)/shard_map/ppermute | solution.py:487
  275.0 17.6 %collective-permute-start.55 = (bf16[4,240,384]{2,1,0:T(8,128)(2,1)S(1)}, bf16[4,240,384]{2,1,0:T(8,128)(2,1)S(1)}, u32[]{:S(2)}, u32[]{:S(2)}) collective-permute-start(bf16[4,240,384]{2,1,0:T(8,128)(2,1)S(1)} %get-tuple-element.368), channel_id=1, source_target_pairs={{0,4},{4,0},{8,12},{12,8},{16,20},{20,16},{24,28},{28,24},{1,5},{5... | collective-permute-start | bytes 2211848 | tf_op jit(solution)/shard_map/ppermute | solution.py:487
  293.1 9.8 %collective-permute-start.57 = (bf16[2,208,384]{2,1,0:T(8,128)(2,1)S(1)}, bf16[2,208,384]{2,1,0:T(8,128)(2,1)S(1)}, u32[]{:S(2)}, u32[]{:S(2)}) collective-permute-start(bf16[2,208,384]{2,1,0:T(8,128)(2,1)S(1)} %get-tuple-element.372), channel_id=1, source_target_pairs={{0,8},{4,12},{8,0},{12,4},{16,24},{20,28},{24,16},{28,20},{1,9},{5... | collective-permute-start | bytes 958472 | tf_op jit(solution)/shard_map/ppermute | solution.py:487
  293.6 11.4 %collective-permute-start.58 = (bf16[2,240,384]{2,1,0:T(8,128)(2,1)S(1)}, bf16[2,240,384]{2,1,0:T(8,128)(2,1)S(1)}, u32[]{:S(2)}, u32[]{:S(2)}) collective-permute-start(bf16[2,240,384]{2,1,0:T(8,128)(2,1)S(1)} %get-tuple-element.374), channel_id=1, source_target_pairs={{0,2},{1,3},{2,0},{3,1},{4,6},{5,7},{6,4},{7,5},{8,10},{9,11},{10,... | collective-permute-start | bytes 1105928 | tf_op jit(solution)/shard_map/ppermute | solution.py:487
  299.8 14.6 %collective-permute-start.65 = (bf16[576,384]{1,0:T(8,128)(2,1)S(1)}, bf16[576,384]{1,0:T(8,128)(2,1)S(1)}, u32[]{:S(2)}, u32[]{:S(2)}) collective-permute-start(bf16[576,384]{1,0:T(8,128)(2,1)S(1)} %pad_maximum_fusion.6), channel_id=1, source_target_pairs={{0,2},{1,3},{2,0},{3,1},{4,6},{5,7},{6,4},{7,5},{8,10},{9,11},{10,... | collective-permute-start | bytes 1327112 | tf_op jit(solution)/shard_map/ppermute | solution.py:487
  305.3 14.3 %collective-permute-start.60 = (bf16[256,768]{1,0:T(8,128)(2,1)S(1)}, bf16[256,768]{1,0:T(8,128)(2,1)S(1)}, u32[]{:S(2)}, u32[]{:S(2)}) collective-permute-start(bf16[256,768]{1,0:T(8,128)(2,1)S(1)} %fusion.80), channel_id=1, source_target_pairs={{0,2},{1,3},{2,0},{3,1},{4,6},{5,7},{6,4},{7,5},{8,10},{9,11},{10,... | collective-permute-start | bytes 1179656 | tf_op jit(solution)/shard_map/ppermute | solution.py:487
  306.6 18.1 %collective-permute-start.61 = (bf16[1,592,384]{2,1,0:T(8,128)(2,1)S(1)}, bf16[1,592,384]{2,1,0:T(8,128)(2,1)S(1)}, u32[]{:S(2)}, u32[]{:S(2)}) collective-permute-start(bf16[1,592,384]{2,1,0:T(8,128)(2,1)S(1)} %pad_maximum_fusion.5), channel_id=1, source_target_pairs={{0,16},{4,20},{8,24},{12,28},{16,0},{20,4},{24,8},{28,12},{1,17},{... | collective-permute-start | bytes 1363976 | tf_op jit(solution)/shard_map/ppermute | solution.py:487
  314.7 11.0 %collective-permute-start.66 = (bf16[2,576,384]{2,1,0:T(8,128)(2,1)S(1)}, bf16[2,576,384]{2,1,0:T(8,128)(2,1)}, u32[]{:S(2)}, u32[]{:S(2)}) collective-permute-start(bf16[2,576,384]{2,1,0:T(8,128)(2,1)S(1)} %pad_maximum_fusion.2.refs_1_), channel_id=1, source_target_pairs={{0,1},{1,0},{2,3},{3,2},{4,5},{5,4},{6,7},{7,6},{8,9},{9,8},{10,11... | collective-permute-start | bytes 2654216 | tf_op jit(solution)/shard_map/ppermute | solution.py:487
  324.8 11.5 %collective-permute-start.62 = (bf16[592,384]{1,0:T(8,128)(2,1)S(1)}, bf16[592,384]{1,0:T(8,128)(2,1)}, u32[]{:S(2)}, u32[]{:S(2)}) collective-permute-start(bf16[592,384]{1,0:T(8,128)(2,1)S(1)} %fusion.96), channel_id=1, source_target_pairs={{0,2},{1,3},{2,0},{3,1},{4,6},{5,7},{6,4},{7,5},{8,10},{9,11},{10,... | collective-permute-start | bytes 1363976 | tf_op jit(solution)/shard_map/ppermute | solution.py:487
  (143 other events, 1052.0 us)
